TPU v7x, 256 devices: a whole 4x4x8 slice. The times are simulated.
256 devices in a mesh: grp: 8 (over z), blk: 32 (over x, y, core).
Axes of the slice: x: 4, y: 4, z: 8, core: 2. Of those that a mesh axis runs over, the one named last changes fastest.
Arguments:
- tokens: bfloat16 [8, 4096, 1024], P('grp', 'blk'), may hold values from -40 to 40
- lengths: int32 [8, 16], P('grp'), may hold values from 1 to 2176, 4096 in all within a row
- owners: int32 [8], P('grp'), may hold values from 0 to 7
- prefix_cache: bfloat16 [8, 2048, 1024], P('grp', 'blk'), may hold values from -52 to 52
- routes: int32 [8, 4096, 2], P('grp', 'blk'), may hold values from 0 to 7, all different within a row; in each aligned block of 128 rows (0 to 127, 128 to 255, ..., all dimensions but the last counted through in order) at most 40 rows name the same one
- gates: float32 [8, 4096, 2], P('grp', 'blk'), may hold values from 0.2 to 1
- attn_gain: float32 [1024], replicated, may hold values from 0.5 to 1.5
- w_query: bfloat16 [1024, 512], replicated, may hold values from -0.5 to 0.5
- w_keyval: bfloat16 [1024, 1024], replicated, may hold values from -0.1875 to 0.1875
- w_out: bfloat16 [512, 1024], replicated, may hold values from -0.25 to 0.25
- moe_gain: float32 [1024], replicated, may hold values from 0.5 to 1.5
- w_gate: bfloat16 [32, 1024, 704], P('blk'), may hold values from -0.1875 to 0.1875
- w_up: bfloat16 [32, 1024, 704], P('blk'), may hold values from -0.1875 to 0.1875
- w_down: bfloat16 [32, 704, 1024], P('blk'), may hold values from -0.109375 to 0.109375
- final_gain: float32 [1024], replicated, may hold values from 0.5 to 1.5
- unembed: bfloat16 [1024, 32128], P(None, 'blk'), may hold values from -0.5 to 0.5
Outputs:
- hidden: bfloat16 [8, 4096, 1024], P('grp', 'blk')
- suffix_cache: bfloat16 [8, 4096, 1024], P('grp', 'blk')
- request_norm: float32 [8, 16], P('grp')
- greatest: float32 [8, 16], P('grp')
Inputs may be any that keep to these rules, and one draw needn't show every extreme that they name: In each group the lengths sum to 4096, and the longest request has exactly 2176 tokens. `routes`: the two experts of a token differ. Within the 128 rows of one device no expert is named more than 40 times, and in some device's rows an expert is named exactly 40 times.
All inputs are finite; a program needn't handle non-finite values.
Results may differ from a plain program's by a relative error of at most 0.0052.
The roundings to bfloat16 on the way count: a program that leaves them out, or rounds other values in their place, can miss the bound.
Values may be sent and summed in bfloat16 or wider, within the bound.
No kernel may reach another device: no remote copies, remote signals or barrier semaphores. Data moves between devices by JAX's collectives and lax.ppermute only.
A program may use at most 128 MiB of HBM per device.

v0:
```python
import jax
import jax.numpy as jnp
from jax import lax
from jax.sharding import PartitionSpec as P

HEADS = 8
EXPERTS = 8
CAP = 40


epsilon = 1e-06
neg_big = -1e30


def rms_scale(values, gain_vector):
    values = values.astype(jnp.float32)
    return (
        values
        * lax.rsqrt(jnp.mean(values * values, axis=-1, keepdims=True) + epsilon)
        * gain_vector
    )


def request_of(positions, end_points):
    return jnp.sum((positions[:, None] >= end_points[None, :]).astype(jnp.int32), axis=1)


def slot_targets(block_routes):
    flat_routes = block_routes.reshape(-1)
    onehot = (flat_routes[:, None] == jnp.arange(EXPERTS, dtype=jnp.int32)[None, :]).astype(
        jnp.int32
    )
    before = jnp.cumsum(onehot, axis=0) - onehot
    slot_index = jnp.sum(before * onehot, axis=1)
    return (flat_routes * CAP + slot_index).reshape(block_routes.shape)


def dispatch_matrix(targets):
    slot_ids = jnp.arange(EXPERTS * CAP, dtype=jnp.int32)
    matches = (targets[:, 0][None, :] == slot_ids[:, None]) | (
        targets[:, 1][None, :] == slot_ids[:, None]
    )
    return matches.astype(jnp.bfloat16)


def attend_piece(carry_state, query_set, key_part, key_req, key_pos, masked):
    context_sum, row_max, row_total = carry_state
    queries, query_req, query_pos = query_set
    head_count = row_max.shape[0]
    piece_rows = key_part.shape[0]
    attn_width = key_part.shape[1] // 2
    head_size = attn_width // head_count
    key_heads = key_part[:, :attn_width].reshape(piece_rows, head_count, head_size)
    value_heads = key_part[:, attn_width:].reshape(piece_rows, head_count, head_size)
    query_heads = queries.reshape(queries.shape[0], head_count, head_size)
    scores = jnp.einsum(
        "qhd,khd->hqk", query_heads, key_heads, preferred_element_type=jnp.float32
    ) * head_size ** (-0.5)
    if masked:
        allowed = (query_req[:, None] == key_req[None, :]) & (
            key_pos[None, :] <= query_pos[:, None]
        )
        scores = jnp.where(allowed[None], scores, neg_big)
    new_max = jnp.maximum(row_max, jnp.max(scores, axis=-1))
    shrink = jnp.exp(row_max - new_max)
    probs_full = jnp.exp(scores - new_max[..., None])
    row_total = row_total * shrink + jnp.sum(probs_full, axis=-1)
    context_sum = context_sum * shrink[..., None] + jnp.einsum(
        "hqk,khd->hqd",
        probs_full.astype(jnp.bfloat16),
        value_heads,
        preferred_element_type=jnp.float32,
    )
    return (context_sum, new_max, row_total)


def fold_sets(states, query_sets, key_part, key_req, key_pos, masked, request_ends):
    results = []
    for state_one, set_one in zip(states, query_sets):
        if masked:
            first_req = set_one[1][0]
            earliest = jnp.where(first_req > 0, request_ends[jnp.maximum(first_req - 1, 0)], 0)
            needed = (key_pos[0] >= 0) & (key_pos[0] <= set_one[2][-1]) & (key_pos[-1] >= earliest)
            results.append(
                lax.cond(
                    needed,
                    lambda carried: attend_piece(
                        carried, set_one, key_part, key_req, key_pos, True
                    ),
                    lambda carried: carried,
                    state_one,
                )
            )
        else:
            results.append(attend_piece(state_one, set_one, key_part, key_req, key_pos, False))
    return tuple(results)


def empty_state(query_count, head_count, head_size):
    return (
        jnp.zeros((head_count, query_count, head_size), jnp.float32),
        jnp.full((head_count, query_count), neg_big, jnp.float32),
        jnp.zeros((head_count, query_count), jnp.float32),
    )


def finish_context(state_one):
    context_sum, row_max, row_total = state_one
    context = context_sum / row_total[..., None]
    return jnp.transpose(context, (1, 0, 2)).reshape(context.shape[1], -1).astype(jnp.bfloat16)


def local(
    tokens,
    lengths,
    owners,
    prefix_cache,
    routes,
    gates,
    attn_gain,
    w_query,
    w_keyval,
    w_out,
    moe_gain,
    w_gate,
    w_up,
    w_down,
    final_gain,
    unembed,
):
    tok_rows = tokens.shape[1]
    model_width = tokens.shape[2]
    head_count = HEADS
    head_size = w_query.shape[1] // head_count
    blocks = lax.axis_size("blk")
    block_index = lax.axis_index("blk")
    stream = tokens[0]
    normed = rms_scale(stream, attn_gain).astype(jnp.bfloat16)
    queries = jnp.dot(normed, w_query, preferred_element_type=jnp.float32).astype(jnp.bfloat16)
    suffix_kv = jnp.dot(normed, w_keyval, preferred_element_type=jnp.float32).astype(jnp.bfloat16)
    request_ends = jnp.cumsum(lengths[0])
    positions = block_index * tok_rows + jnp.arange(tok_rows, dtype=jnp.int32)
    requests = request_of(positions, request_ends)
    query_sets = ((queries, requests, positions),)
    states = tuple((empty_state(one[0].shape[0], head_count, head_size) for one in query_sets))
    owner_id = owners[0]
    blank_prefix = jnp.zeros_like(prefix_cache[0])
    arrived = lax.all_gather(prefix_cache, "grp", axis=0, tiled=True)
    first_row = jnp.int32(0)
    shard_count = arrived.shape[0]
    inside = (owner_id >= first_row) & (owner_id < first_row + shard_count)
    offset = jnp.clip(owner_id, 0, shard_count - 1)
    owner_prefix = jnp.where(
        inside, lax.dynamic_index_in_dim(arrived, offset, 0, keepdims=False), blank_prefix
    )
    states = fold_sets(
        states,
        query_sets,
        lax.all_gather(owner_prefix, "blk", axis=0, tiled=True),
        None,
        None,
        False,
        request_ends,
    )
    arrived = lax.all_gather(suffix_kv, "blk", axis=0, tiled=True)
    key_pos = jnp.arange(arrived.shape[0], dtype=jnp.int32)
    states = fold_sets(
        states, query_sets, arrived, request_of(key_pos, request_ends), key_pos, True, request_ends
    )
    contexts = [finish_context(one) for one in states]
    context = contexts[0]
    mixed_stream = stream.astype(jnp.float32) + jnp.dot(
        context, w_out, preferred_element_type=jnp.float32
    )
    routed_in = rms_scale(mixed_stream, moe_gain).astype(jnp.bfloat16)
    targets = slot_targets(routes[0])
    dispatch = dispatch_matrix(targets)
    packed = jnp.dot(dispatch, routed_in, preferred_element_type=jnp.float32).astype(jnp.bfloat16)
    split_count = blocks // EXPERTS
    outgoing = jnp.broadcast_to(
        packed.reshape(EXPERTS, 1, CAP, model_width), (EXPERTS, split_count, CAP, model_width)
    ).reshape(blocks, CAP, model_width)
    arrived = lax.all_to_all(outgoing, "blk", split_axis=0, concat_axis=0, tiled=True)
    flat_rows = arrived.reshape(-1, model_width)
    gate_value = jnp.dot(flat_rows, w_gate[0], preferred_element_type=jnp.float32)
    up_value = jnp.dot(flat_rows, w_up[0], preferred_element_type=jnp.float32)
    hidden = (jax.nn.gelu(gate_value, approximate=True) * up_value).astype(jnp.bfloat16)
    partial_value = (
        jnp.dot(hidden, w_down[0], preferred_element_type=jnp.float32)
        .astype(jnp.bfloat16)
        .reshape(arrived.shape)
    )
    returned_parts = lax.all_to_all(partial_value, "blk", split_axis=0, concat_axis=0, tiled=True)
    summed = jnp.sum(
        returned_parts.reshape(EXPERTS, split_count, CAP, model_width).astype(jnp.float32), axis=1
    ).reshape(EXPERTS * CAP, model_width)
    first_pick = jnp.take(summed, targets[:, 0], axis=0)
    second_pick = jnp.take(summed, targets[:, 1], axis=0)
    moe_out = gates[0][:, 0:1] * first_pick + gates[0][:, 1:2] * second_pick
    hidden_out = (mixed_stream + moe_out).astype(jnp.bfloat16)
    squares = jnp.sum(jnp.square(hidden_out.astype(jnp.float32)), axis=1)
    member = requests[:, None] == jnp.arange(lengths.shape[1], dtype=jnp.int32)[None, :]
    norm_terms = jnp.sum(jnp.where(member, squares[:, None], 0.0), axis=0)
    is_last = positions[:, None] == (request_ends - 1)[None, :]
    final_rows = rms_scale(hidden_out, final_gain).astype(jnp.bfloat16)
    last_terms = jnp.einsum(
        "tr,td->rd", is_last.astype(jnp.bfloat16), final_rows, preferred_element_type=jnp.float32
    )
    norm_sums, last_rows = (
        lax.psum(norm_terms.astype(jnp.bfloat16), "blk").astype(jnp.float32),
        lax.psum(last_terms.astype(jnp.bfloat16), "blk").astype(jnp.float32),
    )
    logits = jnp.dot(last_rows.astype(jnp.bfloat16), unembed, preferred_element_type=jnp.float32)
    greatest = lax.pmax(jnp.max(logits, axis=1), "blk")
    request_norm = jnp.sqrt(norm_sums / (lengths[0].astype(jnp.float32) * model_width))
    return (hidden_out[None], suffix_kv[None], request_norm[None], greatest[None])


def solution(mesh):
    placed = (
        P("grp", "blk", None),
        P("grp", None),
        P("grp"),
        P("grp", "blk", None),
        P("grp", "blk", None),
        P("grp", "blk", None),
        P(),
        P(),
        P(),
        P(),
        P(),
        P("blk", None, None),
        P("blk", None, None),
        P("blk", None, None),
        P(),
        P(None, "blk"),
    )
    return jax.shard_map(
        local,
        mesh=mesh,
        in_specs=placed,
        out_specs=(P("grp", "blk", None), P("grp", "blk", None), P("grp", None), P("grp", None)),
        check_vma=False,
    )
```

profile of v0, /device:TPU:1, one launch (start us, length us, event | category | flops | bytes accessed | tf_op | source)
XLA Modules:
  0.0 506.1 jit_solution(9666139919563082497)
XLA Ops:
  8.9 38.4 %all-gather.5.cloned.1.call-done = bf16[8,64,1024]{2,1,0:T(8,128)(2,1)} async-done(((bf16[1,64,1024]{2,1,0:T(8,128)(2,1)}), bf16[8,64,1024]{2,1,0:T(8,128)(2,1)}) %all-gather.5.cloned.1.call-update) | async-done | bytes 1048592 | tf_op jit(solution)/shard_map/all_gather | solution.py:148
  47.3 1.6 dynamic-slice_select_fusion
  49.0 1.1 fusion.37
  50.1 2.2 convolution_convert_fusion.2
  57.5 48.1 %all-gather.9.cloned.1.call-done = bf16[1,2048,1024]{2,1,0:T(8,128)(2,1)} async-done(((bf16[1,64,1024]{2,1,0:T(8,128)(2,1)}), bf16[1,2048,1024]{2,1,0:T(8,128)(2,1)}) %all-gather.9.cloned.1.call-update) | async-done | bytes 4194320 | tf_op jit(solution)/shard_map/all_gather | solution.py:159
  105.6 3.8 fusion.69
  109.4 2.5 copy.56
  111.9 2.9 copy.55
  114.8 1.4 multiply_reduce_fusion
  116.2 1.6 fusion.11
  117.9 1.9 fusion.29
  119.7 46.3 %all-gather.7.cloned.1.call-done = bf16[4096,1024]{1,0:T(8,128)(2,1)} async-done(((bf16[128,1024]{1,0:T(8,128)(2,1)}), bf16[4096,1024]{1,0:T(8,128)(2,1)}) %all-gather.7.cloned.1.call-update) | async-done | bytes 8388624 | tf_op jit(solution)/shard_map/all_gather | solution.py:165
  166.1 40.8 %conditional.1 = ((f32[8,128,64]{1,2,0:T(8,128)S(1)}, f32[8,128]{1,0:T(8,128)S(1)})) conditional(s32[]{:T(128)} %convert_element_type.95, (f32[8,128,64]{1,2,0:T(8,128)S(1)}, f32[8,128]{1,0:T(8,128)S(1)}) %tuple.16, (s32[128]{0:T(128)S(1)}, s32[4096,16]{0,1:T(8,128)S(1)}, s32[4096]{0:T(1024)S(1)}, s32[128]{0:T(128)S(1)}, ...), branch_computations={%region_5.6_spmd, %region_6.10_spmd} | conditional | flops 1121646592 | bytes 162767936 | solution.py:85
  166.3 11.4 %copy.58 = bf16[4096,1024]{0,1:T(8,128)(2,1)} copy(bf16[4096,1024]{1,0:T(8,128)(2,1)} %get-tuple-element.83) | data formatting | bytes 16777216 | tf_op jit(solution)/shard_map
  177.7 6.1 %fusion.68 = (bf16[4096,512]{0,1:T(8,128)(2,1)}, bf16[4096,512]{0,1:T(8,128)(2,1)}) fusion(bf16[4096,1024]{0,1:T(8,128)(2,1)} %copy.58), kind=kLoop, calls=%fused_computation.115 | loop fusion | bytes 16777216 | tf_op jit(solution)/shard_map/cond/branch_1_fun/slice | solution.py:53
  184.4 5.0 fusion
  189.4 4.8 fusion.1
  194.3 0.9 copy-done.2
  195.1 11.7 %fusion.6 = f32[8,128,64]{1,2,0:T(8,128)S(1)} fusion(bf16[4096,8,64]{0,2,1:T(8,128)(2,1)} %bitcast.90, f32[8,128,4096]{2,1,0:T(8,128)} %copy-done.2, f32[8,128]{1,0:T(8,128)S(1)} %max.12, pred[128,4096]{1,0:T(8,128)(4,1)S(1)} %compare_and_fusion, f32[8,128,64]{1,2,0:T(8,128)S(1)} %get-tuple-element.25, f32[8,128]{1,0:T(8,128)S(1)} %get-tuple-element.92), kind=kOutput, calls=%fused_computation.10 | convolution fusion | flops 553779200 | bytes 22028288 | tf_op jit(solution)/shard_map/cond/branch_1_fun/hqk,khd->hqd/dot_general | solution.py:68
  208.1 39.5 %all_to_all.10 = bf16[32,40,1024]{2,1,0:T(8,128)(2,1)S(1)} all-to-all(bf16[32,40,1024]{2,1,0:T(8,128)(2,1)S(1)} %bitcast.86), channel_id=1, replica_groups=mesh['grp'=8,'blk'=32] {'blk'}, dimensions={0} | all-to-all | bytes 5242880 | tf_op jit(solution)/shard_map/all_to_all | solution.py:183
  247.6 1.5 copy-done.6
  249.2 3.8 fusion.27
  253.0 9.7 %convolution_convert_fusion = bf16[1280,1024]{1,0:T(8,128)(2,1)} fusion(bf16[1,704,1024]{2,1,0:T(8,128)(2,1)S(1)} %copy-done.20, bf16[1280,1024]{1,0:T(8,128)(2,1)} %bitcast.93, f32[1280,704]{0,1:T(8,128)} %fusion.27, bf16[1,1024,704]{1,2,0:T(8,128)(2,1)} %param.32), kind=kOutput, calls=%fused_computation.25 | convolution fusion | flops 3701309440 | bytes 11730944 | tf_op jit(solution)/shard_map/dot_general | solution.py:189
  262.8 4.7 all-to-all-start.1
  267.6 33.5 %all-to-all-done.1 = bf16[32,40,1024]{2,1,0:T(8,128)(2,1)} async-done(((bf16[32,40,1024]{2,1,0:T(8,128)(2,1)}), bf16[32,40,1024]{2,1,0:T(8,128)(2,1)}, u32[]{:S(2)}, u32[]{:S(2)}) %all-to-all-start.1) | async-done | bytes 2621472 | tf_op jit(solution)/shard_map/all_to_all | solution.py:193
  301.1 2.4 convert_reduce_fusion
  303.5 1.6 gather_fusion.1
  305.0 1.6 gather_fusion
  306.6 1.7 fusion.34
  308.7 119.8 %all-reduce = (bf16[16]{0:T(256)(128)(2,1)S(1)}, bf16[16,1024]{1,0:T(8,128)(2,1)S(1)}) all-reduce(bf16[16]{0:T(256)(128)(2,1)S(1)} %select_reduce_fusion, bf16[16,1024]{1,0:T(8,128)(2,1)S(1)} %convolution_convert_fusion.4), channel_id=1, replica_groups=mesh['grp'=8,'blk'=32] {'blk'}, use_global_device_ids=true, to_apply=%region_17.19 | all-reduce | flops 16400 | bytes 65600 | tf_op jit(solution)/shard_map/psum | solution.py:210
  429.0 2.3 convolution_reduce_fusion
  431.4 68.2 %pmax.7 = f32[1,16]{1,0:T(1,128)} all-reduce(f32[1,16]{1,0:T(1,128)S(1)} %bitcast.101), channel_id=1, replica_groups=mesh['grp'=8,'blk'=32] {'blk'}, use_global_device_ids=true, to_apply=%region_20.22 | all-reduce | flops 16 | bytes 128 | tf_op jit(solution)/shard_map/pmax | solution.py:214
  (96 shorter events, 7.4 us)
Async XLA Ops:
  7.2 42.9 %copy-start = (bf16[1024,1024]{1,0:T(8,128)(2,1)S(1)}, bf16[1024,1024]{1,0:T(8,128)(2,1)}, u32[]{:S(2)}) copy-start(bf16[1024,1024]{1,0:T(8,128)(2,1)} %param.28) | copy-start | bytes 6291460
  7.2 48.3 %copy-start.5 = (bf16[1,128,1024]{2,1,0:T(8,128)(2,1)S(1)}, bf16[1,128,1024]{2,1,0:T(8,128)(2,1)}, u32[]{:S(2)}) copy-start(bf16[1,128,1024]{2,1,0:T(8,128)(2,1)} %param.20) | copy-start | bytes 786436
  7.2 48.3 %copy-start.10 = (f32[1024]{0:T(1024)S(1)}, f32[1024]{0:T(1024)}, u32[]{:S(2)}) copy-start(f32[1024]{0:T(1024)} %param.26) | copy-start | bytes 12292
  7.2 45.0 %copy-start.12 = (s32[1,128,2]{1,2,0:T(2,128)S(1)}, s32[1,128,2]{1,2,0:T(2,128)}, u32[]{:S(2)}) copy-start(s32[1,128,2]{1,2,0:T(2,128)} %param.24) | copy-start | bytes 3076
  7.2 46.7 %copy-start.14 = (s32[1,16]{1,0:T(1,128)S(1)}, s32[1,16]{1,0:T(1,128)}, u32[]{:S(2)}) copy-start(s32[1,16]{1,0:T(1,128)} %param.21) | copy-start | bytes 196
  7.2 48.3 %copy-start.7 = (bf16[1024,512]{1,0:T(8,128)(2,1)S(1)}, bf16[1024,512]{1,0:T(8,128)(2,1)}, u32[]{:S(2)}) copy-start(bf16[1024,512]{1,0:T(8,128)(2,1)} %param.27) | copy-start | bytes 3145732
  7.2 40.1 %all-gather.5.cloned.1.call-start = ((), (), s32[]{:S(2)}) async-start(), calls=%async_computation.2 | async-start | bytes 1179648 | tf_op jit(solution)/shard_map/all_gather | solution.py:148
  8.0 97.6 %all-gather.9.cloned.1.call-start = ((), (), s32[]{:S(2)}) async-start(), calls=%async_computation.4 | async-start | bytes 4325376 | tf_op jit(solution)/shard_map/all_gather | solution.py:159
  48.9 117.2 %all-gather.7.cloned.1.call-start = ((), (), s32[]{:S(2)}) async-start(), calls=%async_computation.3 | async-start | bytes 8650752 | tf_op jit(solution)/shard_map/all_gather | solution.py:165
  52.7 3.4 copy-start.15
  54.3 1.6 copy-start.17
  116.2 1.7 copy-start.3
  117.9 48.2 %copy-start.16 = (s32[128]{0:T(128)S(1)}, s32[128]{0:T(128)}, u32[]{:S(2)}) copy-start(s32[128]{0:T(128)} %copy-done.15) | copy-start | bytes 1540
  117.9 48.2 %copy-start.18 = (s32[128]{0:T(128)S(1)}, s32[128]{0:T(128)}, u32[]{:S(2)}) copy-start(s32[128]{0:T(128)} %copy-done.17) | copy-start | bytes 1540
  166.1 40.8 %copy-start.8 = (bf16[512,1024]{1,0:T(8,128)(2,1)S(1)}, bf16[512,1024]{1,0:T(8,128)(2,1)}, u32[]{:S(2)}) copy-start(bf16[512,1024]{1,0:T(8,128)(2,1)} %param.29) | copy-start | bytes 3145732
  166.1 41.3 %copy-start.11 = (f32[1024]{0:T(1024)S(1)}, f32[1024]{0:T(1024)}, u32[]{:S(2)}) copy-start(f32[1024]{0:T(1024)} %param.30) | copy-start | bytes 12292
  189.4 5.7 %copy-start.2 = (f32[8,128,4096]{2,1,0:T(8,128)}, f32[8,128,4096]{2,1,0:T(8,128)S(1)}, u32[]{:S(2)}) copy-start(f32[8,128,4096]{2,1,0:T(8,128)S(1)} %get-tuple-element.98) | copy-start | bytes 50331652 | tf_op jit(solution)/shard_map/cond
  207.3 40.3 %copy-start.4 = (f32[128,1024]{1,0:T(8,128)}, f32[128,1024]{1,0:T(8,128)S(1)}, u32[]{:S(2)}) copy-start(f32[128,1024]{1,0:T(8,128)S(1)} %get-tuple-element.108) | copy-start | bytes 1572868
  207.8 41.4 %copy-start.19 = (bf16[1,1024,704]{1,2,0:T(8,128)(2,1)S(1)}, bf16[1,1024,704]{1,2,0:T(8,128)(2,1)}, u32[]{:S(2)}) copy-start(bf16[1,1024,704]{1,2,0:T(8,128)(2,1)} %param.31) | copy-start | bytes 4325380
  247.6 1.5 copy-start.6
  249.2 3.8 copy-start.20
  262.8 4.8 copy-start.13
  262.8 38.3 %all-to-all-start.1 = ((bf16[32,40,1024]{2,1,0:T(8,128)(2,1)}), bf16[32,40,1024]{2,1,0:T(8,128)(2,1)}, u32[]{:S(2)}, u32[]{:S(2)}) async-start(bf16[32,40,1024]{2,1,0:T(8,128)(2,1)} %bitcast.91), calls=%async_computation.1 | async-start | bytes 5242880 | tf_op jit(solution)/shard_map/all_to_all | solution.py:193
  303.5 196.1 %copy-start.1 = (bf16[1024,1024]{1,0:T(8,128)(2,1)S(1)}, bf16[1024,1024]{1,0:T(8,128)(2,1)}, u32[]{:S(2)}) copy-start(bf16[1024,1024]{1,0:T(8,128)(2,1)} %param.28) | copy-start | bytes 6291460
  305.0 3.3 copy-start.21
  308.3 191.2 %copy-start.9 = (bf16[128,1024]{1,0:T(8,128)(2,1)}, bf16[128,1024]{1,0:T(8,128)(2,1)S(1)}, u32[]{:S(2)}) copy-start(bf16[128,1024]{1,0:T(8,128)(2,1)S(1)} %get-tuple-element.94) | copy-start | bytes 786436
Sparse Core Ops, SparseCore 0:
  9.9 37.4 all-gather.4
  50.5 55.0 all-gather.8
  108.7 57.3 all-gather.6
where the time goes:
time: 507 us; the launch traced here: 506 us
  blocking collectives  227 us (45%)
  waiting for transfers between devices  167 us (33%)
  matrix products  39.4 us (8%)
  local copies, waits for them, and re-layouts  35.1 us (7%)
  between operations  16.4 us (3%)
  other arithmetic  15.5 us (3%)
    psum x1, blocking collectives, local(): lax.psum(norm_terms.astype(jnp.bfloat16), 'blk').astype(jnp.float32)  120 us
    pmax x1, blocking collectives, local(): greatest = lax.pmax(jnp.max(logits, axis=1), 'blk')  68.2 us
    all_gather x1, waiting for transfers between devices, local(): lax.all_gather(owner_prefix, 'blk', axis=0, tiled=True)  48.1 us
    all_gather x1, waiting for transfers between devices, local(): arrived = lax.all_gather(suffix_kv, 'blk', axis=0, tiled=True)  46.3 us
    all_to_all x1, blocking collectives, local(): lax.all_to_all(outgoing, 'blk', split_axis=0, concat_axis=0, tiled=True)  39.5 us
    all_gather x1, waiting for transfers between devices, local(): arrived = lax.all_gather(prefix_cache, 'grp', axis=0, tiled=True)  38.4 us
    all_to_all x1, waiting for transfers between devices, local(): lax.all_to_all(partial_value, 'blk', split_axis=0, concat_axis=0, tiled=T...  33.5 us
    dot_general x2, matrix products, attend_piece(): jnp.einsum('hqk,khd->hqd', probs_full.astype(jnp.bfloat16), value_heads,...  13.6 us
  transfers between devices with their start and end apart: 4, of which 4 were waited for; matrix products, arithmetic and copies ran while one was open for 4% of the time, Pallas kernels for 0%

commit v1 on v0

v1 whole, which is shorter than its diff:
```python
import jax
import jax.numpy as jnp
from jax import lax
from jax.experimental import pallas as pl
from jax.experimental.pallas import tpu as pltpu
from jax.sharding import PartitionSpec as P

HEADS = 8
EXPERTS = 8
QUARTERS = 4
CAP = 40
SLOT_ROWS = 48
REQS = 16
ROWS = 128
HALF = 64
LANES = 128
KEY_TILE = 1024
QUERY_TILE = 256

epsilon = 1e-06
neg_big = -1e30
bf16 = jnp.bfloat16
f32 = jnp.float32


def rms_scale(values, gain_vector):
    return (
        values * lax.rsqrt(jnp.mean(values * values, axis=-1, keepdims=True) + epsilon) * gain_vector
    )


def lane_of(shape):
    return lax.broadcasted_iota(jnp.int32, shape, len(shape) - 1)


def head_split(first, second):
    low = lane_of(first.shape) < HALF
    axis = len(first.shape) - 1
    even = jnp.where(low, first, pltpu.roll(second, HALF, axis))
    odd = jnp.where(low, pltpu.roll(first, HALF, axis), second)
    return even, odd


def project_kernel(tok_ref, gain_ref, wq_ref, wk_ref, wv_ref, kv_ref, send_ref, normed_ref):
    pair = pl.program_id(0)

    @pl.when(pair == 0)
    def _():
        normed_ref[...] = rms_scale(tok_ref[...].astype(f32), gain_ref[...]).astype(bf16)

    normed = normed_ref[...]
    query = jnp.dot(normed, wq_ref[...], preferred_element_type=f32).astype(bf16)
    key = jnp.dot(normed, wk_ref[...], preferred_element_type=f32).astype(bf16)
    value = jnp.dot(normed, wv_ref[...], preferred_element_type=f32).astype(bf16)
    column = pl.multiple_of(pair * LANES, LANES)
    kv_ref[:, pl.ds(column, LANES)] = key
    kv_ref[:, pl.ds(HEADS * HALF + column, LANES)] = value
    even, odd = head_split(key.astype(f32), value.astype(f32))
    even = even.astype(bf16)
    odd = odd.astype(bf16)
    scaled = query.astype(f32) * (HALF**-0.5)
    for quarter in range(QUARTERS):
        first = scaled[quarter * 32 : quarter * 32 + 16]
        second = scaled[quarter * 32 + 16 : quarter * 32 + 32]
        query_even, query_odd = head_split(first, second)
        send_ref[0, quarter, 0:ROWS, :] = even
        send_ref[1, quarter, 0:ROWS, :] = odd
        send_ref[0, quarter, ROWS : ROWS + 16, :] = query_even.astype(bf16)
        send_ref[1, quarter, ROWS : ROWS + 16, :] = query_odd.astype(bf16)


def project(stream, gain, w_query, w_keyval):
    width = stream.shape[1]
    return pl.pallas_call(
        project_kernel,
        grid=(HEADS // 2,),
        in_specs=[
            pl.BlockSpec((ROWS, width), lambda i: (0, 0)),
            pl.BlockSpec((1, width), lambda i: (0, 0)),
            pl.BlockSpec((width, LANES), lambda i: (0, i)),
            pl.BlockSpec((width, LANES), lambda i: (0, i)),
            pl.BlockSpec((width, LANES), lambda i: (0, i + HEADS // 2)),
        ],
        out_specs=[
            pl.BlockSpec((ROWS, 2 * HEADS * HALF), lambda i: (0, 0)),
            pl.BlockSpec((2, QUARTERS, ROWS + 16, LANES), lambda i: (i, 0, 0, 0)),
        ],
        out_shape=[
            jax.ShapeDtypeStruct((ROWS, 2 * HEADS * HALF), bf16),
            jax.ShapeDtypeStruct((HEADS, QUARTERS, ROWS + 16, LANES), bf16),
        ],
        scratch_shapes=[pltpu.VMEM((ROWS, width), bf16)],
        name="project",
    )(stream, gain, w_query, w_keyval, w_keyval)


def prefix_pack_kernel(owner_ref, in_ref, out_ref):
    for pair in range(HEADS // 2):
        key = in_ref[0, :, pair * LANES : (pair + 1) * LANES].astype(f32)
        base = HEADS * HALF + pair * LANES
        value = in_ref[0, :, base : base + LANES].astype(f32)
        even, odd = head_split(key, value)
        for quarter in range(QUARTERS):
            out_ref[2 * pair, quarter] = even.astype(bf16)
            out_ref[2 * pair + 1, quarter] = odd.astype(bf16)


def prefix_pack(arrived, owners):
    _, rows, width = arrived.shape
    return pl.pallas_call(
        prefix_pack_kernel,
        grid_spec=pltpu.PrefetchScalarGridSpec(
            num_scalar_prefetch=1,
            grid=(1,),
            in_specs=[pl.BlockSpec((1, rows, width), lambda i, owner: (owner[0], 0, 0))],
            out_specs=pl.BlockSpec((HEADS, QUARTERS, rows, LANES), lambda i, owner: (0, 0, 0, 0)),
        ),
        out_shape=jax.ShapeDtypeStruct((HEADS, QUARTERS, rows, LANES), bf16),
        name="prefix_pack",
    )(owners, arrived)


def query_tile(got_ref, tile):
    blocks = QUERY_TILE // 32
    packed = got_ref[pl.ds(tile * blocks, blocks), ROWS : ROWS + 16, :]
    packed = packed.reshape(QUERY_TILE // 2, LANES).astype(f32)
    low = lane_of(packed.shape) < HALF
    first = jnp.where(low, packed, 0.0)
    second = jnp.where(low, pltpu.roll(packed, HALF, 1), 0.0)
    return jnp.concatenate([first, second], axis=0).astype(bf16)


def start_of(position, lengths_ref, zero):
    end = jnp.int32(0)
    start = zero
    for request in range(REQS):
        end = end + lengths_ref[request]
        start = jnp.where(position >= end, end, start)
    return start


def suffix_kernel(quarter_ref, lengths_ref, got_ref, out_ref):
    tile = pl.program_id(0)
    blocks = QUERY_TILE // 32
    key_blocks = KEY_TILE // ROWS
    query = query_tile(got_ref, tile)
    row = lax.broadcasted_iota(jnp.int32, (QUERY_TILE, 1), 0)
    half_rows = QUERY_TILE // 2
    second = (row >= half_rows).astype(jnp.int32)
    within = row - second * half_rows
    first_position = tile * blocks * ROWS + quarter_ref[0] * 32
    position = first_position + (within // 16) * ROWS + second * 16 + within % 16
    start = start_of(position, lengths_ref, jnp.zeros_like(position))
    lowest = start_of(first_position, lengths_ref, jnp.int32(0))
    span = blocks * ROWS
    last_tile = (tile * span + span - 1) // KEY_TILE

    def step(j, carry):
        acc, top, total = carry
        keys = got_ref[pl.ds(j * key_blocks, key_blocks), 0:ROWS, :].reshape(KEY_TILE, LANES)
        scores = lax.dot_general(
            query, keys, (((1,), (1,)), ((), ())), preferred_element_type=f32
        )
        key_position = j * KEY_TILE + lane_of(scores.shape)
        allowed = (key_position >= start) & (key_position <= position)
        scores = jnp.where(allowed, scores, neg_big)
        new_top = jnp.maximum(top, jnp.max(scores, axis=1, keepdims=True))
        shrink = jnp.exp(top - new_top)
        probs = jnp.exp(scores - new_top)
        total = total * shrink + jnp.sum(probs, axis=1, keepdims=True)
        acc = acc * shrink + jnp.dot(probs.astype(bf16), keys, preferred_element_type=f32)
        return acc, new_top, total

    acc, top, total = lax.fori_loop(
        lowest // KEY_TILE,
        last_tile + 1,
        step,
        (
            jnp.zeros((QUERY_TILE, LANES), f32),
            jnp.full((QUERY_TILE, 1), neg_big, f32),
            jnp.zeros((QUERY_TILE, 1), f32),
        ),
    )
    lane = lane_of(acc.shape)
    out_ref[...] = jnp.where(lane == 0, top, jnp.where(lane == 1, total, acc))


def suffix_attention(quarter, lengths, got):
    blocks = got.shape[0]
    queries = blocks * 32
    return pl.pallas_call(
        suffix_kernel,
        grid_spec=pltpu.PrefetchScalarGridSpec(
            num_scalar_prefetch=2,
            grid=(queries // QUERY_TILE,),
            in_specs=[pl.BlockSpec(got.shape, lambda i, q, l: (0, 0, 0))],
            out_specs=pl.BlockSpec((QUERY_TILE, LANES), lambda i, q, l: (i, 0)),
        ),
        out_shape=jax.ShapeDtypeStruct((queries, LANES), f32),
        compiler_params=pltpu.CompilerParams(vmem_limit_bytes=32 << 20),
        name="suffix_attention",
    )(quarter, lengths, got)


def prefix_kernel(got_ref, keys_ref, part_ref, out_ref):
    tile = pl.program_id(0)
    query = query_tile(got_ref, tile)
    keys = keys_ref[...].reshape(-1, LANES)
    scores = lax.dot_general(query, keys, (((1,), (1,)), ((), ())), preferred_element_type=f32)
    part = part_ref[...]
    part_top = part[:, 0:1]
    part_total = part[:, 1:2]
    top = jnp.maximum(part_top, jnp.max(scores, axis=1, keepdims=True))
    probs = jnp.exp(scores - top)
    shrink = jnp.exp(part_top - top)
    total = part_total * shrink + jnp.sum(probs, axis=1, keepdims=True)
    acc = part * shrink + jnp.dot(probs.astype(bf16), keys, preferred_element_type=f32)
    context = acc / total
    half_rows = QUERY_TILE // 2
    low = lane_of((half_rows, LANES)) < HALF
    packed = jnp.where(low, pltpu.roll(context[:half_rows], HALF, 1), context[half_rows:])
    out_ref[...] = packed.astype(bf16).reshape(out_ref.shape)


def prefix_attention(got, keys, part):
    blocks = got.shape[0]
    queries = blocks * 32
    tile_blocks = QUERY_TILE // 32
    return pl.pallas_call(
        prefix_kernel,
        grid=(queries // QUERY_TILE,),
        in_specs=[
            pl.BlockSpec(got.shape, lambda i: (0, 0, 0)),
            pl.BlockSpec(keys.shape, lambda i: (0, 0, 0)),
            pl.BlockSpec((QUERY_TILE, LANES), lambda i: (i, 0)),
        ],
        out_specs=pl.BlockSpec((tile_blocks, 16, LANES), lambda i: (i, 0, 0)),
        out_shape=jax.ShapeDtypeStruct((blocks, 16, LANES), bf16),
        compiler_params=pltpu.CompilerParams(vmem_limit_bytes=32 << 20),
        name="prefix_attention",
    )(got, keys, part)


def mix_kernel(ctx_ref, tok_ref, wout_ref, gain_ref, routes_ref, mixed_ref, send_ref):
    tiles = []
    for pair in range(HEADS // 2):
        even = ctx_ref[2 * pair].astype(f32)
        odd = ctx_ref[2 * pair + 1].astype(f32)
        first, second = head_split(even, odd)
        both = jnp.stack([first, second], axis=1)
        tiles.append(both.reshape(ROWS, LANES).astype(bf16))
    context = jnp.concatenate(tiles, axis=1)
    mixed = tok_ref[...].astype(f32) + jnp.dot(
        context, wout_ref[...], preferred_element_type=f32
    )
    mixed_ref[...] = mixed
    routed = rms_scale(mixed, gain_ref[...]).astype(bf16)
    expert = lax.broadcasted_iota(jnp.int32, (EXPERTS, ROWS), 0)
    named = (routes_ref[0:1, :] == expert) | (routes_ref[1:2, :] == expert)
    named_f = named.astype(f32)
    earlier = (
        lax.broadcasted_iota(jnp.int32, (ROWS, ROWS), 0)
        < lax.broadcasted_iota(jnp.int32, (ROWS, ROWS), 1)
    ).astype(bf16)
    slots = jnp.dot(named_f.astype(bf16), earlier, preferred_element_type=f32)
    slots = jnp.where(named, slots, -1.0).astype(jnp.int32)
    slot_id = lax.broadcasted_iota(jnp.int32, (SLOT_ROWS, ROWS), 0)
    for e in range(EXPERTS):
        pick = (slots[e : e + 1, :] == slot_id).astype(f32).astype(bf16)
        rows = jnp.dot(pick, routed, preferred_element_type=f32).astype(bf16)
        send_ref[e, 0] = rows
        send_ref[e, 1] = rows


def mix(ctx, stream, w_out, gain, routes_t):
    width = stream.shape[1]
    return pl.pallas_call(
        mix_kernel,
        out_shape=[
            jax.ShapeDtypeStruct((ROWS, width), f32),
            jax.ShapeDtypeStruct((EXPERTS, 2, SLOT_ROWS, width), bf16),
        ],
        compiler_params=pltpu.CompilerParams(vmem_limit_bytes=32 << 20),
        name="mix",
    )(ctx, stream, w_out, gain, routes_t)


def gelu(v):
    return 0.5 * v * (1.0 + jnp.tanh(0.7978845608028654 * (v + 0.044715 * v * v * v)))


FFN_TILE = 256


def expert_kernel(x_ref, g0, u0, d0, g1, u1, d1, out_ref, gate_v, up_v, down_v, acc_v, sems):
    sources = ((g0, u0, d0), (g1, u1, d1))
    places = (gate_v, up_v, down_v)
    copies = [
        [
            pltpu.make_async_copy(sources[part][kind], places[kind].at[part], sems.at[part, kind])
            for kind in range(3)
        ]
        for part in range(2)
    ]
    for part in range(2):
        for kind in range(3):
            copies[part][kind].start()
    for part in range(2):
        for tile in range(x_ref.shape[0] // FFN_TILE):
            rows = slice(tile * FFN_TILE, (tile + 1) * FFN_TILE)
            if tile == 0:
                copies[part][0].wait()
                copies[part][1].wait()
            x = x_ref[rows, :]
            gate = jnp.dot(x, gate_v[part], preferred_element_type=f32)
            up = jnp.dot(x, up_v[part], preferred_element_type=f32)
            hidden = (gelu(gate) * up).astype(bf16)
            if tile == 0:
                copies[part][2].wait()
            down = jnp.dot(hidden, down_v[part], preferred_element_type=f32)
            if part == 0:
                acc_v[rows, :] = down
            else:
                out_ref[rows, :] = (acc_v[rows, :] + down).astype(bf16)


def expert(rows, own, other):
    count, width = rows.shape
    units = own[0].shape[1]
    hbm = pl.BlockSpec(memory_space=pl.ANY)
    vmem = pl.BlockSpec(memory_space=pltpu.VMEM)
    return pl.pallas_call(
        expert_kernel,
        in_specs=[vmem] + [hbm] * 6,
        out_specs=vmem,
        out_shape=jax.ShapeDtypeStruct((count, width), bf16),
        scratch_shapes=[
            pltpu.VMEM((2, width, units), bf16),
            pltpu.VMEM((2, width, units), bf16),
            pltpu.VMEM((2, units, width), bf16),
            pltpu.VMEM((count, width), f32),
            pltpu.SemaphoreType.DMA((2, 3)),
        ],
        compiler_params=pltpu.CompilerParams(vmem_limit_bytes=48 << 20),
        name="expert",
    )(rows, *own, *other)


def combine_kernel(
    block_ref, lengths_ref, mixed_ref, got_ref, routes_ref, gates_ref, gain_ref, hidden_ref, last_ref, norm_ref
):
    routes = routes_ref[...]
    first = routes[:, 0:1]
    second = routes[:, 1:2]
    lane = lane_of((ROWS, LANES))
    named = ((first == lane) | (second == lane)).astype(f32).astype(bf16)
    earlier = (
        lax.broadcasted_iota(jnp.int32, (ROWS, ROWS), 1)
        < lax.broadcasted_iota(jnp.int32, (ROWS, ROWS), 0)
    ).astype(bf16)
    slots = jnp.dot(earlier, named, preferred_element_type=f32)
    got = got_ref[...]
    column = lane_of((ROWS, got.shape[0]))
    gates = gates_ref[...]
    hidden = mixed_ref[...]
    moe = None
    for which, chosen in enumerate((first, second)):
        slot = jnp.sum(jnp.where(chosen == lane, slots, 0.0), axis=1, keepdims=True)
        target = chosen * (2 * SLOT_ROWS) + slot.astype(jnp.int32)
        pick = ((column == target) | (column == target + SLOT_ROWS)).astype(f32).astype(bf16)
        picked = jnp.dot(pick, got, preferred_element_type=f32)
        term = gates[:, which : which + 1] * picked
        moe = term if moe is None else moe + term
    hidden = (hidden + moe).astype(bf16)
    hidden_ref[...] = hidden
    wide = hidden.astype(f32)
    squares = jnp.sum(wide * wide, axis=1, keepdims=True)
    position = block_ref[0] * ROWS + lax.broadcasted_iota(jnp.int32, (ROWS, LANES), 0)
    starts = jnp.zeros((1, LANES), jnp.int32)
    ends = jnp.zeros((1, LANES), jnp.int32)
    lasts = jnp.full((REQS, LANES), -1, jnp.int32)
    request = lax.broadcasted_iota(jnp.int32, (REQS, LANES), 0)
    lane_row = lane_of((1, LANES))
    end = jnp.int32(0)
    for r in range(REQS):
        starts = jnp.where(lane_row == r, end, starts)
        end = end + lengths_ref[r]
        ends = jnp.where(lane_row == r, end, ends)
        lasts = jnp.where(request == r, end - 1, lasts)
    member = (position >= starts) & (position < ends)
    norm_ref[...] = jnp.sum(jnp.where(member, squares, 0.0), axis=0, keepdims=True)
    final = rms_scale(wide, gain_ref[...]).astype(bf16)
    is_last = (lasts == block_ref[0] * ROWS + lane_of((REQS, LANES))).astype(f32).astype(bf16)
    last_ref[...] = jnp.dot(is_last, final, preferred_element_type=f32).astype(bf16)


def combine(block, lengths, mixed, got, routes, gates, gain):
    width = mixed.shape[1]
    vmem = pl.BlockSpec(memory_space=pltpu.VMEM)
    smem = pl.BlockSpec(memory_space=pltpu.SMEM)
    return pl.pallas_call(
        combine_kernel,
        in_specs=[smem, smem] + [vmem] * 5,
        out_specs=[vmem] * 3,
        out_shape=[
            jax.ShapeDtypeStruct((ROWS, width), bf16),
            jax.ShapeDtypeStruct((REQS, width), bf16),
            jax.ShapeDtypeStruct((1, LANES), f32),
        ],
        compiler_params=pltpu.CompilerParams(vmem_limit_bytes=32 << 20),
        name="combine",
    )(block, lengths, mixed, got, routes, gates, gain)


def exchange(rows):
    return lax.all_to_all(rows, "blk", split_axis=0, concat_axis=0, tiled=True)


def local(
    tokens,
    lengths,
    owners,
    prefix_cache,
    routes,
    gates,
    attn_gain,
    w_query,
    w_keyval,
    w_out,
    moe_gain,
    w_gate,
    w_up,
    w_down,
    final_gain,
    unembed,
):
    blocks = lax.axis_size("blk")
    block_index = lax.axis_index("blk")
    width = tokens.shape[2]
    stream = tokens[0]
    block = block_index.astype(jnp.int32).reshape(1)
    quarter = block % QUARTERS
    swap = [(i, i ^ 1) for i in range(blocks)]
    with jax.named_scope("prefix_gather"):
        arrived = lax.all_gather(prefix_cache, "grp", axis=0, tiled=True)
    with jax.named_scope("weight_swap"):
        own = (w_gate[0], w_up[0], w_down[0])
        other = tuple(lax.ppermute(one, "blk", swap) for one in own)
    suffix_kv, send = project(stream, attn_gain.reshape(1, -1), w_query, w_keyval)
    with jax.named_scope("qkv_exchange"):
        got = exchange(send.reshape(blocks, ROWS + 16, LANES))
    part = suffix_attention(quarter, lengths[0], got)
    packed = prefix_pack(arrived, owners)
    with jax.named_scope("prefix_exchange"):
        prefix_keys = exchange(packed.reshape(blocks, packed.shape[2], LANES))
    context = prefix_attention(got, prefix_keys, part)
    with jax.named_scope("context_exchange"):
        ctx = exchange(context).reshape(HEADS, QUARTERS, 16, LANES)
    mixed, outgoing = mix(ctx, stream, w_out, moe_gain.reshape(1, -1), routes[0].T)
    with jax.named_scope("dispatch_exchange"):
        rows = exchange(outgoing.reshape(blocks, SLOT_ROWS // 2, width))
    results = expert(rows.reshape(-1, width), own, other)
    with jax.named_scope("return_exchange"):
        returned = exchange(results.reshape(blocks, SLOT_ROWS // 2, width)).reshape(-1, width)
    hidden, last_terms, norm_terms = combine(
        block, lengths[0], mixed, returned, routes[0], gates[0], final_gain.reshape(1, -1)
    )
    with jax.named_scope("last_exchange"):
        spread = jnp.broadcast_to(last_terms[None], (blocks,) + last_terms.shape)
        last_rows = jnp.sum(exchange(spread).astype(f32), axis=0).astype(bf16)
    logits = jnp.dot(last_rows, unembed, preferred_element_type=f32)
    best = jnp.max(logits, axis=1)
    with jax.named_scope("final_exchange"):
        final = jnp.concatenate([norm_terms[:, :REQS], best[None, :]], axis=1)
        final = jnp.pad(final, ((0, 0), (0, LANES - 2 * REQS)))
        final = exchange(jnp.broadcast_to(final[None], (blocks, 1, LANES)))[:, 0, :]
    norm_sums = jnp.sum(final[:, :REQS], axis=0)
    greatest = jnp.max(final[:, REQS : 2 * REQS], axis=0)
    request_norm = jnp.sqrt(norm_sums / (lengths[0].astype(f32) * width))
    return (hidden[None], suffix_kv[None], request_norm[None], greatest[None])


def solution(mesh):
    placed = (
        P("grp", "blk", None),
        P("grp", None),
        P("grp"),
        P("grp", "blk", None),
        P("grp", "blk", None),
        P("grp", "blk", None),
        P(),
        P(),
        P(),
        P(),
        P(),
        P("blk", None, None),
        P("blk", None, None),
        P("blk", None, None),
        P(),
        P(None, "blk"),
    )
    return jax.shard_map(
        local,
        mesh=mesh,
        in_specs=placed,
        out_specs=(P("grp", "blk", None), P("grp", "blk", None), P("grp", None), P("grp", None)),
        check_vma=False,
    )
```

time: 507 us -> 212 us (0.42)
  blocking collectives: 227 us -> 31.7 us
  waiting for transfers between devices: 167 us -> 71.4 us
  matrix products: 39.4 us -> 0.76 us
  Pallas kernels: 0 us -> 36 us
  starting transfers between devices: 4.83 us -> 35.5 us
  local copies, waits for them, and re-layouts: 35.1 us -> 17.7 us
  other arithmetic: 15.5 us -> 2.59 us
    psum x1 -> x0, blocking collectives: 120 us -> none  [local(): lax.psum(norm_terms.astype(jnp.bfloat16), 'blk').astype(jnp.float32)]
    all_gather x2 -> x0, waiting for transfers between devices: 94.5 us -> none  [the longest x1 48.1 us: local(): lax.all_gather(owner_prefix, 'blk', axis=0, tiled=True)]
    pmax x1 -> x0, blocking collectives: 68.2 us -> none  [local(): greatest = lax.pmax(jnp.max(logits, axis=1), 'blk')]
    dot_general x12 -> x1, matrix products: 39.4 us -> 0.76 us  [local(): logits = jnp.dot(last_rows, unembed, preferred_element_type=f32)]
    pallas_call x0 -> x7, Pallas kernels: none -> 36 us  [the longest x1 11.4 us: expert(): pl.pallas_call(expert_kernel, in_specs=[vmem] + [hbm] * 6, out_specs=vmem...]
    all_to_all x1 -> x5, starting transfers between devices: 4.72 us -> 34.5 us  [exchange(): return lax.all_to_all(rows, 'blk', split_axis=0, concat_axis=0, tiled=True)]
    slice x9 -> x0, local copies, waits for them, and re-layouts: 16.3 us -> none  [the longest x3 12.8 us: attend_piece(): key_part[:, :attn_width].reshape(piece_rows, head_count, head_size)]
    all_gather x1, waiting for transfers between devices: 38.4 us -> 25.9 us  [local(): arrived = lax.all_gather(prefix_cache, 'grp', axis=0, tiled=True)]
  transfers between devices with their start and end apart: 4 -> 9, of which waited for: 4 -> 5; matrix products, arithmetic and copies ran while one was open for 4% -> 5% of each run, Pallas kernels for 0% -> 7%
where the time goes in v1:
time: 212 us; the launch traced here: 211 us
  waiting for transfers between devices  71.4 us (34%)
  Pallas kernels  36 us (17%)
  starting transfers between devices  35.5 us (17%)
  blocking collectives  31.7 us (15%)
  local copies, waits for them, and re-layouts  17.7 us (8%)
  between operations  14.9 us (7%)
  other arithmetic  2.59 us (1%)
    all_to_all x5, waiting for transfers between devices, exchange(): return lax.all_to_all(rows, 'blk', split_axis=0, concat_axis=0, tiled=True)  44.8 us
    all_to_all x5, starting transfers between devices, exchange(): return lax.all_to_all(rows, 'blk', split_axis=0, concat_axis=0, tiled=True)  34.5 us
    all_to_all x2, blocking collectives, exchange(): return lax.all_to_all(rows, 'blk', split_axis=0, concat_axis=0, tiled=True)  31.7 us
    all_gather x1, waiting for transfers between devices, local(): arrived = lax.all_gather(prefix_cache, 'grp', axis=0, tiled=True)  25.9 us
    unnamed x40, local copies, waits for them, and re-layouts  12.3 us
    pallas_call x1, Pallas kernels, expert(): pl.pallas_call(expert_kernel, in_specs=[vmem] + [hbm] * 6, out_specs=vmem...  11.4 us
    pallas_call x1, Pallas kernels, suffix_attention(): pl.pallas_call(suffix_kernel, grid_spec=pltpu.PrefetchScalarGridSpec(num_...  7.67 us
    pallas_call x1, Pallas kernels, prefix_attention(): pl.pallas_call(prefix_kernel, grid=(queries // QUERY_TILE,), in_specs=[pl...  6.1 us
  transfers between devices with their start and end apart: 9, of which 5 were waited for; matrix products, arithmetic and copies ran while one was open for 5% of the time, Pallas kernels for 7%

profile of v1, /device:TPU:1, one launch (start us, length us, event | category | flops | bytes accessed | tf_op | source)
XLA Modules:
  0.0 210.6 jit_solution(6020792682684464520)
XLA Ops:
  7.2 0.7 all-gather.2.cloned.1.call-update
  7.9 5.0 %project.1 = (bf16[128,1024]{1,0:T(8,128)(2,1)}, bf16[8,4,144,128]{3,2,1,0:T(8,128)(2,1)}) custom-call(bf16[128,1024]{1,0:T(8,128)(2,1)} %bitcast.40, f32[1,1024]{1,0:T(1,128)} %bitcast.58, bf16[1024,512]{1,0:T(8,128)(2,1)} %wq_ref.1, bf16[1024,1024]{1,0:T(8,128)(2,1)} %wv_ref.1, bf16[1024,1024]{1,0:T(8,128)(2,1)} %wv_ref.1), custom_call_target="tpu_custom_call" | custom-call | tf_op jit(solution)/shard_map/project/pallas_call | solution.py:74
  12.9 8.6 %all-to-all-start = ((bf16[32,144,128]{2,1,0:T(8,128)(2,1)}), bf16[32,144,128]{2,1,0:T(8,128)(2,1)S(1)}, u32[]{:S(2)}, u32[]{:S(2)}) async-start(bf16[32,144,128]{2,1,0:T(8,128)(2,1)} %bitcast.56), calls=%async_computation | async-start | bytes 2359296 | tf_op jit(solution)/shard_map/qkv_exchange/all_to_all | solution.py:416
  22.2 25.9 %all-gather.2.cloned.1.call-done.in_ref = bf16[8,64,1024]{2,1,0:T(8,128)(2,1)} async-done(((bf16[1,64,1024]{2,1,0:T(8,128)(2,1)}), bf16[8,64,1024]{2,1,0:T(8,128)(2,1)}) %all-gather.2.cloned.1.call-update) | async-done | bytes 1048592 | tf_op jit(solution)/shard_map/prefix_gather/all_gather | solution.py:445
  48.1 1.8 prefix_pack.1
  49.9 11.7 %all-to-all-start.1 = ((bf16[32,64,128]{2,1,0:T(8,128)(2,1)}), bf16[32,64,128]{2,1,0:T(8,128)(2,1)}, u32[]{:S(2)}, u32[]{:S(2)}) async-start(bf16[32,64,128]{2,1,0:T(8,128)(2,1)} %bitcast.53), calls=%async_computation.1 | async-start | bytes 1048576 | tf_op jit(solution)/shard_map/prefix_exchange/all_to_all | solution.py:416
  61.7 7.7 %suffix_attention.1.part_ref = f32[1024,128]{1,0:T(8,128)S(1)} custom-call(s32[1]{0:T(128)S(6)} %select_n.7.quarter_ref, s32[16]{0:T(128)S(1)} %bitcast.48, bf16[32,144,128]{2,1,0:T(8,128)(2,1)S(1)} %all-to-all-done.got_ref), custom_call_target="tpu_custom_call" | custom-call | tf_op jit(solution)/shard_map/suffix_attention/pallas_call | solution.py:191
  69.3 0.8 copy-done.2
  70.1 3.2 %all-to-all-done.1.keys_ref = bf16[32,64,128]{2,1,0:T(8,128)(2,1)} async-done(((bf16[32,64,128]{2,1,0:T(8,128)(2,1)}), bf16[32,64,128]{2,1,0:T(8,128)(2,1)}, u32[]{:S(2)}, u32[]{:S(2)}) %all-to-all-start.1) | async-done | bytes 524320 | tf_op jit(solution)/shard_map/prefix_exchange/all_to_all | solution.py:416
  73.3 1.0 copy-done.3
  74.4 6.1 %prefix_attention.1 = bf16[32,16,128]{2,1,0:T(8,128)(2,1)S(1)} custom-call(bf16[32,144,128]{2,1,0:T(8,128)(2,1)S(1)} %all-to-all-done.got_ref, bf16[32,64,128]{2,1,0:T(8,128)(2,1)} %all-to-all-done.1.keys_ref, f32[1024,128]{1,0:T(8,128)S(1)} %copy-done.3), custom_call_target="tpu_custom_call" | custom-call | tf_op jit(solution)/shard_map/prefix_attention/pallas_call | solution.py:229
  81.1 4.2 %all-to-all-start.2 = ((bf16[32,16,128]{2,1,0:T(8,128)(2,1)}), bf16[32,16,128]{2,1,0:T(8,128)(2,1)S(1)}, u32[]{:S(2)}, u32[]{:S(2)}) async-start(bf16[32,16,128]{2,1,0:T(8,128)(2,1)} %copy-done.10), calls=%async_computation.2 | async-start | bytes 262144 | tf_op jit(solution)/shard_map/context_exchange/all_to_all | solution.py:416
  85.5 7.5 %all-to-all-done.2 = bf16[32,16,128]{2,1,0:T(8,128)(2,1)S(1)} async-done(((bf16[32,16,128]{2,1,0:T(8,128)(2,1)}), bf16[32,16,128]{2,1,0:T(8,128)(2,1)S(1)}, u32[]{:S(2)}, u32[]{:S(2)}) %all-to-all-start.2) | async-done | bytes 131104 | tf_op jit(solution)/shard_map/context_exchange/all_to_all | solution.py:416
  93.1 1.2 copy-done.7
  94.3 0.9 mix.1
  95.2 1.2 copy-done.4
  96.3 0.8 copy-done.11
  97.2 4.8 %all-to-all-start.3 = ((bf16[32,24,1024]{2,1,0:T(8,128)(2,1)}), bf16[32,24,1024]{2,1,0:T(8,128)(2,1)}, u32[]{:S(2)}, u32[]{:S(2)}) async-start(bf16[32,24,1024]{2,1,0:T(8,128)(2,1)} %bitcast.37), calls=%async_computation.3 | async-start | bytes 3145728 | tf_op jit(solution)/shard_map/dispatch_exchange/all_to_all | solution.py:416
  103.0 2.6 %copy.45 = bf16[1,1024,704]{2,1,0:T(8,128)(2,1)} copy(bf16[1,1024,704]{1,2,0:T(8,128)(2,1)} %param.27) | data formatting | bytes 2883584 | tf_op args[11]
  105.6 2.6 %copy.46 = bf16[1,1024,704]{2,1,0:T(8,128)(2,1)} copy(bf16[1,1024,704]{1,2,0:T(8,128)(2,1)} %param.28) | data formatting | bytes 2883584 | tf_op args[12]
  108.1 2.6 %copy.49.g1 = bf16[1024,704]{1,0:T(8,128)(2,1)} copy(bf16[1024,704]{0,1:T(8,128)(2,1)} %collective-permute-done) | data formatting | bytes 2883584 | tf_op jit(solution)/shard_map/weight_swap/ppermute | solution.py:448
  110.7 2.6 %copy.50.u1 = bf16[1024,704]{1,0:T(8,128)(2,1)} copy(bf16[1024,704]{0,1:T(8,128)(2,1)} %collective-permute-done.1) | data formatting | bytes 2883584 | tf_op jit(solution)/shard_map/weight_swap/ppermute | solution.py:448
  113.4 11.4 %all-to-all-done.3 = bf16[32,24,1024]{2,1,0:T(8,128)(2,1)} async-done(((bf16[32,24,1024]{2,1,0:T(8,128)(2,1)}), bf16[32,24,1024]{2,1,0:T(8,128)(2,1)}, u32[]{:S(2)}, u32[]{:S(2)}) %all-to-all-start.3) | async-done | bytes 1572896 | tf_op jit(solution)/shard_map/dispatch_exchange/all_to_all | solution.py:416
  124.8 11.4 %expert.1 = bf16[768,1024]{1,0:T(8,128)(2,1)S(1)} custom-call(bf16[768,1024]{1,0:T(8,128)(2,1)} %bitcast.11.x_ref, bf16[1024,704]{1,0:T(8,128)(2,1)} %bitcast.51, bf16[1024,704]{1,0:T(8,128)(2,1)} %bitcast.52, bf16[704,1024]{1,0:T(8,128)(2,1)S(1)} %bitcast.39, bf16[1024,704]{1,0:T(8,128)(2,1)} %copy.49.g1, bf16[1024,704]{1,0:T(8,128)(2,1)} %copy.50.u1, ...), custom_call_target="tpu_custom_call" | custom-call | tf_op jit(solution)/shard_map/expert/pallas_call | solution.py:332
  136.2 1.1 copy-done.1
  137.3 5.1 %all-to-all-start.4 = ((bf16[32,24,1024]{2,1,0:T(8,128)(2,1)}), bf16[32,24,1024]{2,1,0:T(8,128)(2,1)}, u32[]{:S(2)}, u32[]{:S(2)}) async-start(bf16[32,24,1024]{2,1,0:T(8,128)(2,1)} %bitcast.36), calls=%async_computation.4 | async-start | bytes 3145728 | tf_op jit(solution)/shard_map/return_exchange/all_to_all | solution.py:416
  142.6 22.7 %all-to-all-done.4 = bf16[32,24,1024]{2,1,0:T(8,128)(2,1)} async-done(((bf16[32,24,1024]{2,1,0:T(8,128)(2,1)}), bf16[32,24,1024]{2,1,0:T(8,128)(2,1)}, u32[]{:S(2)}, u32[]{:S(2)}) %all-to-all-start.4) | async-done | bytes 1572896 | tf_op jit(solution)/shard_map/return_exchange/all_to_all | solution.py:416
  165.3 3.2 %combine.1 = (bf16[128,1024]{1,0:T(8,128)(2,1)}, bf16[16,1024]{1,0:T(8,128)(2,1)S(1)}, f32[1,128]{1,0:T(1,128)S(1)}) custom-call(s32[1]{0:T(128)} %bitcast.block_ref, s32[16]{0:T(128)S(1)} %bitcast.49, f32[128,1024]{1,0:T(8,128)S(1)} %copy-done.12, bf16[768,1024]{1,0:T(8,128)(2,1)} %bitcast.18.got_ref, s32[128,2]{1,0:T(8,128)S(1)} %bitcast.43, ...), custom_call_target="tpu_custom_call" | custom-call | tf_op jit(solution)/shard_map/combine/pallas_call | solution.py:401
  168.6 21.0 %all_to_all.35 = bf16[32,16,1024]{2,1,0:T(8,128)(2,1)} all-to-all(bf16[32,16,1024]{2,1,0:T(8,128)(2,1)S(1)} %broadcast_in_dim.29), channel_id=1, replica_groups=mesh['grp'=8,'blk'=32] {'blk'}, dimensions={0} | all-to-all | bytes 2097152 | tf_op jit(solution)/shard_map/last_exchange/all_to_all | solution.py:416
  189.7 1.4 reduce_sum.23
  191.1 0.8 convolution_reduce_fusion
  191.9 10.7 %all_to_all.36 = f32[32,1,128]{2,1,0:T(1,128)S(1)} all-to-all(f32[32,1,128]{2,1,0:T(1,128)S(1)} %broadcast_in_dim.32), channel_id=1, replica_groups=mesh['grp'=8,'blk'=32] {'blk'}, dimensions={0} | all-to-all | bytes 32768 | tf_op jit(solution)/shard_map/final_exchange/all_to_all | solution.py:416
  (46 shorter events, 3.4 us)
Async XLA Ops:
  7.2 183.9 %copy-start = (bf16[1024,1004]{0,1:T(8,128)(2,1)S(1)}, bf16[1024,1004]{0,1:T(8,128)(2,1)}, u32[]{:S(2)}) copy-start(bf16[1024,1004]{0,1:T(8,128)(2,1)} %param.31) | copy-start | bytes 6168580
  7.2 40.9 %all-gather.2.cloned.1.call-start = ((), (), s32[]{:S(2)}) async-start(), calls=%async_computation.7 | async-start | bytes 1179648 | tf_op jit(solution)/shard_map/prefix_gather/all_gather | solution.py:445
  12.9 37.0 %all-to-all-start = ((bf16[32,144,128]{2,1,0:T(8,128)(2,1)}), bf16[32,144,128]{2,1,0:T(8,128)(2,1)S(1)}, u32[]{:S(2)}, u32[]{:S(2)}) async-start(bf16[32,144,128]{2,1,0:T(8,128)(2,1)} %bitcast.56), calls=%async_computation | async-start | bytes 2359296 | tf_op jit(solution)/shard_map/qkv_exchange/all_to_all | solution.py:416
  21.5 40.1 %copy-start.15 = (s32[1,16]{1,0:T(1,128)S(1)}, s32[1,16]{1,0:T(1,128)}, u32[]{:S(2)}) copy-start(s32[1,16]{1,0:T(1,128)} %param.17) | copy-start | bytes 196
  49.9 23.4 %all-to-all-start.1 = ((bf16[32,64,128]{2,1,0:T(8,128)(2,1)}), bf16[32,64,128]{2,1,0:T(8,128)(2,1)}, u32[]{:S(2)}, u32[]{:S(2)}) async-start(bf16[32,64,128]{2,1,0:T(8,128)(2,1)} %bitcast.53), calls=%async_computation.1 | async-start | bytes 1048576 | tf_op jit(solution)/shard_map/prefix_exchange/all_to_all | solution.py:416
  69.3 0.8 copy-start.2
  73.3 1.0 copy-start.3
  74.3 11.0 %copy-start.16 = (s32[1,128,2]{1,2,0:T(2,128)S(1)}, s32[1,128,2]{1,2,0:T(2,128)}, u32[]{:S(2)}) copy-start(s32[1,128,2]{1,2,0:T(2,128)} %param.20) | copy-start | bytes 3076
  74.4 18.7 %copy-start.6 = (bf16[1,128,1024]{2,1,0:T(8,128)(2,1)S(1)}, bf16[1,128,1024]{2,1,0:T(8,128)(2,1)}, u32[]{:S(2)}) copy-start(bf16[1,128,1024]{2,1,0:T(8,128)(2,1)} %param.16) | copy-start | bytes 786436
  74.4 18.7 %copy-start.13 = (f32[1024]{0:T(1024)S(1)}, f32[1024]{0:T(1024)}, u32[]{:S(2)}) copy-start(f32[1024]{0:T(1024)} %param.26) | copy-start | bytes 12292
  80.5 0.7 copy-start.10
  81.1 11.9 %all-to-all-start.2 = ((bf16[32,16,128]{2,1,0:T(8,128)(2,1)}), bf16[32,16,128]{2,1,0:T(8,128)(2,1)S(1)}, u32[]{:S(2)}, u32[]{:S(2)}) async-start(bf16[32,16,128]{2,1,0:T(8,128)(2,1)} %copy-done.10), calls=%async_computation.2 | async-start | bytes 262144 | tf_op jit(solution)/shard_map/context_exchange/all_to_all | solution.py:416
  85.5 11.7 %copy-start.8 = (s32[1,128,2]{2,1,0:T(8,128)}, s32[1,128,2]{2,1,0:T(8,128)S(1)}, u32[]{:S(2)}) copy-start(s32[1,128,2]{2,1,0:T(8,128)S(1)} %copy.43) | copy-start | bytes 3076
  93.0 1.2 copy-start.7
  95.1 1.2 copy-start.4
  96.3 0.8 copy-start.11
  97.1 5.4 %copy-start.5 = (bf16[1,704,1024]{2,1,0:T(8,128)(2,1)S(1)}, bf16[1,704,1024]{2,1,0:T(8,128)(2,1)}, u32[]{:S(2)}) copy-start(bf16[1,704,1024]{2,1,0:T(8,128)(2,1)} %param.29) | copy-start | bytes 4325380
  97.2 27.7 %all-to-all-start.3 = ((bf16[32,24,1024]{2,1,0:T(8,128)(2,1)}), bf16[32,24,1024]{2,1,0:T(8,128)(2,1)}, u32[]{:S(2)}, u32[]{:S(2)}) async-start(bf16[32,24,1024]{2,1,0:T(8,128)(2,1)} %bitcast.37), calls=%async_computation.3 | async-start | bytes 3145728 | tf_op jit(solution)/shard_map/dispatch_exchange/all_to_all | solution.py:416
  102.0 6.2 %collective-permute-start = (bf16[1024,704]{0,1:T(8,128)(2,1)}, bf16[1024,704]{0,1:T(8,128)(2,1)}, u32[]{:S(2)}, u32[]{:S(2)}) collective-permute-start(bf16[1024,704]{0,1:T(8,128)(2,1)} %bitcast.54), channel_id=1, source_target_pairs={{0,1},{1,0},{2,3},{3,2},{4,5},{5,4},{6,7},{7,6},{8,9},{9,8},{10,11... | collective-permute-start | bytes 4325384 | tf_op jit(solution)/shard_map/weight_swap/ppermute | solution.py:448
  102.5 8.2 %collective-permute-start.1 = (bf16[1024,704]{0,1:T(8,128)(2,1)}, bf16[1024,704]{0,1:T(8,128)(2,1)}, u32[]{:S(2)}, u32[]{:S(2)}) collective-permute-start(bf16[1024,704]{0,1:T(8,128)(2,1)} %bitcast.55), channel_id=1, source_target_pairs={{0,1},{1,0},{2,3},{3,2},{4,5},{5,4},{6,7},{7,6},{8,9},{9,8},{10,11... | collective-permute-start | bytes 4325384 | tf_op jit(solution)/shard_map/weight_swap/ppermute | solution.py:448
  102.6 10.8 %collective-permute-start.2 = (bf16[704,1024]{1,0:T(8,128)(2,1)S(1)}, bf16[704,1024]{1,0:T(8,128)(2,1)}, u32[]{:S(2)}, u32[]{:S(2)}) collective-permute-start(bf16[704,1024]{1,0:T(8,128)(2,1)S(1)} %bitcast.38), channel_id=1, source_target_pairs={{0,1},{1,0},{2,3},{3,2},{4,5},{5,4},{6,7},{7,6},{8,9},{9,8},{10,11... | collective-permute-start | bytes 4325384 | tf_op jit(solution)/shard_map/weight_swap/ppermute | solution.py:448
  136.2 1.1 copy-start.1
  137.3 5.1 %copy-start.17 = (f32[1,128,2]{1,2,0:T(2,128)S(1)}, f32[1,128,2]{1,2,0:T(2,128)}, u32[]{:S(2)}) copy-start(f32[1,128,2]{1,2,0:T(2,128)} %param.21) | copy-start | bytes 3076
  137.3 28.0 %copy-start.9 = (s32[1,128,2]{2,1,0:T(8,128)S(1)}, s32[1,128,2]{2,1,0:T(8,128)}, u32[]{:S(2)}) copy-start(s32[1,128,2]{2,1,0:T(8,128)} %copy-done.8) | copy-start | bytes 3076
  137.3 28.0 %copy-start.12 = (f32[128,1024]{1,0:T(8,128)S(1)}, f32[128,1024]{1,0:T(8,128)}, u32[]{:S(2)}) copy-start(f32[128,1024]{1,0:T(8,128)} %copy-done.11) | copy-start | bytes 1572868
  137.3 28.0 %copy-start.14 = (f32[1024]{0:T(1024)S(1)}, f32[1024]{0:T(1024)}, u32[]{:S(2)}) copy-start(f32[1024]{0:T(1024)} %param.30) | copy-start | bytes 12292
  137.3 27.9 %all-to-all-start.4 = ((bf16[32,24,1024]{2,1,0:T(8,128)(2,1)}), bf16[32,24,1024]{2,1,0:T(8,128)(2,1)}, u32[]{:S(2)}, u32[]{:S(2)}) async-start(bf16[32,24,1024]{2,1,0:T(8,128)(2,1)} %bitcast.36), calls=%async_computation.4 | async-start | bytes 3145728 | tf_op jit(solution)/shard_map/return_exchange/all_to_all | solution.py:416
Sparse Core Ops, SparseCore 0:
  9.8 38.2 all-gather.1

commit v2 on v1

v2 whole, which is shorter than its diff:
```python
import jax
import jax.numpy as jnp
from jax import lax
from jax.experimental import pallas as pl
from jax.experimental.pallas import tpu as pltpu
from jax.sharding import PartitionSpec as P

HEADS = 8
EXPERTS = 8
QUARTERS = 4
CAP = 40
SLOT_ROWS = 48
PART_ROWS = 24
PART_SLOTS = 20
SEND_ROWS = 176
REQS = 16
ROWS = 128
HALF = 64
LANES = 128
KEY_TILE = 1024
QUERY_TILE = 256

epsilon = 1e-06
neg_big = -1e30
bf16 = jnp.bfloat16
f32 = jnp.float32


def rms_scale(values, gain_vector):
    return (
        values * lax.rsqrt(jnp.mean(values * values, axis=-1, keepdims=True) + epsilon) * gain_vector
    )


def lane_of(shape):
    return lax.broadcasted_iota(jnp.int32, shape, len(shape) - 1)


def head_split(first, second):
    low = lane_of(first.shape) < HALF
    axis = len(first.shape) - 1
    even = jnp.where(low, first, pltpu.roll(second, HALF, axis))
    odd = jnp.where(low, pltpu.roll(first, HALF, axis), second)
    return even, odd


def last_matrix(lengths_ref, positions):
    request = lax.broadcasted_iota(jnp.int32, positions.shape, 0)
    lasts = jnp.full(positions.shape, -1, jnp.int32)
    end = jnp.int32(0)
    for r in range(REQS):
        end = end + lengths_ref[r]
        lasts = jnp.where(request == r, end - 1, lasts)
    return (lasts == positions).astype(f32).astype(bf16)


def three_parts(values):
    high = values.astype(bf16).astype(f32)
    middle = (values - high).astype(bf16).astype(f32)
    low = (values - high - middle).astype(bf16).astype(f32)
    return high, middle, low


def project_kernel(
    block_ref, lengths_ref, tok_ref, gain_ref, wq_ref, wk_ref, wv_ref, routes_ref, gates_ref,
    kv_ref, send_ref, normed_ref, gate_ref,
):
    pair = pl.program_id(0)
    is_last = last_matrix(lengths_ref, block_ref[0] * ROWS + lane_of((REQS, ROWS)))

    @pl.when(pair == 0)
    def _():
        normed_ref[...] = rms_scale(tok_ref[...].astype(f32), gain_ref[...]).astype(bf16)
        row = lax.broadcasted_iota(jnp.int32, (LANES, ROWS), 0)
        named = row % EXPERTS
        weight = jnp.where(
            routes_ref[0:1, :] == named,
            gates_ref[0:1, :],
            jnp.where(routes_ref[1:2, :] == named, gates_ref[1:2, :], 0.0),
        )
        high, middle, low = three_parts(weight)
        piece = row // EXPERTS
        pieces = jnp.where(
            piece == 0, high, jnp.where(piece == 1, middle, jnp.where(piece == 2, low, 0.0))
        )
        gate_ref[...] = lax.dot_general(
            is_last, pieces.astype(bf16), (((1,), (1,)), ((), ())), preferred_element_type=f32
        ).astype(bf16)

    normed = normed_ref[...]
    query = jnp.dot(normed, wq_ref[...], preferred_element_type=f32).astype(bf16)
    key = jnp.dot(normed, wk_ref[...], preferred_element_type=f32).astype(bf16)
    value = jnp.dot(normed, wv_ref[...], preferred_element_type=f32).astype(bf16)
    column = pl.multiple_of(pair * LANES, LANES)
    kv_ref[:, pl.ds(column, LANES)] = key
    kv_ref[:, pl.ds(HEADS * HALF + column, LANES)] = value
    even, odd = head_split(key.astype(f32), value.astype(f32))
    even = even.astype(bf16)
    odd = odd.astype(bf16)
    wide = pl.multiple_of(pair * 2 * LANES, 2 * LANES)
    ends = jnp.dot(
        is_last, tok_ref[:, pl.ds(wide, 2 * LANES)], preferred_element_type=f32
    ).astype(bf16)
    scaled = query.astype(f32) * (HALF**-0.5)
    for quarter in range(QUARTERS):
        first = scaled[quarter * 32 : quarter * 32 + 16]
        second = scaled[quarter * 32 + 16 : quarter * 32 + 32]
        query_even, query_odd = head_split(first, second)
        send_ref[0, quarter, 0:ROWS, :] = even
        send_ref[1, quarter, 0:ROWS, :] = odd
        send_ref[0, quarter, ROWS : ROWS + 16, :] = query_even.astype(bf16)
        send_ref[1, quarter, ROWS : ROWS + 16, :] = query_odd.astype(bf16)
        for which in range(2):
            send_ref[which, quarter, ROWS + 16 : ROWS + 32, :] = ends[
                :, which * LANES : (which + 1) * LANES
            ]
            send_ref[which, quarter, ROWS + 32 : ROWS + 48, :] = gate_ref[...]


def project(block, lengths, stream, gain, w_query, w_keyval, routes_t, gates_t):
    width = stream.shape[1]
    return pl.pallas_call(
        project_kernel,
        grid_spec=pltpu.PrefetchScalarGridSpec(
            num_scalar_prefetch=2,
            grid=(HEADS // 2,),
            in_specs=[
                pl.BlockSpec((ROWS, width), lambda i, b, l: (0, 0)),
                pl.BlockSpec((1, width), lambda i, b, l: (0, 0)),
                pl.BlockSpec((width, LANES), lambda i, b, l: (0, i)),
                pl.BlockSpec((width, LANES), lambda i, b, l: (0, i)),
                pl.BlockSpec((width, LANES), lambda i, b, l: (0, i + HEADS // 2)),
                pl.BlockSpec((2, ROWS), lambda i, b, l: (0, 0)),
                pl.BlockSpec((2, ROWS), lambda i, b, l: (0, 0)),
            ],
            out_specs=[
                pl.BlockSpec((ROWS, 2 * HEADS * HALF), lambda i, b, l: (0, 0)),
                pl.BlockSpec((2, QUARTERS, SEND_ROWS, LANES), lambda i, b, l: (i, 0, 0, 0)),
            ],
            scratch_shapes=[pltpu.VMEM((ROWS, width), bf16), pltpu.VMEM((REQS, LANES), bf16)],
        ),
        out_shape=[
            jax.ShapeDtypeStruct((ROWS, 2 * HEADS * HALF), bf16),
            jax.ShapeDtypeStruct((HEADS, QUARTERS, SEND_ROWS, LANES), bf16),
        ],
        name="project",
    )(block, lengths, stream, gain, w_query, w_keyval, w_keyval, routes_t, gates_t)


def prefix_pack_kernel(owner_ref, in_ref, ends_ref, out_ref):
    rows = in_ref.shape[1]
    for pair in range(HEADS // 2):
        key = in_ref[0, :, pair * LANES : (pair + 1) * LANES].astype(f32)
        base = HEADS * HALF + pair * LANES
        value = in_ref[0, :, base : base + LANES].astype(f32)
        even, odd = head_split(key, value)
        for quarter in range(QUARTERS):
            out_ref[2 * pair, quarter, 0:rows, :] = even.astype(bf16)
            out_ref[2 * pair + 1, quarter, 0:rows, :] = odd.astype(bf16)
    ends = jnp.sum(ends_ref[...].astype(f32), axis=0).astype(bf16)
    for head in range(HEADS):
        for quarter in range(QUARTERS):
            out_ref[head, quarter, rows : rows + REQS, :] = ends


def prefix_pack(arrived, owners, got):
    _, rows, width = arrived.shape
    return pl.pallas_call(
        prefix_pack_kernel,
        grid_spec=pltpu.PrefetchScalarGridSpec(
            num_scalar_prefetch=1,
            grid=(1,),
            in_specs=[
                pl.BlockSpec((1, rows, width), lambda i, owner: (owner[0], 0, 0)),
                pl.BlockSpec((got.shape[0], REQS, LANES), lambda i, owner: (0, 9, 0)),
            ],
            out_specs=pl.BlockSpec(
                (HEADS, QUARTERS, rows + REQS, LANES), lambda i, owner: (0, 0, 0, 0)
            ),
        ),
        out_shape=jax.ShapeDtypeStruct((HEADS, QUARTERS, rows + REQS, LANES), bf16),
        name="prefix_pack",
    )(owners, arrived, got)


def query_tile(got_ref, tile):
    blocks = QUERY_TILE // 32
    packed = got_ref[pl.ds(tile * blocks, blocks), ROWS : ROWS + 16, :]
    packed = packed.reshape(QUERY_TILE // 2, LANES).astype(f32)
    low = lane_of(packed.shape) < HALF
    first = jnp.where(low, packed, 0.0)
    second = jnp.where(low, pltpu.roll(packed, HALF, 1), 0.0)
    return jnp.concatenate([first, second], axis=0).astype(bf16)


def offset_of(row):
    half_rows = QUERY_TILE // 2
    second = (row >= half_rows).astype(jnp.int32)
    within = row - second * half_rows
    return (within // 16) * ROWS + second * 16 + within % 16


def start_of(position, lengths_ref, zero):
    end = jnp.int32(0)
    start = zero
    for request in range(REQS):
        end = end + lengths_ref[request]
        start = jnp.where(position >= end, end, start)
    return start


def suffix_kernel(quarter_ref, lengths_ref, got_ref, out_ref):
    tile = pl.program_id(0)
    blocks = QUERY_TILE // 32
    key_blocks = KEY_TILE // ROWS
    query = query_tile(got_ref, tile)
    first_position = tile * blocks * ROWS + quarter_ref[0] * 32
    position = first_position + offset_of(lax.broadcasted_iota(jnp.int32, (QUERY_TILE, 1), 0))
    start = start_of(position, lengths_ref, jnp.zeros_like(position))
    lowest = start_of(first_position, lengths_ref, jnp.int32(0))
    span = blocks * ROWS
    last_tile = (tile * span + span - 1) // KEY_TILE

    def step(j, carry):
        acc, top, total = carry
        keys = got_ref[pl.ds(j * key_blocks, key_blocks), 0:ROWS, :].reshape(KEY_TILE, LANES)
        scores = lax.dot_general(
            query, keys, (((1,), (1,)), ((), ())), preferred_element_type=f32
        )
        key_position = j * KEY_TILE + lane_of(scores.shape)
        allowed = (key_position >= start) & (key_position <= position)
        scores = jnp.where(allowed, scores, neg_big)
        new_top = jnp.maximum(top, jnp.max(scores, axis=1, keepdims=True))
        shrink = jnp.exp(top - new_top)
        probs = jnp.exp(scores - new_top)
        total = total * shrink + jnp.sum(probs, axis=1, keepdims=True)
        acc = acc * shrink + jnp.dot(probs.astype(bf16), keys, preferred_element_type=f32)
        return acc, new_top, total

    acc, top, total = lax.fori_loop(
        lowest // KEY_TILE,
        last_tile + 1,
        step,
        (
            jnp.zeros((QUERY_TILE, LANES), f32),
            jnp.full((QUERY_TILE, 1), neg_big, f32),
            jnp.zeros((QUERY_TILE, 1), f32),
        ),
    )
    lane = lane_of(acc.shape)
    out_ref[...] = jnp.where(lane == 0, top, jnp.where(lane == 1, total, acc))


def suffix_attention(quarter, lengths, got):
    blocks = got.shape[0]
    queries = blocks * 32
    return pl.pallas_call(
        suffix_kernel,
        grid_spec=pltpu.PrefetchScalarGridSpec(
            num_scalar_prefetch=2,
            grid=(queries // QUERY_TILE,),
            in_specs=[pl.BlockSpec(got.shape, lambda i, q, l: (0, 0, 0))],
            out_specs=pl.BlockSpec((QUERY_TILE, LANES), lambda i, q, l: (i, 0)),
        ),
        out_shape=jax.ShapeDtypeStruct((queries, LANES), f32),
        compiler_params=pltpu.CompilerParams(vmem_limit_bytes=24 << 20),
        name="suffix_attention",
    )(quarter, lengths, got)


def prefix_kernel(quarter_ref, lengths_ref, got_ref, keys_ref, part_ref, out_ref, last_ref):
    tile = pl.program_id(0)
    query = query_tile(got_ref, tile)
    keys = keys_ref[...].reshape(-1, LANES)
    scores = lax.dot_general(query, keys, (((1,), (1,)), ((), ())), preferred_element_type=f32)
    part = part_ref[...]
    part_top = part[:, 0:1]
    part_total = part[:, 1:2]
    top = jnp.maximum(part_top, jnp.max(scores, axis=1, keepdims=True))
    probs = jnp.exp(scores - top)
    shrink = jnp.exp(part_top - top)
    total = part_total * shrink + jnp.sum(probs, axis=1, keepdims=True)
    acc = part * shrink + jnp.dot(probs.astype(bf16), keys, preferred_element_type=f32)
    context = acc / total
    half_rows = QUERY_TILE // 2
    tile_blocks = QUERY_TILE // 32
    low = lane_of((half_rows, LANES)) < HALF
    packed = jnp.where(low, pltpu.roll(context[:half_rows], HALF, 1), context[half_rows:])
    out_ref[pl.ds(tile * tile_blocks, tile_blocks), 0:16, :] = packed.astype(bf16).reshape(
        tile_blocks, 16, LANES
    )
    positions = tile * tile_blocks * ROWS + quarter_ref[0] * 32
    positions = positions + offset_of(lane_of((REQS, QUERY_TILE)))
    is_last = last_matrix(lengths_ref, positions)
    ends = jnp.where(lane_of(context.shape) < HALF, 0.0, context).astype(bf16)
    ends = jnp.dot(is_last, ends, preferred_element_type=f32)

    @pl.when(tile == 0)
    def _():
        last_ref[...] = ends

    @pl.when(tile > 0)
    def _():
        last_ref[...] = last_ref[...] + ends

    @pl.when(tile == pl.num_programs(0) - 1)
    def _():
        every = last_ref[...].astype(bf16)
        for block in range(out_ref.shape[0]):
            out_ref[block, 16:32, :] = every


def prefix_attention(quarter, lengths, got, keys, part):
    blocks = got.shape[0]
    queries = blocks * 32
    rows = keys.shape[1] - REQS
    return pl.pallas_call(
        prefix_kernel,
        grid_spec=pltpu.PrefetchScalarGridSpec(
            num_scalar_prefetch=2,
            grid=(queries // QUERY_TILE,),
            in_specs=[
                pl.BlockSpec(got.shape, lambda i, q, l: (0, 0, 0)),
                pl.BlockSpec((blocks, rows, LANES), lambda i, q, l: (0, 0, 0)),
                pl.BlockSpec((QUERY_TILE, LANES), lambda i, q, l: (i, 0)),
            ],
            out_specs=pl.BlockSpec((blocks, 32, LANES), lambda i, q, l: (0, 0, 0)),
            scratch_shapes=[pltpu.VMEM((REQS, LANES), f32)],
        ),
        out_shape=jax.ShapeDtypeStruct((blocks, 32, LANES), bf16),
        compiler_params=pltpu.CompilerParams(vmem_limit_bytes=24 << 20),
        name="prefix_attention",
    )(quarter, lengths, got, keys, part)


def gelu(v):
    return 0.5 * v * (1.0 + jnp.tanh(0.7978845608028654 * (v + 0.044715 * v * v * v)))


def dot_nt(a, b):
    return lax.dot_general(a, b, (((1,), (1,)), ((), ())), preferred_element_type=f32)


def mix_kernel(
    block_ref, ctx_ref, tok_ref, tok_last_ref, gate_last_ref, wout_ref, gain_ref, routes_ref, g_ref, u_ref, d_ref,
    mixed_ref, mixed_last_ref, send_ref, g_v, u_v, d_v, send_v, sems, out_sems,
):
    copies = [
        pltpu.make_async_copy(source, place, sems.at[kind])
        for kind, (source, place) in enumerate(((g_ref, g_v), (u_ref, u_v), (d_ref, d_v)))
    ]
    for copy in copies:
        copy.start()
    tiles = []
    for pair in range(HEADS // 2):
        even = ctx_ref[2 * pair].astype(f32)
        odd = ctx_ref[2 * pair + 1].astype(f32)
        first, second = head_split(even[:, 0:16], odd[:, 0:16])
        both = jnp.stack([first, second], axis=1).reshape(ROWS, LANES)
        even_last = jnp.sum(even[:, 16:32], axis=0)
        odd_last = jnp.sum(odd[:, 16:32], axis=0)
        low = lane_of(even_last.shape) < HALF
        ends = jnp.where(low, pltpu.roll(even_last, HALF, 1), odd_last)
        tiles.append(jnp.concatenate([both, ends], axis=0).astype(bf16))
    context = jnp.concatenate(tiles, axis=1)
    lift = jnp.dot(context, wout_ref[...], preferred_element_type=f32)
    mixed = tok_ref[...].astype(f32) + lift[:ROWS]
    mixed_ref[...] = mixed
    routed = rms_scale(mixed, gain_ref[...]).astype(bf16)
    tok_last = jnp.concatenate([tok_last_ref[QUARTERS * j] for j in range(8)], axis=1)
    mixed_last = tok_last.astype(f32) + lift[ROWS:]
    mixed_last_ref[...] = mixed_last
    routed_last = rms_scale(mixed_last, gain_ref[...]).astype(bf16)
    expert_id = block_ref[0] // QUARTERS
    weights = jnp.sum(gate_last_ref[...].astype(f32), axis=0)
    lane = lane_of(weights.shape)
    mine = (lane % EXPERTS == expert_id) & (lane < 3 * EXPERTS)
    weight = jnp.sum(jnp.where(mine, weights, 0.0), axis=1, keepdims=True)
    copies[0].wait()
    copies[1].wait()
    act = (gelu(dot_nt(routed_last, g_v[...])) * dot_nt(routed_last, u_v[...])).astype(bf16)
    copies[2].wait()
    partial_last = weight * jnp.dot(act, d_v[...], preferred_element_type=f32)
    high = partial_last.astype(bf16)
    low_part = (partial_last - high.astype(f32)).astype(bf16)
    source = jnp.concatenate([routed, high, low_part], axis=0)
    columns = ROWS + 2 * REQS
    expert = lax.broadcasted_iota(jnp.int32, (EXPERTS, ROWS), 0)
    named = (routes_ref[0:1, :] == expert) | (routes_ref[1:2, :] == expert)
    earlier = (
        lax.broadcasted_iota(jnp.int32, (ROWS, ROWS), 0)
        < lax.broadcasted_iota(jnp.int32, (ROWS, ROWS), 1)
    ).astype(bf16)
    slots = jnp.dot(named.astype(f32).astype(bf16), earlier, preferred_element_type=f32)
    slots = jnp.where(named, slots, -1.0).astype(jnp.int32)
    place = slots + jnp.where(slots >= PART_SLOTS, PART_ROWS - PART_SLOTS, 0)
    place_id = lax.broadcasted_iota(jnp.int32, (SLOT_ROWS, ROWS), 0)
    extra_row = lax.broadcasted_iota(jnp.int32, (SLOT_ROWS, 2 * REQS), 0) % PART_ROWS
    extra_column = lane_of((SLOT_ROWS, 2 * REQS))
    sends = []
    for e in range(EXPERTS):
        pick = (place[e : e + 1, :] == place_id).astype(f32)
        for chip in range(2):
            row_last = 2 * e + chip
            extra = ((extra_row == PART_SLOTS) & (extra_column == row_last)) | (
                (extra_row == PART_SLOTS + 1) & (extra_column == REQS + row_last)
            )
            both = jnp.concatenate([pick, extra.astype(f32)], axis=1).astype(bf16)
            send_v[e, chip] = jnp.dot(both, source, preferred_element_type=f32).astype(bf16)
        send = pltpu.make_async_copy(send_v.at[e], send_ref.at[e], out_sems.at[e])
        send.start()
        sends.append(send)
    for send in sends:
        send.wait()


def mix(block, ctx, stream, prefix_got, got, w_out, gain, routes_t, own):
    width = stream.shape[1]
    blocks = got.shape[0]
    units = own[0].shape[0]
    hbm = pl.BlockSpec(memory_space=pl.ANY)

    def whole(shape):
        return pl.BlockSpec(shape, lambda i, b: (0,) * len(shape))

    return pl.pallas_call(
        mix_kernel,
        grid_spec=pltpu.PrefetchScalarGridSpec(
            num_scalar_prefetch=1,
            grid=(1,),
            in_specs=[
                whole(ctx.shape),
                whole(stream.shape),
                pl.BlockSpec((blocks, REQS, LANES), lambda i, b: (0, 4, 0)),
                pl.BlockSpec((blocks, REQS, LANES), lambda i, b: (0, 10, 0)),
                whole(w_out.shape),
                whole(gain.shape),
                whole(routes_t.shape),
                hbm,
                hbm,
                hbm,
            ],
            out_specs=[
                whole((ROWS, width)),
                whole((REQS, width)),
                pl.BlockSpec(memory_space=pltpu.HBM),
            ],
            scratch_shapes=[
                pltpu.VMEM((units, width), bf16),
                pltpu.VMEM((units, width), bf16),
                pltpu.VMEM((units, width), bf16),
                pltpu.VMEM((EXPERTS, 2, SLOT_ROWS, width), bf16),
                pltpu.SemaphoreType.DMA((3,)),
                pltpu.SemaphoreType.DMA((EXPERTS,)),
            ],
        ),
        out_shape=[
            jax.ShapeDtypeStruct((ROWS, width), f32),
            jax.ShapeDtypeStruct((REQS, width), f32),
            jax.ShapeDtypeStruct((EXPERTS, 2, SLOT_ROWS, width), bf16),
        ],
        compiler_params=pltpu.CompilerParams(vmem_limit_bytes=28 << 20),
        name="mix",
    )(block, ctx, stream, prefix_got, got, w_out, gain, routes_t, *own)


FFN_TILE = 256


def expert_kernel(
    x_ref, g0, u0, d0, g1, u1, d1, out_ref, gate_v, up_v, down_v, acc_v, out_v, sems, out_sems
):
    sources = ((g0, u0, d0), (g1, u1, d1))
    places = (gate_v, up_v, down_v)
    copies = [
        [
            pltpu.make_async_copy(sources[part][kind], places[kind].at[part], sems.at[part, kind])
            for kind in range(3)
        ]
        for part in range(2)
    ]
    for part in range(2):
        for kind in range(3):
            copies[part][kind].start()
    count = x_ref.shape[0]
    within = lane_of((16, count)) % PART_ROWS
    extra = ((within == PART_SLOTS) | (within == PART_SLOTS + 1)).astype(f32).astype(bf16)
    total = jnp.dot(extra, x_ref[...], preferred_element_type=f32)[0:1]
    high = total.astype(bf16).astype(f32)
    low = (total - high).astype(bf16).astype(f32)
    sends = []
    for part in range(2):
        for tile in range(count // FFN_TILE):
            rows = slice(tile * FFN_TILE, (tile + 1) * FFN_TILE)
            if tile == 0:
                copies[part][0].wait()
                copies[part][1].wait()
            x = x_ref[rows, :]
            hidden = (gelu(dot_nt(x, gate_v[part])) * dot_nt(x, up_v[part])).astype(bf16)
            if tile == 0:
                copies[part][2].wait()
            down = jnp.dot(hidden, down_v[part], preferred_element_type=f32)
            if part == 0:
                acc_v[rows, :] = down
            else:
                row = tile * FFN_TILE + lax.broadcasted_iota(jnp.int32, (FFN_TILE, 1), 0)
                row = row % PART_ROWS
                result = acc_v[rows, :] + down
                result = jnp.where(row == PART_SLOTS, high, result)
                result = jnp.where(row == PART_SLOTS + 1, low, result)
                out_v[rows, :] = result.astype(bf16)
                send = pltpu.make_async_copy(
                    out_v.at[pl.ds(tile * FFN_TILE, FFN_TILE), :],
                    out_ref.at[pl.ds(tile * FFN_TILE, FFN_TILE), :],
                    out_sems.at[tile],
                )
                send.start()
                sends.append(send)
    for send in sends:
        send.wait()


def expert(rows, own, other):
    count, width = rows.shape
    units = own[0].shape[0]
    hbm = pl.BlockSpec(memory_space=pl.ANY)
    vmem = pl.BlockSpec(memory_space=pltpu.VMEM)
    return pl.pallas_call(
        expert_kernel,
        in_specs=[vmem] + [hbm] * 6,
        out_specs=pl.BlockSpec(memory_space=pltpu.HBM),
        out_shape=jax.ShapeDtypeStruct((count, width), bf16),
        scratch_shapes=[
            pltpu.VMEM((2, units, width), bf16),
            pltpu.VMEM((2, units, width), bf16),
            pltpu.VMEM((2, units, width), bf16),
            pltpu.VMEM((count, width), f32),
            pltpu.VMEM((count, width), bf16),
            pltpu.SemaphoreType.DMA((2, 3)),
            pltpu.SemaphoreType.DMA((count // FFN_TILE,)),
        ],
        compiler_params=pltpu.CompilerParams(vmem_limit_bytes=48 << 20),
        name="expert",
    )(rows, *own, *other)


def combine_kernel(
    block_ref, lengths_ref, mixed_ref, mixed_last_ref, got_ref, routes_ref, gates_ref, gain_ref,
    hidden_ref, last_ref, norm_ref,
):
    got = got_ref[...]
    count = got.shape[0]
    request_row = lax.broadcasted_iota(jnp.int32, (REQS, count), 0)
    wanted = request_row * (2 * PART_ROWS) + PART_SLOTS
    source = lane_of((REQS, count))
    pick_last = ((source == wanted) | (source == wanted + 1)).astype(f32).astype(bf16)
    moe_last = jnp.dot(pick_last, got, preferred_element_type=f32)
    hidden_last = (mixed_last_ref[...] + moe_last).astype(bf16).astype(f32)
    last_ref[...] = rms_scale(hidden_last, gain_ref[...]).astype(bf16)
    routes = routes_ref[...]
    first = routes[:, 0:1]
    second = routes[:, 1:2]
    lane = lane_of((ROWS, LANES))
    named = ((first == lane) | (second == lane)).astype(f32).astype(bf16)
    earlier = (
        lax.broadcasted_iota(jnp.int32, (ROWS, ROWS), 1)
        < lax.broadcasted_iota(jnp.int32, (ROWS, ROWS), 0)
    ).astype(bf16)
    slots = jnp.dot(earlier, named, preferred_element_type=f32)
    column = lane_of((ROWS, count))
    gates = gates_ref[...]
    moe = None
    for which, chosen in enumerate((first, second)):
        slot = jnp.sum(jnp.where(chosen == lane, slots, 0.0), axis=1, keepdims=True)
        slot = slot.astype(jnp.int32)
        place = slot + jnp.where(slot >= PART_SLOTS, PART_ROWS - PART_SLOTS, 0)
        target = chosen * (2 * SLOT_ROWS) + place
        pick = ((column == target) | (column == target + SLOT_ROWS)).astype(f32).astype(bf16)
        picked = jnp.dot(pick, got, preferred_element_type=f32)
        term = gates[:, which : which + 1] * picked
        moe = term if moe is None else moe + term
    hidden = (mixed_ref[...] + moe).astype(bf16)
    hidden_ref[...] = hidden
    wide = hidden.astype(f32)
    squares = jnp.sum(wide * wide, axis=1, keepdims=True)
    position = block_ref[0] * ROWS + lax.broadcasted_iota(jnp.int32, (ROWS, LANES), 0)
    starts = jnp.zeros((1, LANES), jnp.int32)
    ends = jnp.zeros((1, LANES), jnp.int32)
    lane_row = lane_of((1, LANES))
    end = jnp.int32(0)
    for r in range(REQS):
        starts = jnp.where(lane_row == r, end, starts)
        end = end + lengths_ref[r]
        ends = jnp.where(lane_row == r, end, ends)
    member = (position >= starts) & (position < ends)
    norm_ref[...] = jnp.sum(jnp.where(member, squares, 0.0), axis=0, keepdims=True)


def combine(block, lengths, mixed, mixed_last, got, routes, gates, gain):
    width = mixed.shape[1]
    vmem = pl.BlockSpec(memory_space=pltpu.VMEM)
    smem = pl.BlockSpec(memory_space=pltpu.SMEM)
    return pl.pallas_call(
        combine_kernel,
        in_specs=[smem, smem] + [vmem] * 6,
        out_specs=[vmem] * 3,
        out_shape=[
            jax.ShapeDtypeStruct((ROWS, width), bf16),
            jax.ShapeDtypeStruct((REQS, width), bf16),
            jax.ShapeDtypeStruct((1, LANES), f32),
        ],
        compiler_params=pltpu.CompilerParams(vmem_limit_bytes=24 << 20),
        name="combine",
    )(block, lengths, mixed, mixed_last, got, routes, gates, gain)


def exchange(rows):
    return lax.all_to_all(rows, "blk", split_axis=0, concat_axis=0, tiled=True)


def local(
    tokens,
    lengths,
    owners,
    prefix_cache,
    routes,
    gates,
    attn_gain,
    w_query,
    w_keyval,
    w_out,
    moe_gain,
    w_gate,
    w_up,
    w_down,
    final_gain,
    unembed,
):
    blocks = lax.axis_size("blk")
    block_index = lax.axis_index("blk")
    width = tokens.shape[2]
    stream = tokens[0]
    block = block_index.astype(jnp.int32).reshape(1)
    quarter = block % QUARTERS
    swap = [(i, i ^ 1) for i in range(blocks)]
    with jax.named_scope("prefix_gather"):
        arrived = lax.all_gather(prefix_cache, "grp", axis=0, tiled=True)
    with jax.named_scope("weight_swap"):
        own = (w_gate[0].T, w_up[0].T, w_down[0])
        other = tuple(lax.ppermute(one, "blk", swap) for one in own)
    routes_t = routes[0].T
    suffix_kv, send = project(
        block, lengths[0], stream, attn_gain.reshape(1, -1), w_query, w_keyval, routes_t, gates[0].T
    )
    with jax.named_scope("qkv_exchange"):
        got = exchange(send.reshape(blocks, SEND_ROWS, LANES))
    part = suffix_attention(quarter, lengths[0], got)
    packed = prefix_pack(arrived, owners, got)
    with jax.named_scope("prefix_exchange"):
        prefix_got = exchange(packed.reshape(blocks, packed.shape[2], LANES))
    context = prefix_attention(quarter, lengths[0], got, prefix_got, part)
    with jax.named_scope("context_exchange"):
        ctx = exchange(context).reshape(HEADS, QUARTERS, 32, LANES)
    mixed, mixed_last, outgoing = mix(
        block, ctx, stream, prefix_got, got, w_out, moe_gain.reshape(1, -1), routes_t, own
    )
    with jax.named_scope("dispatch_exchange"):
        rows = exchange(outgoing.reshape(blocks, PART_ROWS, width))
    results = expert(rows.reshape(-1, width), own, other)
    with jax.named_scope("return_exchange"):
        returned = exchange(results.reshape(blocks, PART_ROWS, width)).reshape(-1, width)
    hidden, last_rows, norm_terms = combine(
        block, lengths[0], mixed, mixed_last, returned, routes[0], gates[0], final_gain.reshape(1, -1)
    )
    logits = jnp.dot(last_rows, unembed, preferred_element_type=f32)
    best = jnp.max(logits, axis=1)
    with jax.named_scope("final_exchange"):
        final = jnp.concatenate([norm_terms[:, :REQS], best[None, :]], axis=1)
        final = jnp.pad(final, ((0, 0), (0, LANES - 2 * REQS)))
        final = exchange(jnp.broadcast_to(final[None], (blocks, 1, LANES)))[:, 0, :]
    norm_sums = jnp.sum(final[:, :REQS], axis=0)
    greatest = jnp.max(final[:, REQS : 2 * REQS], axis=0)
    request_norm = jnp.sqrt(norm_sums / (lengths[0].astype(f32) * width))
    return (hidden[None], suffix_kv[None], request_norm[None], greatest[None])


def solution(mesh):
    placed = (
        P("grp", "blk", None),
        P("grp", None),
        P("grp"),
        P("grp", "blk", None),
        P("grp", "blk", None),
        P("grp", "blk", None),
        P(),
        P(),
        P(),
        P(),
        P(),
        P("blk", None, None),
        P("blk", None, None),
        P("blk", None, None),
        P(),
        P(None, "blk"),
    )
    return jax.shard_map(
        local,
        mesh=mesh,
        in_specs=placed,
        out_specs=(P("grp", "blk", None), P("grp", "blk", None), P("grp", None), P("grp", None)),
        check_vma=False,
    )
```

time: 212 us -> 202 us (0.953)
  waiting for transfers between devices: 71.4 us -> 46.8 us
  blocking collectives: 31.7 us -> 50.8 us
  starting transfers between devices: 35.5 us -> 25.9 us
  Pallas kernels: 36 us -> 44.1 us
    all_gather x1, waiting for transfers between devices: 25.9 us -> 1.77 us  [local(): arrived = lax.all_gather(prefix_cache, 'grp', axis=0, tiled=True)]
    all_to_all x2 -> x3, blocking collectives: 31.7 us -> 50.8 us  [exchange(): return lax.all_to_all(rows, 'blk', split_axis=0, concat_axis=0, tiled=True)]
    all_to_all x5 -> x3, starting transfers between devices: 34.5 us -> 24.9 us  [exchange(): return lax.all_to_all(rows, 'blk', split_axis=0, concat_axis=0, tiled=True)]
    pallas_call x5, Pallas kernels: 26.6 us -> 34.5 us  [the longest x1 11.8 us: expert(): pl.pallas_call(expert_kernel, in_specs=[vmem] + [hbm] * 6, out_specs=pl.B...]
    all_to_all x5 -> x3, waiting for transfers between devices: 44.8 us -> 38.7 us  [exchange(): return lax.all_to_all(rows, 'blk', split_axis=0, concat_axis=0, tiled=True)]
    ppermute x3, waiting for transfers between devices: 0.01 us -> 5.69 us  [local(): other = tuple((lax.ppermute(one, 'blk', swap) for one in own))]
    ppermute x2 -> x0, local copies, waits for them, and re-layouts: 5.21 us -> none  [local(): other = tuple((lax.ppermute(one, 'blk', swap) for one in own))]
    unnamed x40 -> x60, local copies, waits for them, and re-layouts: 12.3 us -> 15.2 us
  transfers between devices with their start and end apart: 9 -> 7, of which waited for: 5 -> 7; matrix products, arithmetic and copies ran while one was open for 5% -> 1% of each run, Pallas kernels for 7% -> 7%
where the time goes in v2:
time: 202 us; the launch traced here: 201 us
  blocking collectives  50.8 us (25%)
  waiting for transfers between devices  46.8 us (23%)
  Pallas kernels  44.1 us (22%)
  starting transfers between devices  25.9 us (13%)
  local copies, waits for them, and re-layouts  16.5 us (8%)
  between operations  14.9 us (7%)
    all_to_all x3, blocking collectives, exchange(): return lax.all_to_all(rows, 'blk', split_axis=0, concat_axis=0, tiled=True)  50.8 us
    all_to_all x3, waiting for transfers between devices, exchange(): return lax.all_to_all(rows, 'blk', split_axis=0, concat_axis=0, tiled=True)  38.7 us
    all_to_all x3, starting transfers between devices, exchange(): return lax.all_to_all(rows, 'blk', split_axis=0, concat_axis=0, tiled=True)  24.9 us
    unnamed x60, local copies, waits for them, and re-layouts  15.2 us
    pallas_call x1, Pallas kernels, expert(): pl.pallas_call(expert_kernel, in_specs=[vmem] + [hbm] * 6, out_specs=pl.B...  11.8 us
    pallas_call x1, Pallas kernels, suffix_attention(): pl.pallas_call(suffix_kernel, grid_spec=pltpu.PrefetchScalarGridSpec(num_...  7.7 us
    pallas_call x1, Pallas kernels, mix(): pl.pallas_call(mix_kernel, grid_spec=pltpu.PrefetchScalarGridSpec(num_sca...  7.33 us
    pallas_call x1, Pallas kernels, prefix_attention(): pl.pallas_call(prefix_kernel, grid_spec=pltpu.PrefetchScalarGridSpec(num_...  7.29 us
  transfers between devices with their start and end apart: 7, of which 7 were waited for; matrix products, arithmetic and copies ran while one was open for 1% of the time, Pallas kernels for 7%

profile of v2, /device:TPU:1, one launch (start us, length us, event | category | flops | bytes accessed | tf_op | source)
XLA Modules:
  0.0 201.1 jit_solution(16317918887893545329)
XLA Ops:
  7.9 0.8 copy.35
  9.3 0.8 copy.36
  10.8 5.7 %project.1 = (bf16[128,1024]{1,0:T(8,128)(2,1)}, bf16[8,4,176,128]{3,2,1,0:T(8,128)(2,1)}) custom-call(s32[1]{0:T(128)} %bitcast.block_ref, s32[16]{0:T(128)} %bitcast.58, bf16[128,1024]{1,0:T(8,128)(2,1)} %bitcast.51, f32[1,1024]{1,0:T(1,128)} %bitcast.69, bf16[1024,512]{1,0:T(8,128)(2,1)} %wq_ref.1, bf16[1024,1024]{1,0:T(8,128)(2,1)} %wv_ref.1, ...), custom_call_target="tpu_custom_call" | custom-call | tf_op jit(solution)/shard_map/project/pallas_call | solution.py:122
  16.5 8.6 %all-to-all-start = ((bf16[32,176,128]{2,1,0:T(8,128)(2,1)}), bf16[32,176,128]{2,1,0:T(8,128)(2,1)S(1)}, u32[]{:S(2)}, u32[]{:S(2)}) async-start(bf16[32,176,128]{2,1,0:T(8,128)(2,1)} %bitcast.67), calls=%async_computation | async-start | bytes 2883584 | tf_op jit(solution)/shard_map/qkv_exchange/all_to_all | solution.py:618
  25.8 20.6 %all-to-all-done.ends_ref.got_ref.gate_last_ref = bf16[32,176,128]{2,1,0:T(8,128)(2,1)S(1)} async-done(((bf16[32,176,128]{2,1,0:T(8,128)(2,1)}), bf16[32,176,128]{2,1,0:T(8,128)(2,1)S(1)}, u32[]{:S(2)}, u32[]{:S(2)}) %all-to-all-start) | async-done | bytes 1441824 | tf_op jit(solution)/shard_map/qkv_exchange/all_to_all | solution.py:618
  46.4 1.8 all-gather.2.cloned.1.call-done.in_ref
  48.1 1.9 prefix_pack.1
  50.1 11.6 %all-to-all-start.1 = ((bf16[32,80,128]{2,1,0:T(8,128)(2,1)}), bf16[32,80,128]{2,1,0:T(8,128)(2,1)}, u32[]{:S(2)}, u32[]{:S(2)}) async-start(bf16[32,80,128]{2,1,0:T(8,128)(2,1)} %bitcast.66), calls=%async_computation.1 | async-start | bytes 1310720 | tf_op jit(solution)/shard_map/prefix_exchange/all_to_all | solution.py:618
  61.7 1.4 copy-done.2
  63.1 7.7 %suffix_attention.1.part_ref = f32[1024,128]{1,0:T(8,128)S(1)} custom-call(s32[1]{0:T(128)S(6)} %select_n.7.quarter_ref, s32[16]{0:T(128)S(1)} %bitcast.59, bf16[32,176,128]{2,1,0:T(8,128)(2,1)S(1)} %copy-done.2), custom_call_target="tpu_custom_call" | custom-call | tf_op jit(solution)/shard_map/suffix_attention/pallas_call | solution.py:257
  70.8 0.8 copy-done.10
  71.6 3.1 %all-to-all-done.1.keys_ref.tok_last_ref = bf16[32,80,128]{2,1,0:T(8,128)(2,1)} async-done(((bf16[32,80,128]{2,1,0:T(8,128)(2,1)}), bf16[32,80,128]{2,1,0:T(8,128)(2,1)}, u32[]{:S(2)}, u32[]{:S(2)}) %all-to-all-start.1) | async-done | bytes 655392 | tf_op jit(solution)/shard_map/prefix_exchange/all_to_all | solution.py:618
  74.7 1.0 copy-done.11
  75.8 7.3 %prefix_attention.1 = bf16[32,32,128]{2,1,0:T(8,128)(2,1)S(1)} custom-call(s32[1]{0:T(128)S(6)} %select_n.7.quarter_ref, s32[16]{0:T(128)S(1)} %bitcast.60, bf16[32,176,128]{2,1,0:T(8,128)(2,1)S(1)} %copy-done.3, bf16[32,80,128]{2,1,0:T(8,128)(2,1)} %all-to-all-done.1.keys_ref.tok_last_ref, f32[1024,128]{1,0:T(8,128)S(1)} %copy-done.11), custom_call_target="tpu_custom_call" | custom-call | tf_op jit(solution)/shard_map/prefix_attention/pallas_call | solution.py:317
  83.1 13.1 %all_to_all.30 = bf16[32,32,128]{2,1,0:T(8,128)(2,1)S(1)} all-to-all(bf16[32,32,128]{2,1,0:T(8,128)(2,1)S(1)} %prefix_attention.1), channel_id=1, replica_groups=mesh['grp'=8,'blk'=32] {'blk'}, dimensions={0} | all-to-all | bytes 524288 | tf_op jit(solution)/shard_map/context_exchange/all_to_all | solution.py:618
  96.2 1.4 copy-done.8
  97.5 1.2 copy-done.15
  98.8 7.3 %mix.1 = (f32[128,1024]{1,0:T(8,128)S(1)}, f32[16,1024]{1,0:T(8,128)S(1)}, bf16[8,2,48,1024]{3,2,1,0:T(8,128)(2,1)S(1)}) custom-call(s32[1]{0:T(128)} %bitcast.block_ref, bf16[8,4,32,128]{3,2,1,0:T(8,128)(2,1)S(1)} %bitcast.53, bf16[128,1024]{1,0:T(8,128)(2,1)S(1)} %bitcast.52, bf16[32,80,128]{2,1,0:T(8,128)(2,1)} %all-to-all-done.1.keys_ref.tok_last_ref, ...), custom_call_target="tpu_custom_call" | custom-call | tf_op jit(solution)/shard_map/mix/pallas_call | solution.py:426
  106.1 1.1 copy-done.12
  107.3 0.8 copy-done.21
  108.7 4.6 %all-to-all-start.3 = ((bf16[32,24,1024]{2,1,0:T(8,128)(2,1)}), bf16[32,24,1024]{2,1,0:T(8,128)(2,1)}, u32[]{:S(2)}, u32[]{:S(2)}) async-start(bf16[32,24,1024]{2,1,0:T(8,128)(2,1)} %bitcast.50), calls=%async_computation.3 | async-start | bytes 3145728 | tf_op jit(solution)/shard_map/dispatch_exchange/all_to_all | solution.py:618
  114.4 3.3 %collective-permute-done.g1 = bf16[704,1024]{1,0:T(8,128)(2,1)S(1)} collective-permute-done((bf16[704,1024]{1,0:T(8,128)(2,1)S(1)}, bf16[704,1024]{1,0:T(8,128)(2,1)S(1)}, u32[]{:S(2)}, u32[]{:S(2)}) %collective-permute-start) | collective-permute-done | bytes 1441824 | tf_op jit(solution)/shard_map/weight_swap/ppermute | solution.py:650
  117.7 1.1 copy-done.13
  119.1 2.1 %collective-permute-done.2.d1 = bf16[704,1024]{1,0:T(8,128)(2,1)} collective-permute-done((bf16[704,1024]{1,0:T(8,128)(2,1)}, bf16[704,1024]{1,0:T(8,128)(2,1)}, u32[]{:S(2)}, u32[]{:S(2)}) %collective-permute-start.2) | collective-permute-done | bytes 1441824 | tf_op jit(solution)/shard_map/weight_swap/ppermute | solution.py:650
  121.2 15.0 %all-to-all-done.3 = bf16[32,24,1024]{2,1,0:T(8,128)(2,1)} async-done(((bf16[32,24,1024]{2,1,0:T(8,128)(2,1)}), bf16[32,24,1024]{2,1,0:T(8,128)(2,1)}, u32[]{:S(2)}, u32[]{:S(2)}) %all-to-all-start.3) | async-done | bytes 1572896 | tf_op jit(solution)/shard_map/dispatch_exchange/all_to_all | solution.py:618
  136.2 1.4 copy-done.7
  137.5 1.4 copy-done.9
  138.9 1.4 copy-done.14
  140.3 11.8 %expert.1 = bf16[768,1024]{1,0:T(8,128)(2,1)} custom-call(bf16[768,1024]{1,0:T(8,128)(2,1)} %bitcast.19.x_ref, bf16[704,1024]{1,0:T(8,128)(2,1)S(1)} %bitcast.43, bf16[704,1024]{1,0:T(8,128)(2,1)S(1)} %bitcast.46, bf16[704,1024]{1,0:T(8,128)(2,1)S(1)} %bitcast.49, bf16[704,1024]{1,0:T(8,128)(2,1)S(1)} %copy-done.14, ...), custom_call_target="tpu_custom_call" | custom-call | tf_op jit(solution)/shard_map/expert/pallas_call | solution.py:528
  152.2 27.4 %all_to_all.31 = bf16[32,24,1024]{2,1,0:T(8,128)(2,1)S(1)} all-to-all(bf16[32,24,1024]{2,1,0:T(8,128)(2,1)} %bitcast.65), channel_id=1, replica_groups=mesh['grp'=8,'blk'=32] {'blk'}, dimensions={0} | all-to-all | bytes 3145728 | tf_op jit(solution)/shard_map/return_exchange/all_to_all | solution.py:618
  179.6 2.3 %combine.1 = (bf16[128,1024]{1,0:T(8,128)(2,1)}, bf16[16,1024]{1,0:T(8,128)(2,1)S(1)}, f32[1,128]{1,0:T(1,128)S(1)}) custom-call(s32[1]{0:T(128)} %bitcast.block_ref, s32[16]{0:T(128)S(1)} %bitcast.61, f32[128,1024]{1,0:T(8,128)S(1)} %copy-done.22, f32[16,1024]{1,0:T(8,128)S(1)} %copy-done.24, bf16[768,1024]{1,0:T(8,128)(2,1)S(1)} %bitcast.40, ...), custom_call_target="tpu_custom_call" | custom-call | tf_op jit(solution)/shard_map/combine/pallas_call | solution.py:603
  182.8 10.3 %all_to_all.32 = f32[32,1,128]{2,1,0:T(1,128)S(1)} all-to-all(f32[32,1,128]{2,1,0:T(1,128)S(1)} %broadcast_in_dim.25), channel_id=1, replica_groups=mesh['grp'=8,'blk'=32] {'blk'}, dimensions={0} | all-to-all | bytes 32768 | tf_op jit(solution)/shard_map/final_exchange/all_to_all | solution.py:618
  (60 shorter events, 6.1 us)
Async XLA Ops:
  7.2 174.8 %copy-start = (bf16[1024,1004]{0,1:T(8,128)(2,1)S(1)}, bf16[1024,1004]{0,1:T(8,128)(2,1)}, u32[]{:S(2)}) copy-start(bf16[1024,1004]{0,1:T(8,128)(2,1)} %param.31) | copy-start | bytes 6168580
  7.2 41.0 %all-gather.2.cloned.1.call-start = ((), (), s32[]{:S(2)}) async-start(), calls=%async_computation.6 | async-start | bytes 1179648 | tf_op jit(solution)/shard_map/prefix_gather/all_gather | solution.py:647
  8.7 7.8 %copy-start.17 = (s32[1,128,2]{2,1,0:T(8,128)}, s32[1,128,2]{2,1,0:T(8,128)S(1)}, u32[]{:S(2)}) copy-start(s32[1,128,2]{2,1,0:T(8,128)S(1)} %copy.35) | copy-start | bytes 3076
  10.1 6.4 %copy-start.19 = (f32[1,128,2]{2,1,0:T(8,128)}, f32[1,128,2]{2,1,0:T(8,128)S(1)}, u32[]{:S(2)}) copy-start(f32[1,128,2]{2,1,0:T(8,128)S(1)} %copy.36) | copy-start | bytes 3076
  16.5 29.8 %all-to-all-start = ((bf16[32,176,128]{2,1,0:T(8,128)(2,1)}), bf16[32,176,128]{2,1,0:T(8,128)(2,1)S(1)}, u32[]{:S(2)}, u32[]{:S(2)}) async-start(bf16[32,176,128]{2,1,0:T(8,128)(2,1)} %bitcast.67), calls=%async_computation | async-start | bytes 2883584 | tf_op jit(solution)/shard_map/qkv_exchange/all_to_all | solution.py:618
  25.8 35.9 %copy-start.26 = (s32[1,16]{1,0:T(1,128)S(1)}, s32[1,16]{1,0:T(1,128)}, u32[]{:S(2)}) copy-start(s32[1,16]{1,0:T(1,128)} %param.17) | copy-start | bytes 196
  46.4 1.8 copy-start.1
  50.1 24.6 %all-to-all-start.1 = ((bf16[32,80,128]{2,1,0:T(8,128)(2,1)}), bf16[32,80,128]{2,1,0:T(8,128)(2,1)}, u32[]{:S(2)}, u32[]{:S(2)}) async-start(bf16[32,80,128]{2,1,0:T(8,128)(2,1)} %bitcast.66), calls=%async_computation.1 | async-start | bytes 1310720 | tf_op jit(solution)/shard_map/prefix_exchange/all_to_all | solution.py:618
  61.7 1.4 copy-start.2
  63.1 11.6 %copy-start.3 = (bf16[32,176,128]{2,1,0:T(8,128)(2,1)S(1)}, bf16[32,176,128]{2,1,0:T(8,128)(2,1)}, u32[]{:S(2)}) copy-start(bf16[32,176,128]{2,1,0:T(8,128)(2,1)} %copy-done.1) | copy-start | bytes 4325380
  75.8 20.4 %copy-start.4 = (bf16[1,1024,704]{1,2,0:T(8,128)(2,1)S(1)}, bf16[1,1024,704]{1,2,0:T(8,128)(2,1)}, u32[]{:S(2)}) copy-start(bf16[1,1024,704]{1,2,0:T(8,128)(2,1)} %param.27) | copy-start | bytes 4325380
  75.8 20.4 %copy-start.6 = (bf16[1,1024,704]{1,2,0:T(8,128)(2,1)S(1)}, bf16[1,1024,704]{1,2,0:T(8,128)(2,1)}, u32[]{:S(2)}) copy-start(bf16[1,1024,704]{1,2,0:T(8,128)(2,1)} %param.28) | copy-start | bytes 4325380
  75.8 20.4 %copy-start.16 = (bf16[1,128,1024]{2,1,0:T(8,128)(2,1)S(1)}, bf16[1,128,1024]{2,1,0:T(8,128)(2,1)}, u32[]{:S(2)}) copy-start(bf16[1,128,1024]{2,1,0:T(8,128)(2,1)} %param.16) | copy-start | bytes 786436
  75.8 20.4 %copy-start.25 = (s32[2,128]{1,0:T(2,128)S(1)}, s32[2,128]{1,0:T(2,128)}, u32[]{:S(2)}) copy-start(s32[2,128]{1,0:T(2,128)} %copy.37.routes_ref) | copy-start | bytes 3076
  75.8 20.4 %copy-start.27 = (f32[1024]{0:T(1024)S(1)}, f32[1024]{0:T(1024)}, u32[]{:S(2)}) copy-start(f32[1024]{0:T(1024)} %param.26) | copy-start | bytes 12292
  96.2 1.4 copy-start.8
  97.5 1.2 copy-start.15
  106.1 1.1 copy-start.12
  108.7 4.6 %copy-start.5 = (bf16[1,1024,704]{1,2,0:T(8,128)(2,1)S(1)}, bf16[1,1024,704]{1,2,0:T(8,128)(2,1)}, u32[]{:S(2)}) copy-start(bf16[1,1024,704]{1,2,0:T(8,128)(2,1)} %param.27) | copy-start | bytes 4325380
  108.7 27.4 %all-to-all-start.3 = ((bf16[32,24,1024]{2,1,0:T(8,128)(2,1)}), bf16[32,24,1024]{2,1,0:T(8,128)(2,1)}, u32[]{:S(2)}, u32[]{:S(2)}) async-start(bf16[32,24,1024]{2,1,0:T(8,128)(2,1)} %bitcast.50), calls=%async_computation.3 | async-start | bytes 3145728 | tf_op jit(solution)/shard_map/dispatch_exchange/all_to_all | solution.py:618
  113.4 4.3 %collective-permute-start = (bf16[704,1024]{1,0:T(8,128)(2,1)S(1)}, bf16[704,1024]{1,0:T(8,128)(2,1)S(1)}, u32[]{:S(2)}, u32[]{:S(2)}) collective-permute-start(bf16[704,1024]{1,0:T(8,128)(2,1)S(1)} %bitcast.42), channel_id=1, source_target_pairs={{0,1},{1,0},{2,3},{3,2},{4,5},{5,4},{6,7},{7,6},{8,9},{9,8},{10,11... | collective-permute-start | bytes 4325384 | tf_op jit(solution)/shard_map/weight_swap/ppermute | solution.py:650
  113.9 5.3 %collective-permute-start.1 = (bf16[704,1024]{1,0:T(8,128)(2,1)}, bf16[704,1024]{1,0:T(8,128)(2,1)}, u32[]{:S(2)}, u32[]{:S(2)}) collective-permute-start(bf16[704,1024]{1,0:T(8,128)(2,1)} %bitcast.44), channel_id=1, source_target_pairs={{0,1},{1,0},{2,3},{3,2},{4,5},{5,4},{6,7},{7,6},{8,9},{9,8},{10,11... | collective-permute-start | bytes 4325384 | tf_op jit(solution)/shard_map/weight_swap/ppermute | solution.py:650
  114.0 7.2 %collective-permute-start.2 = (bf16[704,1024]{1,0:T(8,128)(2,1)}, bf16[704,1024]{1,0:T(8,128)(2,1)}, u32[]{:S(2)}, u32[]{:S(2)}) collective-permute-start(bf16[704,1024]{1,0:T(8,128)(2,1)} %bitcast.47), channel_id=1, source_target_pairs={{0,1},{1,0},{2,3},{3,2},{4,5},{5,4},{6,7},{7,6},{8,9},{9,8},{10,11... | collective-permute-start | bytes 4325384 | tf_op jit(solution)/shard_map/weight_swap/ppermute | solution.py:650
  117.7 1.1 copy-start.13
  136.2 1.4 copy-start.7
  137.5 1.4 copy-start.9
  138.9 1.4 copy-start.14
  152.1 27.5 %copy-start.18 = (s32[1,128,2]{2,1,0:T(8,128)S(1)}, s32[1,128,2]{2,1,0:T(8,128)}, u32[]{:S(2)}) copy-start(s32[1,128,2]{2,1,0:T(8,128)} %copy-done.17) | copy-start | bytes 3076
  152.1 27.5 %copy-start.20 = (f32[1,128,2]{2,1,0:T(8,128)S(1)}, f32[1,128,2]{2,1,0:T(8,128)}, u32[]{:S(2)}) copy-start(f32[1,128,2]{2,1,0:T(8,128)} %copy-done.19) | copy-start | bytes 3076
  152.1 27.5 %copy-start.22 = (f32[128,1024]{1,0:T(8,128)S(1)}, f32[128,1024]{1,0:T(8,128)}, u32[]{:S(2)}) copy-start(f32[128,1024]{1,0:T(8,128)} %copy-done.21) | copy-start | bytes 1572868
  152.1 27.4 %copy-start.24 = (f32[16,1024]{1,0:T(8,128)S(1)}, f32[16,1024]{1,0:T(8,128)}, u32[]{:S(2)}) copy-start(f32[16,1024]{1,0:T(8,128)} %copy-done.23) | copy-start | bytes 196612
  152.1 27.4 %copy-start.28 = (f32[1024]{0:T(1024)S(1)}, f32[1024]{0:T(1024)}, u32[]{:S(2)}) copy-start(f32[1024]{0:T(1024)} %param.30) | copy-start | bytes 12292
  (4 other events, 3.3 us)
Sparse Core Ops, SparseCore 0:
  9.8 38.2 all-gather.1

commit v3 on v2

--- a/solution.py
+++ b/solution.py
@@ -59,6 +59,10 @@
     middle = (values - high).astype(bf16).astype(f32)
     low = (values - high - middle).astype(bf16).astype(f32)
     return high, middle, low
+
+
+def in_hbm(*arrays):
+    return tuple(pltpu.with_memory_space_constraint(one, pltpu.HBM) for one in arrays)
 
 
 def project_kernel(
@@ -180,13 +184,11 @@
         ),
         out_shape=jax.ShapeDtypeStruct((HEADS, QUARTERS, rows + REQS, LANES), bf16),
         name="prefix_pack",
-    )(owners, arrived, got)
-
-
-def query_tile(got_ref, tile):
-    blocks = QUERY_TILE // 32
-    packed = got_ref[pl.ds(tile * blocks, blocks), ROWS : ROWS + 16, :]
-    packed = packed.reshape(QUERY_TILE // 2, LANES).astype(f32)
+    )(owners, *in_hbm(arrived, got))
+
+
+def query_tile(query_ref):
+    packed = query_ref[...].reshape(QUERY_TILE // 2, LANES).astype(f32)
     low = lane_of(packed.shape) < HALF
     first = jnp.where(low, packed, 0.0)
     second = jnp.where(low, pltpu.roll(packed, HALF, 1), 0.0)
@@ -209,11 +211,11 @@
     return start
 
 
-def suffix_kernel(quarter_ref, lengths_ref, got_ref, out_ref):
+def suffix_kernel(quarter_ref, lengths_ref, query_ref, got_ref, out_ref):
     tile = pl.program_id(0)
     blocks = QUERY_TILE // 32
     key_blocks = KEY_TILE // ROWS
-    query = query_tile(got_ref, tile)
+    query = query_tile(query_ref)
     first_position = tile * blocks * ROWS + quarter_ref[0] * 32
     position = first_position + offset_of(lax.broadcasted_iota(jnp.int32, (QUERY_TILE, 1), 0))
     start = start_of(position, lengths_ref, jnp.zeros_like(position))
@@ -223,7 +225,7 @@
 
     def step(j, carry):
         acc, top, total = carry
-        keys = got_ref[pl.ds(j * key_blocks, key_blocks), 0:ROWS, :].reshape(KEY_TILE, LANES)
+        keys = got_ref[pl.ds(j * key_blocks, key_blocks), :, :].reshape(KEY_TILE, LANES)
         scores = lax.dot_general(
             query, keys, (((1,), (1,)), ((), ())), preferred_element_type=f32
         )
@@ -259,18 +261,21 @@
         grid_spec=pltpu.PrefetchScalarGridSpec(
             num_scalar_prefetch=2,
             grid=(queries // QUERY_TILE,),
-            in_specs=[pl.BlockSpec(got.shape, lambda i, q, l: (0, 0, 0))],
+            in_specs=[
+                pl.BlockSpec((QUERY_TILE // 32, 16, LANES), lambda i, q, l: (i, ROWS // 16, 0)),
+                pl.BlockSpec((blocks, ROWS, LANES), lambda i, q, l: (0, 0, 0)),
+            ],
             out_specs=pl.BlockSpec((QUERY_TILE, LANES), lambda i, q, l: (i, 0)),
         ),
-        out_shape=jax.ShapeDtypeStruct((queries, LANES), f32),
-        compiler_params=pltpu.CompilerParams(vmem_limit_bytes=24 << 20),
+        out_shape=pltpu.HBM((queries, LANES), f32),
+        compiler_params=pltpu.CompilerParams(vmem_limit_bytes=14 << 20),
         name="suffix_attention",
-    )(quarter, lengths, got)
-
-
-def prefix_kernel(quarter_ref, lengths_ref, got_ref, keys_ref, part_ref, out_ref, last_ref):
+    )(quarter, lengths, *in_hbm(got, got))
+
+
+def prefix_kernel(quarter_ref, lengths_ref, query_ref, keys_ref, part_ref, out_ref, last_ref):
     tile = pl.program_id(0)
-    query = query_tile(got_ref, tile)
+    query = query_tile(query_ref)
     keys = keys_ref[...].reshape(-1, LANES)
     scores = lax.dot_general(query, keys, (((1,), (1,)), ((), ())), preferred_element_type=f32)
     part = part_ref[...]
@@ -320,7 +325,7 @@
             num_scalar_prefetch=2,
             grid=(queries // QUERY_TILE,),
             in_specs=[
-                pl.BlockSpec(got.shape, lambda i, q, l: (0, 0, 0)),
+                pl.BlockSpec((QUERY_TILE // 32, 16, LANES), lambda i, q, l: (i, ROWS // 16, 0)),
                 pl.BlockSpec((blocks, rows, LANES), lambda i, q, l: (0, 0, 0)),
                 pl.BlockSpec((QUERY_TILE, LANES), lambda i, q, l: (i, 0)),
             ],
@@ -328,9 +333,9 @@
             scratch_shapes=[pltpu.VMEM((REQS, LANES), f32)],
         ),
         out_shape=jax.ShapeDtypeStruct((blocks, 32, LANES), bf16),
-        compiler_params=pltpu.CompilerParams(vmem_limit_bytes=24 << 20),
+        compiler_params=pltpu.CompilerParams(vmem_limit_bytes=18 << 20),
         name="prefix_attention",
-    )(quarter, lengths, got, keys, part)
+    )(quarter, lengths, *in_hbm(got, keys, part))
 
 
 def gelu(v):
@@ -455,13 +460,13 @@
             ],
         ),
         out_shape=[
-            jax.ShapeDtypeStruct((ROWS, width), f32),
-            jax.ShapeDtypeStruct((REQS, width), f32),
-            jax.ShapeDtypeStruct((EXPERTS, 2, SLOT_ROWS, width), bf16),
+            pltpu.HBM((ROWS, width), f32),
+            pltpu.HBM((REQS, width), f32),
+            pltpu.HBM((EXPERTS, 2, SLOT_ROWS, width), bf16),
         ],
-        compiler_params=pltpu.CompilerParams(vmem_limit_bytes=28 << 20),
+        compiler_params=pltpu.CompilerParams(vmem_limit_bytes=18 << 20),
         name="mix",
-    )(block, ctx, stream, prefix_got, got, w_out, gain, routes_t, *own)
+    )(block, ctx, stream, *in_hbm(prefix_got, got), w_out, gain, routes_t, *in_hbm(*own))
 
 
 FFN_TILE = 256
@@ -529,7 +534,7 @@
         expert_kernel,
         in_specs=[vmem] + [hbm] * 6,
         out_specs=pl.BlockSpec(memory_space=pltpu.HBM),
-        out_shape=jax.ShapeDtypeStruct((count, width), bf16),
+        out_shape=pltpu.HBM((count, width), bf16),
         scratch_shapes=[
             pltpu.VMEM((2, units, width), bf16),
             pltpu.VMEM((2, units, width), bf16),
@@ -539,9 +544,13 @@
             pltpu.SemaphoreType.DMA((2, 3)),
             pltpu.SemaphoreType.DMA((count // FFN_TILE,)),
         ],
-        compiler_params=pltpu.CompilerParams(vmem_limit_bytes=48 << 20),
+        compiler_params=pltpu.CompilerParams(vmem_limit_bytes=26 << 20),
         name="expert",
-    )(rows, *own, *other)
+    )(rows, *in_hbm(*own, *other))
+
+
+def column_of(row):
+    return jnp.transpose(jnp.broadcast_to(row, (ROWS, LANES)))
 
 
 def combine_kernel(
@@ -557,9 +566,8 @@
     moe_last = jnp.dot(pick_last, got, preferred_element_type=f32)
     hidden_last = (mixed_last_ref[...] + moe_last).astype(bf16).astype(f32)
     last_ref[...] = rms_scale(hidden_last, gain_ref[...]).astype(bf16)
-    routes = routes_ref[...]
-    first = routes[:, 0:1]
-    second = routes[:, 1:2]
+    first = column_of(routes_ref[0:1, :].astype(f32)).astype(jnp.int32)
+    second = column_of(routes_ref[1:2, :].astype(f32)).astype(jnp.int32)
     lane = lane_of((ROWS, LANES))
     named = ((first == lane) | (second == lane)).astype(f32).astype(bf16)
     earlier = (
@@ -568,16 +576,15 @@
     ).astype(bf16)
     slots = jnp.dot(earlier, named, preferred_element_type=f32)
     column = lane_of((ROWS, count))
-    gates = gates_ref[...]
     moe = None
     for which, chosen in enumerate((first, second)):
         slot = jnp.sum(jnp.where(chosen == lane, slots, 0.0), axis=1, keepdims=True)
         slot = slot.astype(jnp.int32)
         place = slot + jnp.where(slot >= PART_SLOTS, PART_ROWS - PART_SLOTS, 0)
-        target = chosen * (2 * SLOT_ROWS) + place
+        target = chosen[:, 0:1] * (2 * SLOT_ROWS) + place
         pick = ((column == target) | (column == target + SLOT_ROWS)).astype(f32).astype(bf16)
         picked = jnp.dot(pick, got, preferred_element_type=f32)
-        term = gates[:, which : which + 1] * picked
+        term = column_of(gates_ref[which : which + 1, :])[:, 0:1] * picked
         moe = term if moe is None else moe + term
     hidden = (mixed_ref[...] + moe).astype(bf16)
     hidden_ref[...] = hidden
@@ -609,7 +616,7 @@
             jax.ShapeDtypeStruct((REQS, width), bf16),
             jax.ShapeDtypeStruct((1, LANES), f32),
         ],
-        compiler_params=pltpu.CompilerParams(vmem_limit_bytes=24 << 20),
+        compiler_params=pltpu.CompilerParams(vmem_limit_bytes=16 << 20),
         name="combine",
     )(block, lengths, mixed, mixed_last, got, routes, gates, gain)
 
@@ -649,8 +656,9 @@
         own = (w_gate[0].T, w_up[0].T, w_down[0])
         other = tuple(lax.ppermute(one, "blk", swap) for one in own)
     routes_t = routes[0].T
+    gates_t = gates[0].T
     suffix_kv, send = project(
-        block, lengths[0], stream, attn_gain.reshape(1, -1), w_query, w_keyval, routes_t, gates[0].T
+        block, lengths[0], stream, attn_gain.reshape(1, -1), w_query, w_keyval, routes_t, gates_t
     )
     with jax.named_scope("qkv_exchange"):
         got = exchange(send.reshape(blocks, SEND_ROWS, LANES))
@@ -670,7 +678,7 @@
     with jax.named_scope("return_exchange"):
         returned = exchange(results.reshape(blocks, PART_ROWS, width)).reshape(-1, width)
     hidden, last_rows, norm_terms = combine(
-        block, lengths[0], mixed, mixed_last, returned, routes[0], gates[0], final_gain.reshape(1, -1)
+        block, lengths[0], mixed, mixed_last, returned, routes_t, gates_t, final_gain.reshape(1, -1)
     )
     logits = jnp.dot(last_rows, unembed, preferred_element_type=f32)
     best = jnp.max(logits, axis=1)

time: 202 us -> 192 us (0.950)
  local copies, waits for them, and re-layouts: 16.5 us -> 2.31 us
  waiting for transfers between devices: 46.8 us -> 49.3 us
    unnamed x60 -> x26, local copies, waits for them, and re-layouts: 15.2 us -> 2.29 us
    all_gather x1, waiting for transfers between devices: 1.77 us -> 5.12 us  [local(): arrived = lax.all_gather(prefix_cache, 'grp', axis=0, tiled=True)]
  transfers between devices with their start and end apart: 7 -> 7, of which waited for: 7 -> 6; matrix products, arithmetic and copies ran while one was open for 1% -> 0% of each run, Pallas kernels for 7% -> 8%
where the time goes in v3:
time: 192 us; the launch traced here: 190 us
  blocking collectives  50.6 us (26%)
  waiting for transfers between devices  49.3 us (26%)
  Pallas kernels  45.6 us (24%)
  starting transfers between devices  25.6 us (13%)
  between operations  14.9 us (8%)
  local copies, waits for them, and re-layouts  2.31 us (1%)
    all_to_all x3, blocking collectives, exchange(): return lax.all_to_all(rows, 'blk', split_axis=0, concat_axis=0, tiled=True)  50.6 us
    all_to_all x3, waiting for transfers between devices, exchange(): return lax.all_to_all(rows, 'blk', split_axis=0, concat_axis=0, tiled=True)  38 us
    all_to_all x3, starting transfers between devices, exchange(): return lax.all_to_all(rows, 'blk', split_axis=0, concat_axis=0, tiled=True)  24.6 us
    pallas_call x1, Pallas kernels, expert(): pl.pallas_call(expert_kernel, in_specs=[vmem] + [hbm] * 6, out_specs=pl.B...  12.3 us
    pallas_call x1, Pallas kernels, suffix_attention(): pl.pallas_call(suffix_kernel, grid_spec=pltpu.PrefetchScalarGridSpec(num_...  9.66 us
    pallas_call x1, Pallas kernels, prefix_attention(): pl.pallas_call(prefix_kernel, grid_spec=pltpu.PrefetchScalarGridSpec(num_...  7.09 us
    pallas_call x1, Pallas kernels, mix(): pl.pallas_call(mix_kernel, grid_spec=pltpu.PrefetchScalarGridSpec(num_sca...  6.57 us
    pallas_call x1, Pallas kernels, project(): pl.pallas_call(project_kernel, grid_spec=pltpu.PrefetchScalarGridSpec(num...  5.76 us
  transfers between devices with their start and end apart: 7, of which 6 were waited for; matrix products, arithmetic and copies ran while one was open for 0% of the time, Pallas kernels for 8%

profile of v3, /device:TPU:1, one launch (start us, length us, event | category | flops | bytes accessed | tf_op | source)
XLA Modules:
  0.0 190.3 jit_solution(8567837348675065606)
XLA Ops:
  7.2 0.0 copy-start
  7.2 0.0 all-gather.2.cloned.1.call-start
  7.2 0.7 all-gather.2.cloned.1.call-update
  7.9 5.8 %project.1 = (bf16[128,1024]{1,0:T(8,128)(2,1)}, bf16[8,4,176,128]{3,2,1,0:T(8,128)(2,1)}) custom-call(s32[1]{0:T(128)} %bitcast.block_ref, s32[16]{0:T(128)} %bitcast.47, bf16[128,1024]{1,0:T(8,128)(2,1)} %bitcast.41, f32[1,1024]{1,0:T(1,128)} %bitcast.70, bf16[1024,512]{1,0:T(8,128)(2,1)} %wq_ref.1, bf16[1024,1024]{1,0:T(8,128)(2,1)} %wv_ref.1, ...), custom_call_target="tpu_custom_call" | custom-call | tf_op jit(solution)/shard_map/project/pallas_call | solution.py:126
  13.7 8.6 %all-to-all-start = ((bf16[32,176,128]{2,1,0:T(8,128)(2,1)}), bf16[32,176,128]{2,1,0:T(8,128)(2,1)}, u32[]{:S(2)}, u32[]{:S(2)}) async-start(bf16[32,176,128]{2,1,0:T(8,128)(2,1)} %bitcast.68), calls=%async_computation | async-start | bytes 2883584 | tf_op jit(solution)/shard_map/qkv_exchange/all_to_all | solution.py:625
  23.0 0.0 copy-start.6
  23.0 20.6 %all-to-all-done.ends_ref.query_ref.got_ref.gate_last_ref = bf16[32,176,128]{2,1,0:T(8,128)(2,1)} async-done(((bf16[32,176,128]{2,1,0:T(8,128)(2,1)}), bf16[32,176,128]{2,1,0:T(8,128)(2,1)}, u32[]{:S(2)}, u32[]{:S(2)}) %all-to-all-start) | async-done | bytes 1441824 | tf_op jit(solution)/shard_map/qkv_exchange/all_to_all | solution.py:625
  43.6 5.1 %all-gather.2.cloned.1.call-done.in_ref = bf16[8,64,1024]{2,1,0:T(8,128)(2,1)} async-done(((bf16[1,64,1024]{2,1,0:T(8,128)(2,1)}), bf16[8,64,1024]{2,1,0:T(8,128)(2,1)}) %all-gather.2.cloned.1.call-update) | async-done | bytes 1048592 | tf_op jit(solution)/shard_map/prefix_gather/all_gather | solution.py:654
  48.7 1.9 %prefix_pack.1 = bf16[8,4,80,128]{3,2,1,0:T(8,128)(2,1)} custom-call(s32[1]{0:T(128)S(6)} %copy.24.owner_ref, bf16[8,64,1024]{2,1,0:T(8,128)(2,1)} %all-gather.2.cloned.1.call-done.in_ref, bf16[32,176,128]{2,1,0:T(8,128)(2,1)} %all-to-all-done.ends_ref.query_ref.got_ref.gate_last_ref), custom_call_target="tpu_custom_call" | custom-call | tf_op jit(solution)/shard_map/prefix_pack/pallas_call | solution.py:172
  50.7 11.2 %all-to-all-start.1 = ((bf16[32,80,128]{2,1,0:T(8,128)(2,1)}), bf16[32,80,128]{2,1,0:T(8,128)(2,1)}, u32[]{:S(2)}, u32[]{:S(2)}) async-start(bf16[32,80,128]{2,1,0:T(8,128)(2,1)} %bitcast.66), calls=%async_computation.1 | async-start | bytes 1310720 | tf_op jit(solution)/shard_map/prefix_exchange/all_to_all | solution.py:625
  61.9 9.7 %suffix_attention.1.part_ref = f32[1024,128]{1,0:T(8,128)} custom-call(s32[1]{0:T(128)S(6)} %select_n.7.quarter_ref, s32[16]{0:T(128)S(1)} %bitcast.48, bf16[32,176,128]{2,1,0:T(8,128)(2,1)} %all-to-all-done.ends_ref.query_ref.got_ref.gate_last_ref, bf16[32,176,128]{2,1,0:T(8,128)(2,1)} %all-to-all-done.ends_ref.query_ref.got_ref.gate_last_ref), custom_call_target="tpu_custom_call" | custom-call | tf_op jit(solution)/shard_map/suffix_attention/pallas_call | solution.py:259
  71.6 3.3 %all-to-all-done.1.keys_ref.tok_last_ref = bf16[32,80,128]{2,1,0:T(8,128)(2,1)} async-done(((bf16[32,80,128]{2,1,0:T(8,128)(2,1)}), bf16[32,80,128]{2,1,0:T(8,128)(2,1)}, u32[]{:S(2)}, u32[]{:S(2)}) %all-to-all-start.1) | async-done | bytes 655392 | tf_op jit(solution)/shard_map/prefix_exchange/all_to_all | solution.py:625
  74.9 7.1 %prefix_attention.1 = bf16[32,32,128]{2,1,0:T(8,128)(2,1)S(1)} custom-call(s32[1]{0:T(128)S(6)} %select_n.7.quarter_ref, s32[16]{0:T(128)S(1)} %bitcast.49, bf16[32,176,128]{2,1,0:T(8,128)(2,1)} %all-to-all-done.ends_ref.query_ref.got_ref.gate_last_ref, bf16[32,80,128]{2,1,0:T(8,128)(2,1)} %all-to-all-done.1.keys_ref.tok_last_ref, ...), custom_call_target="tpu_custom_call" | custom-call | tf_op jit(solution)/shard_map/prefix_attention/pallas_call | solution.py:322
  82.0 12.9 %all_to_all.30 = bf16[32,32,128]{2,1,0:T(8,128)(2,1)S(1)} all-to-all(bf16[32,32,128]{2,1,0:T(8,128)(2,1)S(1)} %prefix_attention.1), channel_id=1, replica_groups=mesh['grp'=8,'blk'=32] {'blk'}, dimensions={0} | all-to-all | bytes 524288 | tf_op jit(solution)/shard_map/context_exchange/all_to_all | solution.py:625
  94.9 6.6 %mix.1 = (f32[128,1024]{1,0:T(8,128)}, f32[16,1024]{1,0:T(8,128)}, bf16[8,2,48,1024]{3,2,1,0:T(8,128)(2,1)}) custom-call(s32[1]{0:T(128)} %bitcast.block_ref, bf16[8,4,32,128]{3,2,1,0:T(8,128)(2,1)S(1)} %bitcast.43, bf16[128,1024]{1,0:T(8,128)(2,1)S(1)} %bitcast.42, bf16[32,80,128]{2,1,0:T(8,128)(2,1)} %all-to-all-done.1.keys_ref.tok_last_ref, ...), custom_call_target="tpu_custom_call" | custom-call | tf_op jit(solution)/shard_map/mix/pallas_call | solution.py:431
  101.5 4.7 %all-to-all-start.3 = ((bf16[32,24,1024]{2,1,0:T(8,128)(2,1)}), bf16[32,24,1024]{2,1,0:T(8,128)(2,1)}, u32[]{:S(2)}, u32[]{:S(2)}) async-start(bf16[32,24,1024]{2,1,0:T(8,128)(2,1)} %bitcast.67), calls=%async_computation.3 | async-start | bytes 3145728 | tf_op jit(solution)/shard_map/dispatch_exchange/all_to_all | solution.py:625
  106.2 0.5 collective-permute-start
  106.7 0.1 collective-permute-start.1
  106.8 0.4 collective-permute-start.2
  107.2 3.4 %collective-permute-done.g1 = bf16[704,1024]{1,0:T(8,128)(2,1)S(1)} collective-permute-done((bf16[704,1024]{1,0:T(8,128)(2,1)S(1)}, bf16[704,1024]{1,0:T(8,128)(2,1)S(1)}, u32[]{:S(2)}, u32[]{:S(2)}) %collective-permute-start) | collective-permute-done | bytes 1441824 | tf_op jit(solution)/shard_map/weight_swap/ppermute | solution.py:657
  110.6 1.1 copy-done.11
  111.7 2.1 %collective-permute-done.1.u1 = bf16[704,1024]{1,0:T(8,128)(2,1)S(1)} collective-permute-done((bf16[704,1024]{1,0:T(8,128)(2,1)}, bf16[704,1024]{1,0:T(8,128)(2,1)S(1)}, u32[]{:S(2)}, u32[]{:S(2)}) %collective-permute-start.1) | collective-permute-done | bytes 1441824 | tf_op jit(solution)/shard_map/weight_swap/ppermute | solution.py:657
  113.8 1.1 copy-done.12
  115.0 14.0 %all-to-all-done.3 = bf16[32,24,1024]{2,1,0:T(8,128)(2,1)} async-done(((bf16[32,24,1024]{2,1,0:T(8,128)(2,1)}), bf16[32,24,1024]{2,1,0:T(8,128)(2,1)}, u32[]{:S(2)}, u32[]{:S(2)}) %all-to-all-start.3) | async-done | bytes 1572896 | tf_op jit(solution)/shard_map/dispatch_exchange/all_to_all | solution.py:625
  129.0 12.3 %expert.1 = bf16[768,1024]{1,0:T(8,128)(2,1)} custom-call(bf16[768,1024]{1,0:T(8,128)(2,1)} %bitcast.18.x_ref, bf16[704,1024]{1,0:T(8,128)(2,1)} %bitcast.58, bf16[704,1024]{1,0:T(8,128)(2,1)} %bitcast.62, bf16[704,1024]{1,0:T(8,128)(2,1)} %bitcast.65, bf16[704,1024]{1,0:T(8,128)(2,1)} %copy-done.11, bf16[704,1024]{1,0:T(8,128)(2,1)} %copy-done.12, ...), custom_call_target="tpu_custom_call" | custom-call | tf_op jit(solution)/shard_map/expert/pallas_call | solution.py:533
  141.4 27.4 %all_to_all.31 = bf16[32,24,1024]{2,1,0:T(8,128)(2,1)S(1)} all-to-all(bf16[32,24,1024]{2,1,0:T(8,128)(2,1)} %bitcast.56), channel_id=1, replica_groups=mesh['grp'=8,'blk'=32] {'blk'}, dimensions={0} | all-to-all | bytes 3145728 | tf_op jit(solution)/shard_map/return_exchange/all_to_all | solution.py:625
  168.8 2.3 %combine.1 = (bf16[128,1024]{1,0:T(8,128)(2,1)}, bf16[16,1024]{1,0:T(8,128)(2,1)S(1)}, f32[1,128]{1,0:T(1,128)S(1)}) custom-call(s32[1]{0:T(128)} %bitcast.block_ref, s32[16]{0:T(128)S(1)} %bitcast.50, f32[128,1024]{1,0:T(8,128)S(1)} %copy-done.3, f32[16,1024]{1,0:T(8,128)S(1)} %copy-done.4, bf16[768,1024]{1,0:T(8,128)(2,1)S(1)} %bitcast.40, ...), custom_call_target="tpu_custom_call" | custom-call | tf_op jit(solution)/shard_map/combine/pallas_call | solution.py:610
  171.1 0.8 convolution_reduce_fusion
  171.9 0.1 fusion.2
  172.0 10.3 %all_to_all.32 = f32[32,1,128]{2,1,0:T(1,128)S(1)} all-to-all(f32[32,1,128]{2,1,0:T(1,128)S(1)} %broadcast_in_dim.25), channel_id=1, replica_groups=mesh['grp'=8,'blk'=32] {'blk'}, dimensions={0} | all-to-all | bytes 32768 | tf_op jit(solution)/shard_map/final_exchange/all_to_all | solution.py:625
  182.3 0.6 slice_reduce_fusion
  182.9 0.5 fusion.1
  (24 shorter events, 0.1 us)
Async XLA Ops:
  7.2 164.0 %copy-start = (bf16[1024,1004]{0,1:T(8,128)(2,1)S(1)}, bf16[1024,1004]{0,1:T(8,128)(2,1)}, u32[]{:S(2)}) copy-start(bf16[1024,1004]{0,1:T(8,128)(2,1)} %param.31) | copy-start | bytes 6168580
  7.2 41.5 %all-gather.2.cloned.1.call-start = ((), (), s32[]{:S(2)}) async-start(), calls=%async_computation.6 | async-start | bytes 1179648 | tf_op jit(solution)/shard_map/prefix_gather/all_gather | solution.py:654
  13.7 29.9 %all-to-all-start = ((bf16[32,176,128]{2,1,0:T(8,128)(2,1)}), bf16[32,176,128]{2,1,0:T(8,128)(2,1)}, u32[]{:S(2)}, u32[]{:S(2)}) async-start(bf16[32,176,128]{2,1,0:T(8,128)(2,1)} %bitcast.68), calls=%async_computation | async-start | bytes 2883584 | tf_op jit(solution)/shard_map/qkv_exchange/all_to_all | solution.py:625
  23.0 38.9 %copy-start.6 = (s32[1,16]{1,0:T(1,128)S(1)}, s32[1,16]{1,0:T(1,128)}, u32[]{:S(2)}) copy-start(s32[1,16]{1,0:T(1,128)} %param.17) | copy-start | bytes 196
  50.7 24.2 %all-to-all-start.1 = ((bf16[32,80,128]{2,1,0:T(8,128)(2,1)}), bf16[32,80,128]{2,1,0:T(8,128)(2,1)}, u32[]{:S(2)}, u32[]{:S(2)}) async-start(bf16[32,80,128]{2,1,0:T(8,128)(2,1)} %bitcast.66), calls=%async_computation.1 | async-start | bytes 1310720 | tf_op jit(solution)/shard_map/prefix_exchange/all_to_all | solution.py:625
  71.6 23.3 %copy-start.1 = (bf16[512,1024]{1,0:T(8,128)(2,1)S(1)}, bf16[512,1024]{1,0:T(8,128)(2,1)}, u32[]{:S(2)}) copy-start(bf16[512,1024]{1,0:T(8,128)(2,1)} %wout_ref.1) | copy-start | bytes 3145732
  71.6 23.3 %copy-start.2 = (bf16[1,128,1024]{2,1,0:T(8,128)(2,1)S(1)}, bf16[1,128,1024]{2,1,0:T(8,128)(2,1)}, u32[]{:S(2)}) copy-start(bf16[1,128,1024]{2,1,0:T(8,128)(2,1)} %param.16) | copy-start | bytes 786436
  71.6 23.3 %copy-start.5 = (s32[1,128,2]{1,2,0:T(2,128)S(1)}, s32[1,128,2]{1,2,0:T(2,128)}, u32[]{:S(2)}) copy-start(s32[1,128,2]{1,2,0:T(2,128)} %param.20) | copy-start | bytes 3076
  71.6 23.3 %copy-start.7 = (f32[1024]{0:T(1024)S(1)}, f32[1024]{0:T(1024)}, u32[]{:S(2)}) copy-start(f32[1024]{0:T(1024)} %param.26) | copy-start | bytes 12292
  101.4 4.7 %copy-start.10 = (bf16[1,1024,704]{1,2,0:T(8,128)(2,1)S(1)}, bf16[1,1024,704]{1,2,0:T(8,128)(2,1)}, u32[]{:S(2)}) copy-start(bf16[1,1024,704]{1,2,0:T(8,128)(2,1)} %param.27) | copy-start | bytes 4325380
  101.5 27.6 %all-to-all-start.3 = ((bf16[32,24,1024]{2,1,0:T(8,128)(2,1)}), bf16[32,24,1024]{2,1,0:T(8,128)(2,1)}, u32[]{:S(2)}, u32[]{:S(2)}) async-start(bf16[32,24,1024]{2,1,0:T(8,128)(2,1)} %bitcast.67), calls=%async_computation.3 | async-start | bytes 3145728 | tf_op jit(solution)/shard_map/dispatch_exchange/all_to_all | solution.py:625
  106.2 4.4 %collective-permute-start = (bf16[704,1024]{1,0:T(8,128)(2,1)S(1)}, bf16[704,1024]{1,0:T(8,128)(2,1)S(1)}, u32[]{:S(2)}, u32[]{:S(2)}) collective-permute-start(bf16[704,1024]{1,0:T(8,128)(2,1)S(1)} %bitcast.59), channel_id=1, source_target_pairs={{0,1},{1,0},{2,3},{3,2},{4,5},{5,4},{6,7},{7,6},{8,9},{9,8},{10,11... | collective-permute-start | bytes 4325384 | tf_op jit(solution)/shard_map/weight_swap/ppermute | solution.py:657
  106.7 7.1 %collective-permute-start.1 = (bf16[704,1024]{1,0:T(8,128)(2,1)}, bf16[704,1024]{1,0:T(8,128)(2,1)S(1)}, u32[]{:S(2)}, u32[]{:S(2)}) collective-permute-start(bf16[704,1024]{1,0:T(8,128)(2,1)} %bitcast.61), channel_id=1, source_target_pairs={{0,1},{1,0},{2,3},{3,2},{4,5},{5,4},{6,7},{7,6},{8,9},{9,8},{10,11... | collective-permute-start | bytes 4325384 | tf_op jit(solution)/shard_map/weight_swap/ppermute | solution.py:657
  106.8 8.2 %collective-permute-start.2 = (bf16[704,1024]{1,0:T(8,128)(2,1)}, bf16[704,1024]{1,0:T(8,128)(2,1)}, u32[]{:S(2)}, u32[]{:S(2)}) collective-permute-start(bf16[704,1024]{1,0:T(8,128)(2,1)} %bitcast.64), channel_id=1, source_target_pairs={{0,1},{1,0},{2,3},{3,2},{4,5},{5,4},{6,7},{7,6},{8,9},{9,8},{10,11... | collective-permute-start | bytes 4325384 | tf_op jit(solution)/shard_map/weight_swap/ppermute | solution.py:657
  110.6 1.1 copy-start.11
  113.8 1.1 copy-start.12
  141.3 27.5 %copy-start.3 = (f32[128,1024]{1,0:T(8,128)S(1)}, f32[128,1024]{1,0:T(8,128)}, u32[]{:S(2)}) copy-start(f32[128,1024]{1,0:T(8,128)} %get-tuple-element.13.mixed_ref) | copy-start | bytes 1572868
  141.3 27.5 %copy-start.4 = (f32[16,1024]{1,0:T(8,128)S(1)}, f32[16,1024]{1,0:T(8,128)}, u32[]{:S(2)}) copy-start(f32[16,1024]{1,0:T(8,128)} %get-tuple-element.14.mixed_last_ref) | copy-start | bytes 196612
  141.3 27.4 %copy-start.8 = (f32[1024]{0:T(1024)S(1)}, f32[1024]{0:T(1024)}, u32[]{:S(2)}) copy-start(f32[1024]{0:T(1024)} %param.30) | copy-start | bytes 12292
  141.3 27.4 %copy-start.9 = (f32[1,128,2]{1,2,0:T(2,128)S(1)}, f32[1,128,2]{1,2,0:T(2,128)}, u32[]{:S(2)}) copy-start(f32[1,128,2]{1,2,0:T(2,128)} %param.21) | copy-start | bytes 3076
Sparse Core Ops, SparseCore 0:
  9.8 38.8 all-gather.1

commit v4 on v3

--- a/solution.py
+++ b/solution.py
@@ -151,12 +151,22 @@
     )(block, lengths, stream, gain, w_query, w_keyval, w_keyval, routes_t, gates_t)
 
 
-def prefix_pack_kernel(owner_ref, in_ref, ends_ref, out_ref):
-    rows = in_ref.shape[1]
+def prefix_pack_kernel(offset_ref, ends_ref, *refs):
+    pieces = refs[: len(refs) - 3]
+    out_ref, prefix_v, sem = refs[len(refs) - 3 :]
+    for k, piece in enumerate(pieces):
+
+        @pl.when(offset_ref[0] == k)
+        def _():
+            copy = pltpu.make_async_copy(piece, prefix_v, sem)
+            copy.start()
+            copy.wait()
+
+    rows = prefix_v.shape[0]
     for pair in range(HEADS // 2):
-        key = in_ref[0, :, pair * LANES : (pair + 1) * LANES].astype(f32)
+        key = prefix_v[:, pair * LANES : (pair + 1) * LANES].astype(f32)
         base = HEADS * HALF + pair * LANES
-        value = in_ref[0, :, base : base + LANES].astype(f32)
+        value = prefix_v[:, base : base + LANES].astype(f32)
         even, odd = head_split(key, value)
         for quarter in range(QUARTERS):
             out_ref[2 * pair, quarter, 0:rows, :] = even.astype(bf16)
@@ -167,24 +177,25 @@
             out_ref[head, quarter, rows : rows + REQS, :] = ends
 
 
-def prefix_pack(arrived, owners, got):
-    _, rows, width = arrived.shape
+def prefix_pack(pieces, offset, got):
+    rows, width = pieces[0].shape
     return pl.pallas_call(
         prefix_pack_kernel,
         grid_spec=pltpu.PrefetchScalarGridSpec(
             num_scalar_prefetch=1,
             grid=(1,),
             in_specs=[
-                pl.BlockSpec((1, rows, width), lambda i, owner: (owner[0], 0, 0)),
                 pl.BlockSpec((got.shape[0], REQS, LANES), lambda i, owner: (0, 9, 0)),
-            ],
+            ]
+            + [pl.BlockSpec(memory_space=pl.ANY)] * len(pieces),
             out_specs=pl.BlockSpec(
                 (HEADS, QUARTERS, rows + REQS, LANES), lambda i, owner: (0, 0, 0, 0)
             ),
+            scratch_shapes=[pltpu.VMEM((rows, width), bf16), pltpu.SemaphoreType.DMA(())],
         ),
         out_shape=jax.ShapeDtypeStruct((HEADS, QUARTERS, rows + REQS, LANES), bf16),
         name="prefix_pack",
-    )(owners, *in_hbm(arrived, got))
+    )(offset, *in_hbm(got, *pieces))
 
 
 def query_tile(query_ref):
@@ -625,6 +636,21 @@
     return lax.all_to_all(rows, "blk", split_axis=0, concat_axis=0, tiled=True)
 
 
+def ring_pieces(piece):
+    size = lax.axis_size("grp")
+
+    def shift(one, by):
+        return lax.ppermute(one, "grp", [(i, (i + by) % size) for i in range(size)])
+
+    pieces = {0: piece}
+    for by in (1, 2, -1, -2):
+        pieces[by % size] = shift(piece, by)
+    pieces[3] = shift(pieces[1], 2)
+    pieces[4] = shift(pieces[2], 2)
+    pieces[5] = shift(pieces[7], -2)
+    return [pieces[k] for k in range(size)]
+
+
 def local(
     tokens,
     lengths,
@@ -651,7 +677,8 @@
     quarter = block % QUARTERS
     swap = [(i, i ^ 1) for i in range(blocks)]
     with jax.named_scope("prefix_gather"):
-        arrived = lax.all_gather(prefix_cache, "grp", axis=0, tiled=True)
+        pieces = ring_pieces(prefix_cache[0])
+        offset = (lax.axis_index("grp").astype(jnp.int32) - owners) % len(pieces)
     with jax.named_scope("weight_swap"):
         own = (w_gate[0].T, w_up[0].T, w_down[0])
         other = tuple(lax.ppermute(one, "blk", swap) for one in own)
@@ -663,7 +690,7 @@
     with jax.named_scope("qkv_exchange"):
         got = exchange(send.reshape(blocks, SEND_ROWS, LANES))
     part = suffix_attention(quarter, lengths[0], got)
-    packed = prefix_pack(arrived, owners, got)
+    packed = prefix_pack(pieces, offset, got)
     with jax.named_scope("prefix_exchange"):
         prefix_got = exchange(packed.reshape(blocks, packed.shape[2], LANES))
     context = prefix_attention(quarter, lengths[0], got, prefix_got, part)

time: 192 us -> 177 us (0.922)
  between operations: 14.9 us -> 1.58 us
  waiting for transfers between devices: 49.3 us -> 37.4 us
  starting transfers between devices: 25.6 us -> 34.5 us
    all_to_all x3, waiting for transfers between devices: 38 us -> 17.3 us  [exchange(): return lax.all_to_all(rows, 'blk', split_axis=0, concat_axis=0, tiled=True)]
    ppermute x0 -> x7, waiting for transfers between devices: none -> 14.5 us  [shift(): return lax.ppermute(one, 'grp', [(i, (i + by) % size) for i in range(size)])]
    ppermute x0 -> x7, starting transfers between devices: none -> 11.7 us  [shift(): return lax.ppermute(one, 'grp', [(i, (i + by) % size) for i in range(size)])]
    all_gather x1 -> x0, waiting for transfers between devices: 5.12 us -> none  [local(): arrived = lax.all_gather(prefix_cache, 'grp', axis=0, tiled=True)]
    all_to_all x3, starting transfers between devices: 24.6 us -> 21.9 us  [exchange(): return lax.all_to_all(rows, 'blk', split_axis=0, concat_axis=0, tiled=True)]
  transfers between devices with their start and end apart: 7 -> 13, of which waited for: 6 -> 8; matrix products, arithmetic and copies ran while one was open for 0% -> 0% of each run, Pallas kernels for 8% -> 5%
where the time goes in v4:
time: 177 us; the launch traced here: 176 us
  blocking collectives  50.6 us (29%)
  Pallas kernels  46.7 us (26%)
  waiting for transfers between devices  37.4 us (21%)
  starting transfers between devices  34.5 us (19%)
  local copies, waits for them, and re-layouts  3.01 us (2%)
    all_to_all x3, blocking collectives, exchange(): return lax.all_to_all(rows, 'blk', split_axis=0, concat_axis=0, tiled=True)  50.6 us
    all_to_all x3, starting transfers between devices, exchange(): return lax.all_to_all(rows, 'blk', split_axis=0, concat_axis=0, tiled=True)  21.9 us
    all_to_all x3, waiting for transfers between devices, exchange(): return lax.all_to_all(rows, 'blk', split_axis=0, concat_axis=0, tiled=True)  17.3 us
    ppermute x7, waiting for transfers between devices, shift(): return lax.ppermute(one, 'grp', [(i, (i + by) % size) for i in range(size)])  14.5 us
    pallas_call x1, Pallas kernels, expert(): pl.pallas_call(expert_kernel, in_specs=[vmem] + [hbm] * 6, out_specs=pl.B...  12.3 us
    ppermute x7, starting transfers between devices, shift(): return lax.ppermute(one, 'grp', [(i, (i + by) % size) for i in range(size)])  11.7 us
    pallas_call x1, Pallas kernels, suffix_attention(): pl.pallas_call(suffix_kernel, grid_spec=pltpu.PrefetchScalarGridSpec(num_...  9.65 us
    pallas_call x1, Pallas kernels, prefix_attention(): pl.pallas_call(prefix_kernel, grid_spec=pltpu.PrefetchScalarGridSpec(num_...  7.08 us
  transfers between devices with their start and end apart: 13, of which 8 were waited for; matrix products, arithmetic and copies ran while one was open for 0% of the time, Pallas kernels for 5%

profile of v4, /device:TPU:1, one launch (start us, length us, event | category | flops | bytes accessed | tf_op | source)
XLA Modules:
  0.0 175.8 jit_solution(16155744839506529759)
XLA Ops:
  0.7 5.9 %project.1 = (bf16[128,1024]{1,0:T(8,128)(2,1)}, bf16[8,4,176,128]{3,2,1,0:T(8,128)(2,1)}) custom-call(s32[1]{0:T(128)} %bitcast.block_ref, s32[16]{0:T(128)} %bitcast.49, bf16[128,1024]{1,0:T(8,128)(2,1)} %bitcast.43, f32[1,1024]{1,0:T(1,128)} %bitcast.77, bf16[1024,512]{1,0:T(8,128)(2,1)} %wq_ref.1, bf16[1024,1024]{1,0:T(8,128)(2,1)} %wv_ref.1, ...), custom_call_target="tpu_custom_call" | custom-call | tf_op jit(solution)/shard_map/project/pallas_call | solution.py:126
  6.5 8.8 %all-to-all-start = ((bf16[32,176,128]{2,1,0:T(8,128)(2,1)}), bf16[32,176,128]{2,1,0:T(8,128)(2,1)}, u32[]{:S(2)}, u32[]{:S(2)}) async-start(bf16[32,176,128]{2,1,0:T(8,128)(2,1)} %bitcast.70), calls=%async_computation | async-start | bytes 2883584 | tf_op jit(solution)/shard_map/qkv_exchange/all_to_all | solution.py:636
  15.3 1.7 collective-permute-start
  17.0 3.0 %collective-permute-start.1 = (bf16[64,1024]{1,0:T(8,128)(2,1)S(1)}, bf16[64,1024]{1,0:T(8,128)(2,1)S(1)}, u32[]{:S(2)}, u32[]{:S(2)}) collective-permute-start(bf16[64,1024]{1,0:T(8,128)(2,1)S(1)} %bitcast.74), channel_id=1, source_target_pairs={{0,64},{32,96},{64,128},{96,160},{128,192},{160,224},{192,0},{224,... | collective-permute-start | bytes 393224 | tf_op jit(solution)/shard_map/prefix_gather/ppermute | solution.py:643
  20.0 1.1 collective-permute-start.4
  21.2 2.3 %collective-permute-start.6 = (bf16[64,1024]{1,0:T(8,128)(2,1)S(1)}, bf16[64,1024]{1,0:T(8,128)(2,1)S(1)}, u32[]{:S(2)}, u32[]{:S(2)}) collective-permute-start(bf16[64,1024]{1,0:T(8,128)(2,1)S(1)} %bitcast.76), channel_id=1, source_target_pairs={{0,192},{32,224},{64,0},{96,32},{128,64},{160,96},{192,128},{224,1... | collective-permute-start | bytes 393224 | tf_op jit(solution)/shard_map/prefix_gather/ppermute | solution.py:643
  23.4 1.3 collective-permute-done.refs_1_
  24.7 4.3 %collective-permute-done.1.refs_2_ = bf16[64,1024]{1,0:T(8,128)(2,1)S(1)} collective-permute-done((bf16[64,1024]{1,0:T(8,128)(2,1)S(1)}, bf16[64,1024]{1,0:T(8,128)(2,1)S(1)}, u32[]{:S(2)}, u32[]{:S(2)}) %collective-permute-start.1) | collective-permute-done | bytes 131104 | tf_op jit(solution)/shard_map/prefix_gather/ppermute | solution.py:643
  29.0 1.6 collective-permute-start.3
  30.6 2.0 %collective-permute-start.5 = (bf16[64,1024]{1,0:T(8,128)(2,1)S(1)}, bf16[64,1024]{1,0:T(8,128)(2,1)S(1)}, u32[]{:S(2)}, u32[]{:S(2)}) collective-permute-start(bf16[64,1024]{1,0:T(8,128)(2,1)S(1)} %collective-permute-done.4.refs_7_), channel_id=1, source_target_pairs={{0,192},{32,224},{64,0},{96,32},{128,64},{160,96},{192,128},{224,1... | collective-permute-start | bytes 393224 | tf_op jit(solution)/shard_map/prefix_gather/ppermute | solution.py:643
  33.3 4.1 %collective-permute-done.2.refs_3_ = bf16[64,1024]{1,0:T(8,128)(2,1)S(1)} collective-permute-done((bf16[64,1024]{1,0:T(8,128)(2,1)S(1)}, bf16[64,1024]{1,0:T(8,128)(2,1)S(1)}, u32[]{:S(2)}, u32[]{:S(2)}) %collective-permute-start.2) | collective-permute-done | bytes 131104 | tf_op jit(solution)/shard_map/prefix_gather/ppermute | solution.py:643
  37.4 4.8 %collective-permute-done.3.refs_4_ = bf16[64,1024]{1,0:T(8,128)(2,1)S(1)} collective-permute-done((bf16[64,1024]{1,0:T(8,128)(2,1)S(1)}, bf16[64,1024]{1,0:T(8,128)(2,1)S(1)}, u32[]{:S(2)}, u32[]{:S(2)}) %collective-permute-start.3) | collective-permute-done | bytes 131104 | tf_op jit(solution)/shard_map/prefix_gather/ppermute | solution.py:643
  42.3 0.6 copy-done.19
  42.9 2.8 %prefix_pack.1 = bf16[8,4,80,128]{3,2,1,0:T(8,128)(2,1)} custom-call(s32[1]{0:T(128)S(6)} %select_n.12.offset_ref, bf16[32,176,128]{2,1,0:T(8,128)(2,1)} %all-to-all-done.ends_ref.query_ref.got_ref.gate_last_ref, bf16[64,1024]{1,0:T(8,128)(2,1)} %bitcast.72, bf16[64,1024]{1,0:T(8,128)(2,1)} %copy-done.14, bf16[64,1024]{1,0:T(8,128)(2,1)} %copy-done.15, ...), custom_call_target="tpu_custom_call" | custom-call | tf_op jit(solution)/shard_map/prefix_pack/pallas_call | solution.py:182
  45.7 8.3 %all-to-all-start.1 = ((bf16[32,80,128]{2,1,0:T(8,128)(2,1)}), bf16[32,80,128]{2,1,0:T(8,128)(2,1)}, u32[]{:S(2)}, u32[]{:S(2)}) async-start(bf16[32,80,128]{2,1,0:T(8,128)(2,1)} %bitcast.68), calls=%async_computation.1 | async-start | bytes 1310720 | tf_op jit(solution)/shard_map/prefix_exchange/all_to_all | solution.py:636
  54.0 9.6 %suffix_attention.1.part_ref = f32[1024,128]{1,0:T(8,128)} custom-call(s32[1]{0:T(128)S(6)} %select_n.11.quarter_ref, s32[16]{0:T(128)S(1)} %bitcast.50, bf16[32,176,128]{2,1,0:T(8,128)(2,1)} %all-to-all-done.ends_ref.query_ref.got_ref.gate_last_ref, bf16[32,176,128]{2,1,0:T(8,128)(2,1)} %all-to-all-done.ends_ref.query_ref.got_ref.gate_last_ref), custom_call_target="tpu_custom_call" | custom-call | tf_op jit(solution)/shard_map/suffix_attention/pallas_call | solution.py:270
  63.7 3.3 %all-to-all-done.1.keys_ref.tok_last_ref = bf16[32,80,128]{2,1,0:T(8,128)(2,1)} async-done(((bf16[32,80,128]{2,1,0:T(8,128)(2,1)}), bf16[32,80,128]{2,1,0:T(8,128)(2,1)}, u32[]{:S(2)}, u32[]{:S(2)}) %all-to-all-start.1) | async-done | bytes 655392 | tf_op jit(solution)/shard_map/prefix_exchange/all_to_all | solution.py:636
  67.0 7.1 %prefix_attention.1 = bf16[32,32,128]{2,1,0:T(8,128)(2,1)S(1)} custom-call(s32[1]{0:T(128)S(6)} %select_n.11.quarter_ref, s32[16]{0:T(128)S(1)} %bitcast.51, bf16[32,176,128]{2,1,0:T(8,128)(2,1)} %all-to-all-done.ends_ref.query_ref.got_ref.gate_last_ref, bf16[32,80,128]{2,1,0:T(8,128)(2,1)} %all-to-all-done.1.keys_ref.tok_last_ref, ...), custom_call_target="tpu_custom_call" | custom-call | tf_op jit(solution)/shard_map/prefix_attention/pallas_call | solution.py:333
  74.1 12.9 %all_to_all.30 = bf16[32,32,128]{2,1,0:T(8,128)(2,1)S(1)} all-to-all(bf16[32,32,128]{2,1,0:T(8,128)(2,1)S(1)} %prefix_attention.1), channel_id=1, replica_groups=mesh['grp'=8,'blk'=32] {'blk'}, dimensions={0} | all-to-all | bytes 524288 | tf_op jit(solution)/shard_map/context_exchange/all_to_all | solution.py:636
  87.0 6.7 %mix.1 = (f32[128,1024]{1,0:T(8,128)}, f32[16,1024]{1,0:T(8,128)}, bf16[8,2,48,1024]{3,2,1,0:T(8,128)(2,1)}) custom-call(s32[1]{0:T(128)} %bitcast.block_ref, bf16[8,4,32,128]{3,2,1,0:T(8,128)(2,1)S(1)} %bitcast.45, bf16[128,1024]{1,0:T(8,128)(2,1)S(1)} %bitcast.44, bf16[32,80,128]{2,1,0:T(8,128)(2,1)} %all-to-all-done.1.keys_ref.tok_last_ref, ...), custom_call_target="tpu_custom_call" | custom-call | tf_op jit(solution)/shard_map/mix/pallas_call | solution.py:442
  93.7 4.8 %all-to-all-start.3 = ((bf16[32,24,1024]{2,1,0:T(8,128)(2,1)}), bf16[32,24,1024]{2,1,0:T(8,128)(2,1)}, u32[]{:S(2)}, u32[]{:S(2)}) async-start(bf16[32,24,1024]{2,1,0:T(8,128)(2,1)} %bitcast.69), calls=%async_computation.3 | async-start | bytes 3145728 | tf_op jit(solution)/shard_map/dispatch_exchange/all_to_all | solution.py:636
  99.5 3.3 %collective-permute-done.7.g1 = bf16[704,1024]{1,0:T(8,128)(2,1)S(1)} collective-permute-done((bf16[704,1024]{1,0:T(8,128)(2,1)S(1)}, bf16[704,1024]{1,0:T(8,128)(2,1)S(1)}, u32[]{:S(2)}, u32[]{:S(2)}) %collective-permute-start.7) | collective-permute-done | bytes 1441824 | tf_op jit(solution)/shard_map/weight_swap/ppermute | solution.py:684
  102.8 1.1 copy-done.11
  103.9 2.3 %collective-permute-done.8.u1 = bf16[704,1024]{1,0:T(8,128)(2,1)S(1)} collective-permute-done((bf16[704,1024]{1,0:T(8,128)(2,1)}, bf16[704,1024]{1,0:T(8,128)(2,1)S(1)}, u32[]{:S(2)}, u32[]{:S(2)}) %collective-permute-start.8) | collective-permute-done | bytes 1441824 | tf_op jit(solution)/shard_map/weight_swap/ppermute | solution.py:684
  106.2 1.2 copy-done.12
  107.3 14.0 %all-to-all-done.3 = bf16[32,24,1024]{2,1,0:T(8,128)(2,1)} async-done(((bf16[32,24,1024]{2,1,0:T(8,128)(2,1)}), bf16[32,24,1024]{2,1,0:T(8,128)(2,1)}, u32[]{:S(2)}, u32[]{:S(2)}) %all-to-all-start.3) | async-done | bytes 1572896 | tf_op jit(solution)/shard_map/dispatch_exchange/all_to_all | solution.py:636
  121.3 12.3 %expert.1 = bf16[768,1024]{1,0:T(8,128)(2,1)} custom-call(bf16[768,1024]{1,0:T(8,128)(2,1)} %bitcast.20.x_ref, bf16[704,1024]{1,0:T(8,128)(2,1)} %bitcast.60, bf16[704,1024]{1,0:T(8,128)(2,1)} %bitcast.64, bf16[704,1024]{1,0:T(8,128)(2,1)} %bitcast.67, bf16[704,1024]{1,0:T(8,128)(2,1)} %copy-done.11, bf16[704,1024]{1,0:T(8,128)(2,1)} %copy-done.12, ...), custom_call_target="tpu_custom_call" | custom-call | tf_op jit(solution)/shard_map/expert/pallas_call | solution.py:544
  133.7 27.4 %all_to_all.31 = bf16[32,24,1024]{2,1,0:T(8,128)(2,1)S(1)} all-to-all(bf16[32,24,1024]{2,1,0:T(8,128)(2,1)} %bitcast.58), channel_id=1, replica_groups=mesh['grp'=8,'blk'=32] {'blk'}, dimensions={0} | all-to-all | bytes 3145728 | tf_op jit(solution)/shard_map/return_exchange/all_to_all | solution.py:636
  161.1 2.3 %combine.1 = (bf16[128,1024]{1,0:T(8,128)(2,1)}, bf16[16,1024]{1,0:T(8,128)(2,1)S(1)}, f32[1,128]{1,0:T(1,128)S(1)}) custom-call(s32[1]{0:T(128)} %bitcast.block_ref, s32[16]{0:T(128)S(1)} %bitcast.52, f32[128,1024]{1,0:T(8,128)S(1)} %copy-done.3, f32[16,1024]{1,0:T(8,128)S(1)} %copy-done.4, bf16[768,1024]{1,0:T(8,128)(2,1)S(1)} %bitcast.42, ...), custom_call_target="tpu_custom_call" | custom-call | tf_op jit(solution)/shard_map/combine/pallas_call | solution.py:621
  163.5 0.8 convolution_reduce_fusion
  164.3 10.3 %all_to_all.32 = f32[32,1,128]{2,1,0:T(1,128)S(1)} all-to-all(f32[32,1,128]{2,1,0:T(1,128)S(1)} %broadcast_in_dim.25), channel_id=1, replica_groups=mesh['grp'=8,'blk'=32] {'blk'}, dimensions={0} | all-to-all | bytes 32768 | tf_op jit(solution)/shard_map/final_exchange/all_to_all | solution.py:636
  174.7 0.6 slice_reduce_fusion
  (51 shorter events, 1.8 us)
Async XLA Ops:
  0.6 162.8 %copy-start = (bf16[1024,1004]{0,1:T(8,128)(2,1)S(1)}, bf16[1024,1004]{0,1:T(8,128)(2,1)}, u32[]{:S(2)}) copy-start(bf16[1024,1004]{0,1:T(8,128)(2,1)} %param.31) | copy-start | bytes 6168580
  6.5 8.8 %copy-start.13 = (bf16[1,64,1024]{2,1,0:T(8,128)(2,1)S(1)}, bf16[1,64,1024]{2,1,0:T(8,128)(2,1)}, u32[]{:S(2)}) copy-start(bf16[1,64,1024]{2,1,0:T(8,128)(2,1)} %param.19) | copy-start | bytes 393220
  6.5 35.7 %all-to-all-start = ((bf16[32,176,128]{2,1,0:T(8,128)(2,1)}), bf16[32,176,128]{2,1,0:T(8,128)(2,1)}, u32[]{:S(2)}, u32[]{:S(2)}) async-start(bf16[32,176,128]{2,1,0:T(8,128)(2,1)} %bitcast.70), calls=%async_computation | async-start | bytes 2883584 | tf_op jit(solution)/shard_map/qkv_exchange/all_to_all | solution.py:636
  15.3 9.4 %collective-permute-start = (bf16[64,1024]{1,0:T(8,128)(2,1)S(1)}, bf16[64,1024]{1,0:T(8,128)(2,1)S(1)}, u32[]{:S(2)}, u32[]{:S(2)}) collective-permute-start(bf16[64,1024]{1,0:T(8,128)(2,1)S(1)} %bitcast.73), channel_id=1, source_target_pairs={{0,32},{32,64},{64,96},{96,128},{128,160},{160,192},{192,224},{224... | collective-permute-start | bytes 393224 | tf_op jit(solution)/shard_map/prefix_gather/ppermute | solution.py:643
  17.0 12.0 %collective-permute-start.1 = (bf16[64,1024]{1,0:T(8,128)(2,1)S(1)}, bf16[64,1024]{1,0:T(8,128)(2,1)S(1)}, u32[]{:S(2)}, u32[]{:S(2)}) collective-permute-start(bf16[64,1024]{1,0:T(8,128)(2,1)S(1)} %bitcast.74), channel_id=1, source_target_pairs={{0,64},{32,96},{64,128},{96,160},{128,192},{160,224},{192,0},{224,... | collective-permute-start | bytes 393224 | tf_op jit(solution)/shard_map/prefix_gather/ppermute | solution.py:643
  20.0 10.6 %collective-permute-start.4 = (bf16[64,1024]{1,0:T(8,128)(2,1)S(1)}, bf16[64,1024]{1,0:T(8,128)(2,1)S(1)}, u32[]{:S(2)}, u32[]{:S(2)}) collective-permute-start(bf16[64,1024]{1,0:T(8,128)(2,1)S(1)} %bitcast.75), channel_id=1, source_target_pairs={{0,224},{32,0},{64,32},{96,64},{128,96},{160,128},{192,160},{224,1... | collective-permute-start | bytes 393224 | tf_op jit(solution)/shard_map/prefix_gather/ppermute | solution.py:643
  21.2 12.1 %collective-permute-start.6 = (bf16[64,1024]{1,0:T(8,128)(2,1)S(1)}, bf16[64,1024]{1,0:T(8,128)(2,1)S(1)}, u32[]{:S(2)}, u32[]{:S(2)}) collective-permute-start(bf16[64,1024]{1,0:T(8,128)(2,1)S(1)} %bitcast.76), channel_id=1, source_target_pairs={{0,192},{32,224},{64,0},{96,32},{128,64},{160,96},{192,128},{224,1... | collective-permute-start | bytes 393224 | tf_op jit(solution)/shard_map/prefix_gather/ppermute | solution.py:643
  24.7 17.5 %copy-start.14 = (bf16[64,1024]{1,0:T(8,128)(2,1)}, bf16[64,1024]{1,0:T(8,128)(2,1)S(1)}, u32[]{:S(2)}) copy-start(bf16[64,1024]{1,0:T(8,128)(2,1)S(1)} %collective-permute-done.refs_1_) | copy-start | bytes 393220
  24.7 12.7 %collective-permute-start.2 = (bf16[64,1024]{1,0:T(8,128)(2,1)S(1)}, bf16[64,1024]{1,0:T(8,128)(2,1)S(1)}, u32[]{:S(2)}, u32[]{:S(2)}) collective-permute-start(bf16[64,1024]{1,0:T(8,128)(2,1)S(1)} %collective-permute-done.refs_1_), channel_id=1, source_target_pairs={{0,64},{32,96},{64,128},{96,160},{128,192},{160,224},{192,0},{224,... | collective-permute-start | bytes 393224 | tf_op jit(solution)/shard_map/prefix_gather/ppermute | solution.py:643
  29.0 13.3 %copy-start.15 = (bf16[64,1024]{1,0:T(8,128)(2,1)}, bf16[64,1024]{1,0:T(8,128)(2,1)S(1)}, u32[]{:S(2)}) copy-start(bf16[64,1024]{1,0:T(8,128)(2,1)S(1)} %collective-permute-done.1.refs_2_) | copy-start | bytes 393220
  29.0 13.2 %collective-permute-start.3 = (bf16[64,1024]{1,0:T(8,128)(2,1)S(1)}, bf16[64,1024]{1,0:T(8,128)(2,1)S(1)}, u32[]{:S(2)}, u32[]{:S(2)}) collective-permute-start(bf16[64,1024]{1,0:T(8,128)(2,1)S(1)} %collective-permute-done.1.refs_2_), channel_id=1, source_target_pairs={{0,64},{32,96},{64,128},{96,160},{128,192},{160,224},{192,0},{224,... | collective-permute-start | bytes 393224 | tf_op jit(solution)/shard_map/prefix_gather/ppermute | solution.py:643
  30.6 11.7 %copy-start.16 = (bf16[64,1024]{1,0:T(8,128)(2,1)}, bf16[64,1024]{1,0:T(8,128)(2,1)S(1)}, u32[]{:S(2)}) copy-start(bf16[64,1024]{1,0:T(8,128)(2,1)S(1)} %collective-permute-done.4.refs_7_) | copy-start | bytes 393220
  30.6 11.6 %collective-permute-start.5 = (bf16[64,1024]{1,0:T(8,128)(2,1)S(1)}, bf16[64,1024]{1,0:T(8,128)(2,1)S(1)}, u32[]{:S(2)}, u32[]{:S(2)}) collective-permute-start(bf16[64,1024]{1,0:T(8,128)(2,1)S(1)} %collective-permute-done.4.refs_7_), channel_id=1, source_target_pairs={{0,192},{32,224},{64,0},{96,32},{128,64},{160,96},{192,128},{224,1... | collective-permute-start | bytes 393224 | tf_op jit(solution)/shard_map/prefix_gather/ppermute | solution.py:643
  33.3 20.7 %copy-start.6 = (s32[1,16]{1,0:T(1,128)S(1)}, s32[1,16]{1,0:T(1,128)}, u32[]{:S(2)}) copy-start(s32[1,16]{1,0:T(1,128)} %param.17) | copy-start | bytes 196
  33.3 9.0 %copy-start.17 = (bf16[64,1024]{1,0:T(8,128)(2,1)}, bf16[64,1024]{1,0:T(8,128)(2,1)S(1)}, u32[]{:S(2)}) copy-start(bf16[64,1024]{1,0:T(8,128)(2,1)S(1)} %collective-permute-done.6.refs_6_) | copy-start | bytes 393220
  37.4 4.9 %copy-start.18 = (bf16[64,1024]{1,0:T(8,128)(2,1)}, bf16[64,1024]{1,0:T(8,128)(2,1)S(1)}, u32[]{:S(2)}) copy-start(bf16[64,1024]{1,0:T(8,128)(2,1)S(1)} %collective-permute-done.2.refs_3_) | copy-start | bytes 393220
  45.7 21.3 %all-to-all-start.1 = ((bf16[32,80,128]{2,1,0:T(8,128)(2,1)}), bf16[32,80,128]{2,1,0:T(8,128)(2,1)}, u32[]{:S(2)}, u32[]{:S(2)}) async-start(bf16[32,80,128]{2,1,0:T(8,128)(2,1)} %bitcast.68), calls=%async_computation.1 | async-start | bytes 1310720 | tf_op jit(solution)/shard_map/prefix_exchange/all_to_all | solution.py:636
  63.7 23.3 %copy-start.1 = (bf16[512,1024]{1,0:T(8,128)(2,1)S(1)}, bf16[512,1024]{1,0:T(8,128)(2,1)}, u32[]{:S(2)}) copy-start(bf16[512,1024]{1,0:T(8,128)(2,1)} %wout_ref.1) | copy-start | bytes 3145732
  63.7 23.3 %copy-start.2 = (bf16[1,128,1024]{2,1,0:T(8,128)(2,1)S(1)}, bf16[1,128,1024]{2,1,0:T(8,128)(2,1)}, u32[]{:S(2)}) copy-start(bf16[1,128,1024]{2,1,0:T(8,128)(2,1)} %param.16) | copy-start | bytes 786436
  63.7 23.3 %copy-start.5 = (s32[1,128,2]{1,2,0:T(2,128)S(1)}, s32[1,128,2]{1,2,0:T(2,128)}, u32[]{:S(2)}) copy-start(s32[1,128,2]{1,2,0:T(2,128)} %param.20) | copy-start | bytes 3076
  63.7 23.3 %copy-start.7 = (f32[1024]{0:T(1024)S(1)}, f32[1024]{0:T(1024)}, u32[]{:S(2)}) copy-start(f32[1024]{0:T(1024)} %param.26) | copy-start | bytes 12292
  93.7 4.8 %copy-start.10 = (bf16[1,1024,704]{1,2,0:T(8,128)(2,1)S(1)}, bf16[1,1024,704]{1,2,0:T(8,128)(2,1)}, u32[]{:S(2)}) copy-start(bf16[1,1024,704]{1,2,0:T(8,128)(2,1)} %param.27) | copy-start | bytes 4325380
  93.7 27.6 %all-to-all-start.3 = ((bf16[32,24,1024]{2,1,0:T(8,128)(2,1)}), bf16[32,24,1024]{2,1,0:T(8,128)(2,1)}, u32[]{:S(2)}, u32[]{:S(2)}) async-start(bf16[32,24,1024]{2,1,0:T(8,128)(2,1)} %bitcast.69), calls=%async_computation.3 | async-start | bytes 3145728 | tf_op jit(solution)/shard_map/dispatch_exchange/all_to_all | solution.py:636
  98.5 4.3 %collective-permute-start.7 = (bf16[704,1024]{1,0:T(8,128)(2,1)S(1)}, bf16[704,1024]{1,0:T(8,128)(2,1)S(1)}, u32[]{:S(2)}, u32[]{:S(2)}) collective-permute-start(bf16[704,1024]{1,0:T(8,128)(2,1)S(1)} %bitcast.61), channel_id=1, source_target_pairs={{0,1},{1,0},{2,3},{3,2},{4,5},{5,4},{6,7},{7,6},{8,9},{9,8},{10,11... | collective-permute-start | bytes 4325384 | tf_op jit(solution)/shard_map/weight_swap/ppermute | solution.py:684
  99.0 7.2 %collective-permute-start.8 = (bf16[704,1024]{1,0:T(8,128)(2,1)}, bf16[704,1024]{1,0:T(8,128)(2,1)S(1)}, u32[]{:S(2)}, u32[]{:S(2)}) collective-permute-start(bf16[704,1024]{1,0:T(8,128)(2,1)} %bitcast.63), channel_id=1, source_target_pairs={{0,1},{1,0},{2,3},{3,2},{4,5},{5,4},{6,7},{7,6},{8,9},{9,8},{10,11... | collective-permute-start | bytes 4325384 | tf_op jit(solution)/shard_map/weight_swap/ppermute | solution.py:684
  99.1 8.2 %collective-permute-start.9 = (bf16[704,1024]{1,0:T(8,128)(2,1)}, bf16[704,1024]{1,0:T(8,128)(2,1)}, u32[]{:S(2)}, u32[]{:S(2)}) collective-permute-start(bf16[704,1024]{1,0:T(8,128)(2,1)} %bitcast.66), channel_id=1, source_target_pairs={{0,1},{1,0},{2,3},{3,2},{4,5},{5,4},{6,7},{7,6},{8,9},{9,8},{10,11... | collective-permute-start | bytes 4325384 | tf_op jit(solution)/shard_map/weight_swap/ppermute | solution.py:684
  102.8 1.1 copy-start.11
  106.2 1.2 copy-start.12
  133.6 27.5 %copy-start.3 = (f32[128,1024]{1,0:T(8,128)S(1)}, f32[128,1024]{1,0:T(8,128)}, u32[]{:S(2)}) copy-start(f32[128,1024]{1,0:T(8,128)} %get-tuple-element.13.mixed_ref) | copy-start | bytes 1572868
  133.6 27.5 %copy-start.4 = (f32[16,1024]{1,0:T(8,128)S(1)}, f32[16,1024]{1,0:T(8,128)}, u32[]{:S(2)}) copy-start(f32[16,1024]{1,0:T(8,128)} %get-tuple-element.14.mixed_last_ref) | copy-start | bytes 196612
  133.7 27.4 %copy-start.8 = (f32[1024]{0:T(1024)S(1)}, f32[1024]{0:T(1024)}, u32[]{:S(2)}) copy-start(f32[1024]{0:T(1024)} %param.30) | copy-start | bytes 12292
  133.7 27.4 %copy-start.9 = (f32[1,128,2]{1,2,0:T(2,128)S(1)}, f32[1,128,2]{1,2,0:T(2,128)}, u32[]{:S(2)}) copy-start(f32[1,128,2]{1,2,0:T(2,128)} %param.21) | copy-start | bytes 3076
  (2 other events, 1.3 us)

commit v5 on v4

--- a/solution.py
+++ b/solution.py
@@ -19,6 +19,8 @@
 LANES = 128
 KEY_TILE = 1024
 QUERY_TILE = 256
+PREFIX_TILE = 1024
+PREFIX_SUB = 128
 
 epsilon = 1e-06
 neg_big = -1e30
@@ -286,27 +288,56 @@
 
 def prefix_kernel(quarter_ref, lengths_ref, query_ref, keys_ref, part_ref, out_ref, last_ref):
     tile = pl.program_id(0)
-    query = query_tile(query_ref)
+    tile_blocks = PREFIX_TILE // 32
+    half_rows = PREFIX_TILE // 2
+    packed = query_ref[...].reshape(half_rows, LANES).astype(f32)
+    low = lane_of(packed.shape) < HALF
+    query = jnp.concatenate(
+        [jnp.where(low, packed, 0.0), jnp.where(low, pltpu.roll(packed, HALF, 1), 0.0)], axis=0
+    ).astype(bf16)
     keys = keys_ref[...].reshape(-1, LANES)
-    scores = lax.dot_general(query, keys, (((1,), (1,)), ((), ())), preferred_element_type=f32)
-    part = part_ref[...]
-    part_top = part[:, 0:1]
-    part_total = part[:, 1:2]
-    top = jnp.maximum(part_top, jnp.max(scores, axis=1, keepdims=True))
-    probs = jnp.exp(scores - top)
-    shrink = jnp.exp(part_top - top)
-    total = part_total * shrink + jnp.sum(probs, axis=1, keepdims=True)
-    acc = part * shrink + jnp.dot(probs.astype(bf16), keys, preferred_element_type=f32)
-    context = acc / total
-    half_rows = QUERY_TILE // 2
-    tile_blocks = QUERY_TILE // 32
-    low = lane_of((half_rows, LANES)) < HALF
+    subs = PREFIX_TILE // PREFIX_SUB
+
+    def score(sub):
+        rows = slice(sub * PREFIX_SUB, (sub + 1) * PREFIX_SUB)
+        return lax.dot_general(
+            query[rows], keys, (((1,), (1,)), ((), ())), preferred_element_type=f32
+        )
+
+    def part_rows(sub):
+        pieces = []
+        per = QUERY_TILE // 2
+        for start in range(sub * PREFIX_SUB, (sub + 1) * PREFIX_SUB, min(per, PREFIX_SUB)):
+            second, rest = divmod(start, half_rows)
+            group, inside = divmod(rest, per)
+            first = group * QUERY_TILE + second * per + inside
+            pieces.append(part_ref[first : first + min(per, PREFIX_SUB), :])
+        return pieces[0] if len(pieces) == 1 else jnp.concatenate(pieces, axis=0)
+
+    contexts = []
+    scores = score(0)
+    for sub in range(subs):
+        following = score(sub + 1) if sub + 1 < subs else None
+        part = part_rows(sub)
+        part_top = part[:, 0:1]
+        part_total = part[:, 1:2]
+        top = jnp.maximum(part_top, jnp.max(scores, axis=1, keepdims=True))
+        probs = jnp.exp(scores - top)
+        shrink = jnp.exp(part_top - top)
+        total = part_total * shrink + jnp.sum(probs, axis=1, keepdims=True)
+        acc = part * shrink + jnp.dot(probs.astype(bf16), keys, preferred_element_type=f32)
+        contexts.append(acc / total)
+        scores = following
+    context = contexts[0] if subs == 1 else jnp.concatenate(contexts, axis=0)
     packed = jnp.where(low, pltpu.roll(context[:half_rows], HALF, 1), context[half_rows:])
     out_ref[pl.ds(tile * tile_blocks, tile_blocks), 0:16, :] = packed.astype(bf16).reshape(
         tile_blocks, 16, LANES
     )
+    row = lane_of((REQS, PREFIX_TILE))
+    second = (row >= half_rows).astype(jnp.int32)
+    within = row - second * half_rows
     positions = tile * tile_blocks * ROWS + quarter_ref[0] * 32
-    positions = positions + offset_of(lane_of((REQS, QUERY_TILE)))
+    positions = positions + (within // 16) * ROWS + second * 16 + within % 16
     is_last = last_matrix(lengths_ref, positions)
     ends = jnp.where(lane_of(context.shape) < HALF, 0.0, context).astype(bf16)
     ends = jnp.dot(is_last, ends, preferred_element_type=f32)
@@ -334,11 +365,11 @@
         prefix_kernel,
         grid_spec=pltpu.PrefetchScalarGridSpec(
             num_scalar_prefetch=2,
-            grid=(queries // QUERY_TILE,),
+            grid=(queries // PREFIX_TILE,),
             in_specs=[
-                pl.BlockSpec((QUERY_TILE // 32, 16, LANES), lambda i, q, l: (i, ROWS // 16, 0)),
+                pl.BlockSpec((PREFIX_TILE // 32, 16, LANES), lambda i, q, l: (i, ROWS // 16, 0)),
                 pl.BlockSpec((blocks, rows, LANES), lambda i, q, l: (0, 0, 0)),
-                pl.BlockSpec((QUERY_TILE, LANES), lambda i, q, l: (i, 0)),
+                pl.BlockSpec((PREFIX_TILE, LANES), lambda i, q, l: (i, 0)),
             ],
             out_specs=pl.BlockSpec((blocks, 32, LANES), lambda i, q, l: (0, 0, 0)),
             scratch_shapes=[pltpu.VMEM((REQS, LANES), f32)],
@@ -350,7 +381,9 @@
 
 
 def gelu(v):
-    return 0.5 * v * (1.0 + jnp.tanh(0.7978845608028654 * (v + 0.044715 * v * v * v)))
+    scale = 0.7978845608028654
+    half = 0.5 * v
+    return half + half * jnp.tanh(v * (scale + (scale * 0.044715) * (v * v)))
 
 
 def dot_nt(a, b):
@@ -505,33 +538,44 @@
     high = total.astype(bf16).astype(f32)
     low = (total - high).astype(bf16).astype(f32)
     sends = []
-    for part in range(2):
-        for tile in range(count // FFN_TILE):
-            rows = slice(tile * FFN_TILE, (tile + 1) * FFN_TILE)
-            if tile == 0:
-                copies[part][0].wait()
-                copies[part][1].wait()
-            x = x_ref[rows, :]
-            hidden = (gelu(dot_nt(x, gate_v[part])) * dot_nt(x, up_v[part])).astype(bf16)
-            if tile == 0:
-                copies[part][2].wait()
-            down = jnp.dot(hidden, down_v[part], preferred_element_type=f32)
-            if part == 0:
-                acc_v[rows, :] = down
-            else:
-                row = tile * FFN_TILE + lax.broadcasted_iota(jnp.int32, (FFN_TILE, 1), 0)
-                row = row % PART_ROWS
-                result = acc_v[rows, :] + down
-                result = jnp.where(row == PART_SLOTS, high, result)
-                result = jnp.where(row == PART_SLOTS + 1, low, result)
-                out_v[rows, :] = result.astype(bf16)
-                send = pltpu.make_async_copy(
-                    out_v.at[pl.ds(tile * FFN_TILE, FFN_TILE), :],
-                    out_ref.at[pl.ds(tile * FFN_TILE, FFN_TILE), :],
-                    out_sems.at[tile],
-                )
-                send.start()
-                sends.append(send)
+    tiles = count // FFN_TILE
+    work = [(part, tile) for part in range(2) for tile in range(tiles)]
+
+    def span(tile):
+        return slice(tile * FFN_TILE, (tile + 1) * FFN_TILE)
+
+    def lift(part, tile):
+        if tile == 0:
+            copies[part][0].wait()
+            copies[part][1].wait()
+        x = x_ref[span(tile), :]
+        return dot_nt(x, gate_v[part]), dot_nt(x, up_v[part])
+
+    ready = lift(*work[0])
+    for index, (part, tile) in enumerate(work):
+        gate, up = ready
+        if index + 1 < len(work):
+            ready = lift(*work[index + 1])
+        hidden = (gelu(gate) * up).astype(bf16)
+        if tile == 0:
+            copies[part][2].wait()
+        down = jnp.dot(hidden, down_v[part], preferred_element_type=f32)
+        if part == 0:
+            acc_v[span(tile), :] = down
+        else:
+            row = tile * FFN_TILE + lax.broadcasted_iota(jnp.int32, (FFN_TILE, 1), 0)
+            row = row % PART_ROWS
+            result = acc_v[span(tile), :] + down
+            result = jnp.where(row == PART_SLOTS, high, result)
+            result = jnp.where(row == PART_SLOTS + 1, low, result)
+            out_v[span(tile), :] = result.astype(bf16)
+            send = pltpu.make_async_copy(
+                out_v.at[pl.ds(tile * FFN_TILE, FFN_TILE), :],
+                out_ref.at[pl.ds(tile * FFN_TILE, FFN_TILE), :],
+                out_sems.at[tile],
+            )
+            send.start()
+            sends.append(send)
     for send in sends:
         send.wait()
 
@@ -643,9 +687,10 @@
         return lax.ppermute(one, "grp", [(i, (i + by) % size) for i in range(size)])
 
     pieces = {0: piece}
-    for by in (1, 2, -1, -2):
+    for by in (1, 2, -1):
         pieces[by % size] = shift(piece, by)
-    pieces[3] = shift(pieces[1], 2)
+    pieces[6] = shift(pieces[7], -1)
+    pieces[3] = shift(pieces[2], 1)
     pieces[4] = shift(pieces[2], 2)
     pieces[5] = shift(pieces[7], -2)
     return [pieces[k] for k in range(size)]
@@ -679,9 +724,7 @@
     with jax.named_scope("prefix_gather"):
         pieces = ring_pieces(prefix_cache[0])
         offset = (lax.axis_index("grp").astype(jnp.int32) - owners) % len(pieces)
-    with jax.named_scope("weight_swap"):
-        own = (w_gate[0].T, w_up[0].T, w_down[0])
-        other = tuple(lax.ppermute(one, "blk", swap) for one in own)
+    own = (w_gate[0].T, w_up[0].T, w_down[0])
     routes_t = routes[0].T
     gates_t = gates[0].T
     suffix_kv, send = project(
@@ -689,10 +732,14 @@
     )
     with jax.named_scope("qkv_exchange"):
         got = exchange(send.reshape(blocks, SEND_ROWS, LANES))
-    part = suffix_attention(quarter, lengths[0], got)
     packed = prefix_pack(pieces, offset, got)
+    with jax.named_scope("weight_swap"):
+        packed, *ready = lax.optimization_barrier((packed, *own))
+        other = [lax.ppermute(one, "blk", swap) for one in ready]
     with jax.named_scope("prefix_exchange"):
         prefix_got = exchange(packed.reshape(blocks, packed.shape[2], LANES))
+    part = suffix_attention(quarter, lengths[0], got)
+    part, *other = lax.optimization_barrier((part, *other))
     context = prefix_attention(quarter, lengths[0], got, prefix_got, part)
     with jax.named_scope("context_exchange"):
         ctx = exchange(context).reshape(HEADS, QUARTERS, 32, LANES)

time: 177 us -> 170 us (0.960)
  blocking collectives: 50.6 us -> 76.7 us
  waiting for transfers between devices: 37.4 us -> 14.6 us
  Pallas kernels: 46.7 us -> 42.7 us
  starting transfers between devices: 34.5 us -> 31.2 us
  local copies, waits for them, and re-layouts: 3.01 us -> 0.69 us
    all_to_all x3 -> x4, blocking collectives: 50.6 us -> 76.7 us  [exchange(): return lax.all_to_all(rows, 'blk', split_axis=0, concat_axis=0, tiled=True)]
    all_to_all x3 -> x2, waiting for transfers between devices: 17.3 us -> 4.01 us  [exchange(): return lax.all_to_all(rows, 'blk', split_axis=0, concat_axis=0, tiled=True)]
    all_to_all x3 -> x2, starting transfers between devices: 21.9 us -> 16 us  [exchange(): return lax.all_to_all(rows, 'blk', split_axis=0, concat_axis=0, tiled=True)]
    ppermute x3, waiting for transfers between devices: 5.53 us -> 0.01 us  [local(): other = [lax.ppermute(one, 'blk', swap) for one in ready]]
    ppermute x7, waiting for transfers between devices: 14.5 us -> 10.5 us  [shift(): return lax.ppermute(one, 'grp', [(i, (i + by) % size) for i in range(size)])]
    ppermute x3, starting transfers between devices: 0.99 us -> 4.79 us  [local(): other = [lax.ppermute(one, 'blk', swap) for one in ready]]
    unnamed x42 -> x36, local copies, waits for them, and re-layouts: 2.99 us -> 0.68 us
    pallas_call x1, Pallas kernels: 7.08 us -> 5.12 us  [prefix_attention(): pl.pallas_call(prefix_kernel, grid_spec=pltpu.PrefetchScalarGridSpec(num_...]
  transfers between devices with their start and end apart: 13 -> 12, of which waited for: 8 -> 7; matrix products, arithmetic and copies ran while one was open for 0% -> 0% of each run, Pallas kernels for 5% -> 5%
where the time goes in v5:
time: 170 us; the launch traced here: 169 us
  blocking collectives  76.7 us (45%)
  Pallas kernels  42.7 us (25%)
  starting transfers between devices  31.2 us (18%)
  waiting for transfers between devices  14.6 us (9%)
    all_to_all x4, blocking collectives, exchange(): return lax.all_to_all(rows, 'blk', split_axis=0, concat_axis=0, tiled=True)  76.7 us
    all_to_all x2, starting transfers between devices, exchange(): return lax.all_to_all(rows, 'blk', split_axis=0, concat_axis=0, tiled=True)  16 us
    pallas_call x1, Pallas kernels, expert(): pl.pallas_call(expert_kernel, in_specs=[vmem] + [hbm] * 6, out_specs=pl.B...  11.1 us
    ppermute x7, waiting for transfers between devices, shift(): return lax.ppermute(one, 'grp', [(i, (i + by) % size) for i in range(size)])  10.5 us
    ppermute x7, starting transfers between devices, shift(): return lax.ppermute(one, 'grp', [(i, (i + by) % size) for i in range(size)])  10.4 us
    pallas_call x1, Pallas kernels, suffix_attention(): pl.pallas_call(suffix_kernel, grid_spec=pltpu.PrefetchScalarGridSpec(num_...  8.9 us
    pallas_call x1, Pallas kernels, mix(): pl.pallas_call(mix_kernel, grid_spec=pltpu.PrefetchScalarGridSpec(num_sca...  6.58 us
    pallas_call x1, Pallas kernels, project(): pl.pallas_call(project_kernel, grid_spec=pltpu.PrefetchScalarGridSpec(num...  5.87 us
  transfers between devices with their start and end apart: 12, of which 7 were waited for; matrix products, arithmetic and copies ran while one was open for 0% of the time, Pallas kernels for 5%

profile of v5, /device:TPU:1, one launch (start us, length us, event | category | flops | bytes accessed | tf_op | source)
XLA Modules:
  0.0 169.4 jit_solution(4265326737523885224)
XLA Ops:
  0.7 5.9 %project.1 = (bf16[128,1024]{1,0:T(8,128)(2,1)}, bf16[8,4,176,128]{3,2,1,0:T(8,128)(2,1)}) custom-call(s32[1]{0:T(128)} %bitcast.block_ref, s32[16]{0:T(128)} %bitcast.50, bf16[128,1024]{1,0:T(8,128)(2,1)} %bitcast.44, f32[1,1024]{1,0:T(1,128)} %bitcast.68, bf16[1024,512]{1,0:T(8,128)(2,1)} %wq_ref.1, bf16[1024,1024]{1,0:T(8,128)(2,1)} %wv_ref.1, ...), custom_call_target="tpu_custom_call" | custom-call | tf_op jit(solution)/shard_map/project/pallas_call | solution.py:128
  6.5 8.8 %all-to-all-start = ((bf16[32,176,128]{2,1,0:T(8,128)(2,1)}), bf16[32,176,128]{2,1,0:T(8,128)(2,1)}, u32[]{:S(2)}, u32[]{:S(2)}) async-start(bf16[32,176,128]{2,1,0:T(8,128)(2,1)} %bitcast.62), calls=%async_computation | async-start | bytes 2883584 | tf_op jit(solution)/shard_map/qkv_exchange/all_to_all | solution.py:680
  15.3 5.7 %collective-permute-start.4 = (bf16[64,1024]{1,0:T(8,128)(2,1)S(1)}, bf16[64,1024]{1,0:T(8,128)(2,1)S(1)}, u32[]{:S(2)}, u32[]{:S(2)}) collective-permute-start(bf16[64,1024]{1,0:T(8,128)(2,1)S(1)} %bitcast.65), channel_id=1, source_target_pairs={{0,224},{32,0},{64,32},{96,64},{128,96},{160,128},{192,160},{224,1... | collective-permute-start | bytes 393224 | tf_op jit(solution)/shard_map/prefix_gather/ppermute | solution.py:687
  21.0 2.6 %collective-permute-done.4.refs_7_ = bf16[64,1024]{1,0:T(8,128)(2,1)S(1)} collective-permute-done((bf16[64,1024]{1,0:T(8,128)(2,1)S(1)}, bf16[64,1024]{1,0:T(8,128)(2,1)S(1)}, u32[]{:S(2)}, u32[]{:S(2)}) %collective-permute-start.4) | collective-permute-done | bytes 131104 | tf_op jit(solution)/shard_map/prefix_gather/ppermute | solution.py:687
  23.6 3.5 %collective-permute-start.6 = (bf16[64,1024]{1,0:T(8,128)(2,1)S(1)}, bf16[64,1024]{1,0:T(8,128)(2,1)S(1)}, u32[]{:S(2)}, u32[]{:S(2)}) collective-permute-start(bf16[64,1024]{1,0:T(8,128)(2,1)S(1)} %collective-permute-done.4.refs_7_), channel_id=1, source_target_pairs={{0,224},{32,0},{64,32},{96,64},{128,96},{160,128},{192,160},{224,1... | collective-permute-start | bytes 393224 | tf_op jit(solution)/shard_map/prefix_gather/ppermute | solution.py:687
  27.1 1.3 collective-permute-done.1.refs_2_
  28.4 1.1 collective-permute-start.3
  29.5 0.1 collective-permute-start.2
  30.3 0.9 collective-permute-done.6.refs_6_
  31.2 4.0 %collective-permute-done.5.refs_5_ = bf16[64,1024]{1,0:T(8,128)(2,1)S(1)} collective-permute-done((bf16[64,1024]{1,0:T(8,128)(2,1)S(1)}, bf16[64,1024]{1,0:T(8,128)(2,1)S(1)}, u32[]{:S(2)}, u32[]{:S(2)}) %collective-permute-start.5) | collective-permute-done | bytes 131104 | tf_op jit(solution)/shard_map/prefix_gather/ppermute | solution.py:687
  35.1 0.7 collective-permute-done.3.refs_4_
  35.8 1.2 collective-permute-done.2.refs_3_
  37.0 0.6 copy-done.17
  37.6 2.8 %prefix_pack.1 = bf16[8,4,80,128]{3,2,1,0:T(8,128)(2,1)} custom-call(s32[1]{0:T(128)S(6)} %select_n.12.offset_ref, bf16[32,176,128]{2,1,0:T(8,128)(2,1)} %all-to-all-done.ends_ref.query_ref.got_ref.gate_last_ref, bf16[64,1024]{1,0:T(8,128)(2,1)} %bitcast.64, bf16[64,1024]{1,0:T(8,128)(2,1)} %copy-done.13, bf16[64,1024]{1,0:T(8,128)(2,1)} %copy-done.12, ...), custom_call_target="tpu_custom_call" | custom-call | tf_op jit(solution)/shard_map/prefix_pack/pallas_call | solution.py:184
  40.4 4.3 %collective-permute-start.7 = (bf16[704,1024]{1,0:T(8,128)(2,1)}, bf16[704,1024]{1,0:T(8,128)(2,1)}, u32[]{:S(2)}, u32[]{:S(2)}) collective-permute-start(bf16[704,1024]{1,0:T(8,128)(2,1)} %bitcast.12.g_ref.g0), channel_id=1, source_target_pairs={{0,1},{1,0},{2,3},{3,2},{4,5},{5,4},{6,7},{7,6},{8,9},{9,8},{10,11... | collective-permute-start | bytes 4325384 | tf_op jit(solution)/shard_map/weight_swap/ppermute | solution.py:738
  44.7 0.1 collective-permute-start.8
  44.8 0.4 collective-permute-start.9
  45.2 7.2 %all-to-all-start.1 = ((bf16[32,80,128]{2,1,0:T(8,128)(2,1)}), bf16[32,80,128]{2,1,0:T(8,128)(2,1)}, u32[]{:S(2)}, u32[]{:S(2)}) async-start(bf16[32,80,128]{2,1,0:T(8,128)(2,1)} %bitcast.60), calls=%async_computation.1 | async-start | bytes 1310720 | tf_op jit(solution)/shard_map/prefix_exchange/all_to_all | solution.py:680
  52.5 8.9 %suffix_attention.1.part_ref = f32[1024,128]{1,0:T(8,128)} custom-call(s32[1]{0:T(128)S(6)} %select_n.11.quarter_ref, s32[16]{0:T(128)S(1)} %bitcast.51, bf16[32,176,128]{2,1,0:T(8,128)(2,1)} %all-to-all-done.ends_ref.query_ref.got_ref.gate_last_ref, bf16[32,176,128]{2,1,0:T(8,128)(2,1)} %all-to-all-done.ends_ref.query_ref.got_ref.gate_last_ref), custom_call_target="tpu_custom_call" | custom-call | tf_op jit(solution)/shard_map/suffix_attention/pallas_call | solution.py:272
  61.4 4.0 %all-to-all-done.1.keys_ref.tok_last_ref = bf16[32,80,128]{2,1,0:T(8,128)(2,1)} async-done(((bf16[32,80,128]{2,1,0:T(8,128)(2,1)}), bf16[32,80,128]{2,1,0:T(8,128)(2,1)}, u32[]{:S(2)}, u32[]{:S(2)}) %all-to-all-start.1) | async-done | bytes 655392 | tf_op jit(solution)/shard_map/prefix_exchange/all_to_all | solution.py:680
  65.4 5.1 %prefix_attention.1 = bf16[32,32,128]{2,1,0:T(8,128)(2,1)S(1)} custom-call(s32[1]{0:T(128)S(6)} %select_n.11.quarter_ref, s32[16]{0:T(128)S(1)} %bitcast.52, bf16[32,176,128]{2,1,0:T(8,128)(2,1)} %all-to-all-done.ends_ref.query_ref.got_ref.gate_last_ref, bf16[32,80,128]{2,1,0:T(8,128)(2,1)} %all-to-all-done.1.keys_ref.tok_last_ref, ...), custom_call_target="tpu_custom_call" | custom-call | tf_op jit(solution)/shard_map/prefix_attention/pallas_call | solution.py:364
  70.5 12.9 %all_to_all.30 = bf16[32,32,128]{2,1,0:T(8,128)(2,1)S(1)} all-to-all(bf16[32,32,128]{2,1,0:T(8,128)(2,1)S(1)} %prefix_attention.1), channel_id=1, replica_groups=mesh['grp'=8,'blk'=32] {'blk'}, dimensions={0} | all-to-all | bytes 524288 | tf_op jit(solution)/shard_map/context_exchange/all_to_all | solution.py:680
  83.5 6.6 %mix.1 = (f32[128,1024]{1,0:T(8,128)}, f32[16,1024]{1,0:T(8,128)}, bf16[8,2,48,1024]{3,2,1,0:T(8,128)(2,1)}) custom-call(s32[1]{0:T(128)} %bitcast.block_ref, bf16[8,4,32,128]{3,2,1,0:T(8,128)(2,1)S(1)} %bitcast.46, bf16[128,1024]{1,0:T(8,128)(2,1)S(1)} %bitcast.45, bf16[32,80,128]{2,1,0:T(8,128)(2,1)} %all-to-all-done.1.keys_ref.tok_last_ref, ...), custom_call_target="tpu_custom_call" | custom-call | tf_op jit(solution)/shard_map/mix/pallas_call | solution.py:475
  90.1 26.9 %all_to_all.31 = bf16[32,24,1024]{2,1,0:T(8,128)(2,1)S(1)} all-to-all(bf16[32,24,1024]{2,1,0:T(8,128)(2,1)} %bitcast.61), channel_id=1, replica_groups=mesh['grp'=8,'blk'=32] {'blk'}, dimensions={0} | all-to-all | bytes 3145728 | tf_op jit(solution)/shard_map/dispatch_exchange/all_to_all | solution.py:680
  117.0 11.1 %expert.1 = bf16[768,1024]{1,0:T(8,128)(2,1)} custom-call(bf16[768,1024]{1,0:T(8,128)(2,1)S(1)} %bitcast.43, bf16[704,1024]{1,0:T(8,128)(2,1)} %bitcast.12.g_ref.g0, bf16[704,1024]{1,0:T(8,128)(2,1)} %bitcast.14.u_ref.u0, bf16[704,1024]{1,0:T(8,128)(2,1)} %bitcast.15.d_ref.d0, bf16[704,1024]{1,0:T(8,128)(2,1)} %collective-permute-done.7.g1, ...), custom_call_target="tpu_custom_call" | custom-call | tf_op jit(solution)/shard_map/expert/pallas_call | solution.py:588
  128.1 26.6 %all_to_all.32 = bf16[32,24,1024]{2,1,0:T(8,128)(2,1)S(1)} all-to-all(bf16[32,24,1024]{2,1,0:T(8,128)(2,1)} %bitcast.59), channel_id=1, replica_groups=mesh['grp'=8,'blk'=32] {'blk'}, dimensions={0} | all-to-all | bytes 3145728 | tf_op jit(solution)/shard_map/return_exchange/all_to_all | solution.py:680
  154.7 2.4 %combine.1 = (bf16[128,1024]{1,0:T(8,128)(2,1)}, bf16[16,1024]{1,0:T(8,128)(2,1)S(1)}, f32[1,128]{1,0:T(1,128)S(1)}) custom-call(s32[1]{0:T(128)} %bitcast.block_ref, s32[16]{0:T(128)S(1)} %bitcast.53, f32[128,1024]{1,0:T(8,128)S(1)} %copy-done.3, f32[16,1024]{1,0:T(8,128)S(1)} %copy-done.4, bf16[768,1024]{1,0:T(8,128)(2,1)S(1)} %bitcast.42, ...), custom_call_target="tpu_custom_call" | custom-call | tf_op jit(solution)/shard_map/combine/pallas_call | solution.py:665
  157.0 0.8 convolution_reduce_fusion
  157.8 0.1 fusion.2
  157.9 10.4 %all_to_all.33 = f32[32,1,128]{2,1,0:T(1,128)S(1)} all-to-all(f32[32,1,128]{2,1,0:T(1,128)S(1)} %broadcast_in_dim.25), channel_id=1, replica_groups=mesh['grp'=8,'blk'=32] {'blk'}, dimensions={0} | all-to-all | bytes 32768 | tf_op jit(solution)/shard_map/final_exchange/all_to_all | solution.py:680
  168.3 0.6 slice_reduce_fusion
  168.9 0.5 fusion.1
  (44 shorter events, 0.1 us)
Async XLA Ops:
  0.6 156.4 %copy-start = (bf16[1024,1004]{0,1:T(8,128)(2,1)S(1)}, bf16[1024,1004]{0,1:T(8,128)(2,1)}, u32[]{:S(2)}) copy-start(bf16[1024,1004]{0,1:T(8,128)(2,1)} %param.31) | copy-start | bytes 6168580
  6.5 8.8 %copy-start.10 = (bf16[1,64,1024]{2,1,0:T(8,128)(2,1)S(1)}, bf16[1,64,1024]{2,1,0:T(8,128)(2,1)}, u32[]{:S(2)}) copy-start(bf16[1,64,1024]{2,1,0:T(8,128)(2,1)} %param.19) | copy-start | bytes 393220
  6.5 30.5 %all-to-all-start = ((bf16[32,176,128]{2,1,0:T(8,128)(2,1)}), bf16[32,176,128]{2,1,0:T(8,128)(2,1)}, u32[]{:S(2)}, u32[]{:S(2)}) async-start(bf16[32,176,128]{2,1,0:T(8,128)(2,1)} %bitcast.62), calls=%async_computation | async-start | bytes 2883584 | tf_op jit(solution)/shard_map/qkv_exchange/all_to_all | solution.py:680
  15.3 8.2 %collective-permute-start.4 = (bf16[64,1024]{1,0:T(8,128)(2,1)S(1)}, bf16[64,1024]{1,0:T(8,128)(2,1)S(1)}, u32[]{:S(2)}, u32[]{:S(2)}) collective-permute-start(bf16[64,1024]{1,0:T(8,128)(2,1)S(1)} %bitcast.65), channel_id=1, source_target_pairs={{0,224},{32,0},{64,32},{96,64},{128,96},{160,128},{192,160},{224,1... | collective-permute-start | bytes 393224 | tf_op jit(solution)/shard_map/prefix_gather/ppermute | solution.py:687
  21.0 7.4 %collective-permute-start.1 = (bf16[64,1024]{1,0:T(8,128)(2,1)S(1)}, bf16[64,1024]{1,0:T(8,128)(2,1)S(1)}, u32[]{:S(2)}, u32[]{:S(2)}) collective-permute-start(bf16[64,1024]{1,0:T(8,128)(2,1)S(1)} %bitcast.66), channel_id=1, source_target_pairs={{0,64},{32,96},{64,128},{96,160},{128,192},{160,224},{192,0},{224,... | collective-permute-start | bytes 393224 | tf_op jit(solution)/shard_map/prefix_gather/ppermute | solution.py:687
  21.0 9.3 %collective-permute-start = (bf16[64,1024]{1,0:T(8,128)(2,1)S(1)}, bf16[64,1024]{1,0:T(8,128)(2,1)S(1)}, u32[]{:S(2)}, u32[]{:S(2)}) collective-permute-start(bf16[64,1024]{1,0:T(8,128)(2,1)S(1)} %bitcast.67), channel_id=1, source_target_pairs={{0,32},{32,64},{64,96},{96,128},{128,160},{160,192},{192,224},{224... | collective-permute-start | bytes 393224 | tf_op jit(solution)/shard_map/prefix_gather/ppermute | solution.py:687
  23.6 13.4 %copy-start.11 = (bf16[64,1024]{1,0:T(8,128)(2,1)}, bf16[64,1024]{1,0:T(8,128)(2,1)S(1)}, u32[]{:S(2)}) copy-start(bf16[64,1024]{1,0:T(8,128)(2,1)S(1)} %collective-permute-done.4.refs_7_) | copy-start | bytes 393220
  23.6 7.6 %collective-permute-start.6 = (bf16[64,1024]{1,0:T(8,128)(2,1)S(1)}, bf16[64,1024]{1,0:T(8,128)(2,1)S(1)}, u32[]{:S(2)}, u32[]{:S(2)}) collective-permute-start(bf16[64,1024]{1,0:T(8,128)(2,1)S(1)} %collective-permute-done.4.refs_7_), channel_id=1, source_target_pairs={{0,224},{32,0},{64,32},{96,64},{128,96},{160,128},{192,160},{224,1... | collective-permute-start | bytes 393224 | tf_op jit(solution)/shard_map/prefix_gather/ppermute | solution.py:687
  27.1 8.1 %collective-permute-start.5 = (bf16[64,1024]{1,0:T(8,128)(2,1)S(1)}, bf16[64,1024]{1,0:T(8,128)(2,1)S(1)}, u32[]{:S(2)}, u32[]{:S(2)}) collective-permute-start(bf16[64,1024]{1,0:T(8,128)(2,1)S(1)} %collective-permute-done.4.refs_7_), channel_id=1, source_target_pairs={{0,192},{32,224},{64,0},{96,32},{128,64},{160,96},{192,128},{224,1... | collective-permute-start | bytes 393224 | tf_op jit(solution)/shard_map/prefix_gather/ppermute | solution.py:687
  28.4 8.6 %copy-start.12 = (bf16[64,1024]{1,0:T(8,128)(2,1)}, bf16[64,1024]{1,0:T(8,128)(2,1)S(1)}, u32[]{:S(2)}) copy-start(bf16[64,1024]{1,0:T(8,128)(2,1)S(1)} %collective-permute-done.1.refs_2_) | copy-start | bytes 393220
  28.4 7.5 %collective-permute-start.3 = (bf16[64,1024]{1,0:T(8,128)(2,1)S(1)}, bf16[64,1024]{1,0:T(8,128)(2,1)S(1)}, u32[]{:S(2)}, u32[]{:S(2)}) collective-permute-start(bf16[64,1024]{1,0:T(8,128)(2,1)S(1)} %collective-permute-done.1.refs_2_), channel_id=1, source_target_pairs={{0,64},{32,96},{64,128},{96,160},{128,192},{160,224},{192,0},{224,... | collective-permute-start | bytes 393224 | tf_op jit(solution)/shard_map/prefix_gather/ppermute | solution.py:687
  29.5 7.5 %collective-permute-start.2 = (bf16[64,1024]{1,0:T(8,128)(2,1)S(1)}, bf16[64,1024]{1,0:T(8,128)(2,1)S(1)}, u32[]{:S(2)}, u32[]{:S(2)}) collective-permute-start(bf16[64,1024]{1,0:T(8,128)(2,1)S(1)} %collective-permute-done.1.refs_2_), channel_id=1, source_target_pairs={{0,32},{32,64},{64,96},{96,128},{128,160},{160,192},{192,224},{224... | collective-permute-start | bytes 393224 | tf_op jit(solution)/shard_map/prefix_gather/ppermute | solution.py:687
  30.3 22.2 %copy-start.6 = (s32[1,16]{1,0:T(1,128)S(1)}, s32[1,16]{1,0:T(1,128)}, u32[]{:S(2)}) copy-start(s32[1,16]{1,0:T(1,128)} %param.17) | copy-start | bytes 196
  30.3 6.7 %copy-start.13 = (bf16[64,1024]{1,0:T(8,128)(2,1)}, bf16[64,1024]{1,0:T(8,128)(2,1)S(1)}, u32[]{:S(2)}) copy-start(bf16[64,1024]{1,0:T(8,128)(2,1)S(1)} %collective-permute-done.refs_1_) | copy-start | bytes 393220
  31.2 5.9 %copy-start.14 = (bf16[64,1024]{1,0:T(8,128)(2,1)}, bf16[64,1024]{1,0:T(8,128)(2,1)S(1)}, u32[]{:S(2)}) copy-start(bf16[64,1024]{1,0:T(8,128)(2,1)S(1)} %collective-permute-done.6.refs_6_) | copy-start | bytes 393220
  35.1 1.9 %copy-start.15 = (bf16[64,1024]{1,0:T(8,128)(2,1)}, bf16[64,1024]{1,0:T(8,128)(2,1)S(1)}, u32[]{:S(2)}) copy-start(bf16[64,1024]{1,0:T(8,128)(2,1)S(1)} %collective-permute-done.5.refs_5_) | copy-start | bytes 393220
  35.8 1.2 copy-start.16
  37.0 0.7 copy-start.17
  40.4 21.0 %collective-permute-start.7 = (bf16[704,1024]{1,0:T(8,128)(2,1)}, bf16[704,1024]{1,0:T(8,128)(2,1)}, u32[]{:S(2)}, u32[]{:S(2)}) collective-permute-start(bf16[704,1024]{1,0:T(8,128)(2,1)} %bitcast.12.g_ref.g0), channel_id=1, source_target_pairs={{0,1},{1,0},{2,3},{3,2},{4,5},{5,4},{6,7},{7,6},{8,9},{9,8},{10,11... | collective-permute-start | bytes 4325384 | tf_op jit(solution)/shard_map/weight_swap/ppermute | solution.py:738
  44.7 16.7 %collective-permute-start.8 = (bf16[704,1024]{1,0:T(8,128)(2,1)}, bf16[704,1024]{1,0:T(8,128)(2,1)}, u32[]{:S(2)}, u32[]{:S(2)}) collective-permute-start(bf16[704,1024]{1,0:T(8,128)(2,1)} %bitcast.14.u_ref.u0), channel_id=1, source_target_pairs={{0,1},{1,0},{2,3},{3,2},{4,5},{5,4},{6,7},{7,6},{8,9},{9,8},{10,11... | collective-permute-start | bytes 4325384 | tf_op jit(solution)/shard_map/weight_swap/ppermute | solution.py:738
  44.8 16.6 %collective-permute-start.9 = (bf16[704,1024]{1,0:T(8,128)(2,1)}, bf16[704,1024]{1,0:T(8,128)(2,1)}, u32[]{:S(2)}, u32[]{:S(2)}) collective-permute-start(bf16[704,1024]{1,0:T(8,128)(2,1)} %bitcast.15.d_ref.d0), channel_id=1, source_target_pairs={{0,1},{1,0},{2,3},{3,2},{4,5},{5,4},{6,7},{7,6},{8,9},{9,8},{10,11... | collective-permute-start | bytes 4325384 | tf_op jit(solution)/shard_map/weight_swap/ppermute | solution.py:738
  45.2 20.2 %all-to-all-start.1 = ((bf16[32,80,128]{2,1,0:T(8,128)(2,1)}), bf16[32,80,128]{2,1,0:T(8,128)(2,1)}, u32[]{:S(2)}, u32[]{:S(2)}) async-start(bf16[32,80,128]{2,1,0:T(8,128)(2,1)} %bitcast.60), calls=%async_computation.1 | async-start | bytes 1310720 | tf_op jit(solution)/shard_map/prefix_exchange/all_to_all | solution.py:680
  61.4 22.1 %copy-start.1 = (bf16[512,1024]{1,0:T(8,128)(2,1)S(1)}, bf16[512,1024]{1,0:T(8,128)(2,1)}, u32[]{:S(2)}) copy-start(bf16[512,1024]{1,0:T(8,128)(2,1)} %wout_ref.1) | copy-start | bytes 3145732
  61.4 22.1 %copy-start.2 = (bf16[1,128,1024]{2,1,0:T(8,128)(2,1)S(1)}, bf16[1,128,1024]{2,1,0:T(8,128)(2,1)}, u32[]{:S(2)}) copy-start(bf16[1,128,1024]{2,1,0:T(8,128)(2,1)} %param.16) | copy-start | bytes 786436
  61.4 22.1 %copy-start.5 = (s32[1,128,2]{1,2,0:T(2,128)S(1)}, s32[1,128,2]{1,2,0:T(2,128)}, u32[]{:S(2)}) copy-start(s32[1,128,2]{1,2,0:T(2,128)} %param.20) | copy-start | bytes 3076
  61.4 22.1 %copy-start.7 = (f32[1024]{0:T(1024)S(1)}, f32[1024]{0:T(1024)}, u32[]{:S(2)}) copy-start(f32[1024]{0:T(1024)} %param.26) | copy-start | bytes 12292
  128.0 26.6 %copy-start.3 = (f32[128,1024]{1,0:T(8,128)S(1)}, f32[128,1024]{1,0:T(8,128)}, u32[]{:S(2)}) copy-start(f32[128,1024]{1,0:T(8,128)} %get-tuple-element.26.mixed_ref) | copy-start | bytes 1572868
  128.1 26.6 %copy-start.4 = (f32[16,1024]{1,0:T(8,128)S(1)}, f32[16,1024]{1,0:T(8,128)}, u32[]{:S(2)}) copy-start(f32[16,1024]{1,0:T(8,128)} %get-tuple-element.27.mixed_last_ref) | copy-start | bytes 196612
  128.1 26.6 %copy-start.8 = (f32[1024]{0:T(1024)S(1)}, f32[1024]{0:T(1024)}, u32[]{:S(2)}) copy-start(f32[1024]{0:T(1024)} %param.30) | copy-start | bytes 12292
  128.1 26.6 %copy-start.9 = (f32[1,128,2]{1,2,0:T(2,128)S(1)}, f32[1,128,2]{1,2,0:T(2,128)}, u32[]{:S(2)}) copy-start(f32[1,128,2]{1,2,0:T(2,128)} %param.21) | copy-start | bytes 3076

commit v6 on v5

--- a/solution.py
+++ b/solution.py
@@ -13,6 +13,7 @@
 PART_ROWS = 24
 PART_SLOTS = 20
 SEND_ROWS = 176
+PAIRS = 2
 REQS = 16
 ROWS = 128
 HALF = 64
@@ -71,10 +72,10 @@
     block_ref, lengths_ref, tok_ref, gain_ref, wq_ref, wk_ref, wv_ref, routes_ref, gates_ref,
     kv_ref, send_ref, normed_ref, gate_ref,
 ):
-    pair = pl.program_id(0)
+    step = pl.program_id(0)
     is_last = last_matrix(lengths_ref, block_ref[0] * ROWS + lane_of((REQS, ROWS)))
 
-    @pl.when(pair == 0)
+    @pl.when(step == 0)
     def _():
         normed_ref[...] = rms_scale(tok_ref[...].astype(f32), gain_ref[...]).astype(bf16)
         row = lax.broadcasted_iota(jnp.int32, (LANES, ROWS), 0)
@@ -97,30 +98,32 @@
     query = jnp.dot(normed, wq_ref[...], preferred_element_type=f32).astype(bf16)
     key = jnp.dot(normed, wk_ref[...], preferred_element_type=f32).astype(bf16)
     value = jnp.dot(normed, wv_ref[...], preferred_element_type=f32).astype(bf16)
-    column = pl.multiple_of(pair * LANES, LANES)
-    kv_ref[:, pl.ds(column, LANES)] = key
-    kv_ref[:, pl.ds(HEADS * HALF + column, LANES)] = value
-    even, odd = head_split(key.astype(f32), value.astype(f32))
-    even = even.astype(bf16)
-    odd = odd.astype(bf16)
-    wide = pl.multiple_of(pair * 2 * LANES, 2 * LANES)
+    column = pl.multiple_of(step * PAIRS * LANES, PAIRS * LANES)
+    kv_ref[:, pl.ds(column, PAIRS * LANES)] = key
+    kv_ref[:, pl.ds(HEADS * HALF + column, PAIRS * LANES)] = value
+    wide = pl.multiple_of(step * 2 * PAIRS * LANES, 2 * PAIRS * LANES)
     ends = jnp.dot(
-        is_last, tok_ref[:, pl.ds(wide, 2 * LANES)], preferred_element_type=f32
+        is_last, tok_ref[:, pl.ds(wide, 2 * PAIRS * LANES)], preferred_element_type=f32
     ).astype(bf16)
     scaled = query.astype(f32) * (HALF**-0.5)
-    for quarter in range(QUARTERS):
-        first = scaled[quarter * 32 : quarter * 32 + 16]
-        second = scaled[quarter * 32 + 16 : quarter * 32 + 32]
-        query_even, query_odd = head_split(first, second)
-        send_ref[0, quarter, 0:ROWS, :] = even
-        send_ref[1, quarter, 0:ROWS, :] = odd
-        send_ref[0, quarter, ROWS : ROWS + 16, :] = query_even.astype(bf16)
-        send_ref[1, quarter, ROWS : ROWS + 16, :] = query_odd.astype(bf16)
-        for which in range(2):
-            send_ref[which, quarter, ROWS + 16 : ROWS + 32, :] = ends[
-                :, which * LANES : (which + 1) * LANES
-            ]
-            send_ref[which, quarter, ROWS + 32 : ROWS + 48, :] = gate_ref[...]
+    for pair in range(PAIRS):
+        lanes = slice(pair * LANES, (pair + 1) * LANES)
+        even, odd = head_split(key[:, lanes].astype(f32), value[:, lanes].astype(f32))
+        even = even.astype(bf16)
+        odd = odd.astype(bf16)
+        for quarter in range(QUARTERS):
+            first = scaled[quarter * 32 : quarter * 32 + 16, lanes]
+            second = scaled[quarter * 32 + 16 : quarter * 32 + 32, lanes]
+            query_even, query_odd = head_split(first, second)
+            send_ref[2 * pair, quarter, 0:ROWS, :] = even
+            send_ref[2 * pair + 1, quarter, 0:ROWS, :] = odd
+            send_ref[2 * pair, quarter, ROWS : ROWS + 16, :] = query_even.astype(bf16)
+            send_ref[2 * pair + 1, quarter, ROWS : ROWS + 16, :] = query_odd.astype(bf16)
+            for which in range(2 * pair, 2 * pair + 2):
+                send_ref[which, quarter, ROWS + 16 : ROWS + 32, :] = ends[
+                    :, which * LANES : (which + 1) * LANES
+                ]
+                send_ref[which, quarter, ROWS + 32 : ROWS + 48, :] = gate_ref[...]
 
 
 def project(block, lengths, stream, gain, w_query, w_keyval, routes_t, gates_t):
@@ -129,19 +132,19 @@
         project_kernel,
         grid_spec=pltpu.PrefetchScalarGridSpec(
             num_scalar_prefetch=2,
-            grid=(HEADS // 2,),
+            grid=(HEADS // 2 // PAIRS,),
             in_specs=[
                 pl.BlockSpec((ROWS, width), lambda i, b, l: (0, 0)),
                 pl.BlockSpec((1, width), lambda i, b, l: (0, 0)),
-                pl.BlockSpec((width, LANES), lambda i, b, l: (0, i)),
-                pl.BlockSpec((width, LANES), lambda i, b, l: (0, i)),
-                pl.BlockSpec((width, LANES), lambda i, b, l: (0, i + HEADS // 2)),
+                pl.BlockSpec((width, PAIRS * LANES), lambda i, b, l: (0, i)),
+                pl.BlockSpec((width, PAIRS * LANES), lambda i, b, l: (0, i)),
+                pl.BlockSpec((width, PAIRS * LANES), lambda i, b, l: (0, i + HEADS // 2 // PAIRS)),
                 pl.BlockSpec((2, ROWS), lambda i, b, l: (0, 0)),
                 pl.BlockSpec((2, ROWS), lambda i, b, l: (0, 0)),
             ],
             out_specs=[
                 pl.BlockSpec((ROWS, 2 * HEADS * HALF), lambda i, b, l: (0, 0)),
-                pl.BlockSpec((2, QUARTERS, SEND_ROWS, LANES), lambda i, b, l: (i, 0, 0, 0)),
+                pl.BlockSpec((2 * PAIRS, QUARTERS, SEND_ROWS, LANES), lambda i, b, l: (i, 0, 0, 0)),
             ],
             scratch_shapes=[pltpu.VMEM((ROWS, width), bf16), pltpu.VMEM((REQS, LANES), bf16)],
         ),
@@ -149,13 +152,18 @@
             jax.ShapeDtypeStruct((ROWS, 2 * HEADS * HALF), bf16),
             jax.ShapeDtypeStruct((HEADS, QUARTERS, SEND_ROWS, LANES), bf16),
         ],
+        compiler_params=pltpu.CompilerParams(vmem_limit_bytes=24 << 20),
         name="project",
-    )(block, lengths, stream, gain, w_query, w_keyval, w_keyval, routes_t, gates_t)
-
-
-def prefix_pack_kernel(offset_ref, ends_ref, *refs):
-    pieces = refs[: len(refs) - 3]
-    out_ref, prefix_v, sem = refs[len(refs) - 3 :]
+    )(block, lengths, *in_hbm(stream, gain, w_query, w_keyval, w_keyval, routes_t, gates_t))
+
+
+def prefix_pack_kernel(offset_ref, got_ref, *refs):
+    pieces = refs[: len(refs) - 5]
+    out_ref, prefix_v, ends_v, sem, ends_sem = refs[len(refs) - 5 :]
+    ends_copy = pltpu.make_async_copy(
+        got_ref.at[:, pl.ds(ROWS + 16, REQS), :], ends_v, ends_sem
+    )
+    ends_copy.start()
     for k, piece in enumerate(pieces):
 
         @pl.when(offset_ref[0] == k)
@@ -165,6 +173,11 @@
             copy.wait()
 
     rows = prefix_v.shape[0]
+    ends_copy.wait()
+    ends = jnp.sum(ends_v[...].astype(f32), axis=0).astype(bf16)
+    for head in range(HEADS):
+        for quarter in range(QUARTERS):
+            out_ref[head, quarter, rows : rows + REQS, :] = ends
     for pair in range(HEADS // 2):
         key = prefix_v[:, pair * LANES : (pair + 1) * LANES].astype(f32)
         base = HEADS * HALF + pair * LANES
@@ -173,10 +186,6 @@
         for quarter in range(QUARTERS):
             out_ref[2 * pair, quarter, 0:rows, :] = even.astype(bf16)
             out_ref[2 * pair + 1, quarter, 0:rows, :] = odd.astype(bf16)
-    ends = jnp.sum(ends_ref[...].astype(f32), axis=0).astype(bf16)
-    for head in range(HEADS):
-        for quarter in range(QUARTERS):
-            out_ref[head, quarter, rows : rows + REQS, :] = ends
 
 
 def prefix_pack(pieces, offset, got):
@@ -186,14 +195,16 @@
         grid_spec=pltpu.PrefetchScalarGridSpec(
             num_scalar_prefetch=1,
             grid=(1,),
-            in_specs=[
-                pl.BlockSpec((got.shape[0], REQS, LANES), lambda i, owner: (0, 9, 0)),
-            ]
-            + [pl.BlockSpec(memory_space=pl.ANY)] * len(pieces),
+            in_specs=[pl.BlockSpec(memory_space=pl.ANY)] * (1 + len(pieces)),
             out_specs=pl.BlockSpec(
                 (HEADS, QUARTERS, rows + REQS, LANES), lambda i, owner: (0, 0, 0, 0)
             ),
-            scratch_shapes=[pltpu.VMEM((rows, width), bf16), pltpu.SemaphoreType.DMA(())],
+            scratch_shapes=[
+                pltpu.VMEM((rows, width), bf16),
+                pltpu.VMEM((got.shape[0], REQS, LANES), bf16),
+                pltpu.SemaphoreType.DMA(()),
+                pltpu.SemaphoreType.DMA(()),
+            ],
         ),
         out_shape=jax.ShapeDtypeStruct((HEADS, QUARTERS, rows + REQS, LANES), bf16),
         name="prefix_pack",
@@ -392,14 +403,8 @@
 
 def mix_kernel(
     block_ref, ctx_ref, tok_ref, tok_last_ref, gate_last_ref, wout_ref, gain_ref, routes_ref, g_ref, u_ref, d_ref,
-    mixed_ref, mixed_last_ref, send_ref, g_v, u_v, d_v, send_v, sems, out_sems,
+    mixed_ref, mixed_last_ref, send_ref, send_v, out_sems,
 ):
-    copies = [
-        pltpu.make_async_copy(source, place, sems.at[kind])
-        for kind, (source, place) in enumerate(((g_ref, g_v), (u_ref, u_v), (d_ref, d_v)))
-    ]
-    for copy in copies:
-        copy.start()
     tiles = []
     for pair in range(HEADS // 2):
         even = ctx_ref[2 * pair].astype(f32)
@@ -425,15 +430,11 @@
     lane = lane_of(weights.shape)
     mine = (lane % EXPERTS == expert_id) & (lane < 3 * EXPERTS)
     weight = jnp.sum(jnp.where(mine, weights, 0.0), axis=1, keepdims=True)
-    copies[0].wait()
-    copies[1].wait()
-    act = (gelu(dot_nt(routed_last, g_v[...])) * dot_nt(routed_last, u_v[...])).astype(bf16)
-    copies[2].wait()
-    partial_last = weight * jnp.dot(act, d_v[...], preferred_element_type=f32)
+    act = (gelu(dot_nt(routed_last, g_ref[...])) * dot_nt(routed_last, u_ref[...])).astype(bf16)
+    partial_last = weight * jnp.dot(act, d_ref[...], preferred_element_type=f32)
     high = partial_last.astype(bf16)
     low_part = (partial_last - high.astype(f32)).astype(bf16)
     source = jnp.concatenate([routed, high, low_part], axis=0)
-    columns = ROWS + 2 * REQS
     expert = lax.broadcasted_iota(jnp.int32, (EXPERTS, ROWS), 0)
     named = (routes_ref[0:1, :] == expert) | (routes_ref[1:2, :] == expert)
     earlier = (
@@ -446,7 +447,7 @@
     place_id = lax.broadcasted_iota(jnp.int32, (SLOT_ROWS, ROWS), 0)
     extra_row = lax.broadcasted_iota(jnp.int32, (SLOT_ROWS, 2 * REQS), 0) % PART_ROWS
     extra_column = lane_of((SLOT_ROWS, 2 * REQS))
-    sends = []
+    picks = []
     for e in range(EXPERTS):
         pick = (place[e : e + 1, :] == place_id).astype(f32)
         for chip in range(2):
@@ -454,21 +455,29 @@
             extra = ((extra_row == PART_SLOTS) & (extra_column == row_last)) | (
                 (extra_row == PART_SLOTS + 1) & (extra_column == REQS + row_last)
             )
-            both = jnp.concatenate([pick, extra.astype(f32)], axis=1).astype(bf16)
-            send_v[e, chip] = jnp.dot(both, source, preferred_element_type=f32).astype(bf16)
-        send = pltpu.make_async_copy(send_v.at[e], send_ref.at[e], out_sems.at[e])
+            picks.append(jnp.concatenate([pick, extra.astype(f32)], axis=1).astype(bf16))
+    sends = []
+    per = len(picks) // MIX_PARTS
+    rows = per * SLOT_ROWS
+    for part in range(MIX_PARTS):
+        chosen = jnp.concatenate(picks[part * per : (part + 1) * per], axis=0)
+        send_v[part] = jnp.dot(chosen, source, preferred_element_type=f32).astype(bf16)
+        send = pltpu.make_async_copy(
+            send_v.at[part], send_ref.at[pl.ds(part * rows, rows), :], out_sems.at[part]
+        )
         send.start()
         sends.append(send)
     for send in sends:
         send.wait()
 
 
+MIX_PARTS = 2
+
+
 def mix(block, ctx, stream, prefix_got, got, w_out, gain, routes_t, own):
     width = stream.shape[1]
     blocks = got.shape[0]
     units = own[0].shape[0]
-    hbm = pl.BlockSpec(memory_space=pl.ANY)
-
     def whole(shape):
         return pl.BlockSpec(shape, lambda i, b: (0,) * len(shape))
 
@@ -485,9 +494,9 @@
                 whole(w_out.shape),
                 whole(gain.shape),
                 whole(routes_t.shape),
-                hbm,
-                hbm,
-                hbm,
+                whole((units, width)),
+                whole((units, width)),
+                whole((units, width)),
             ],
             out_specs=[
                 whole((ROWS, width)),
@@ -495,42 +504,27 @@
                 pl.BlockSpec(memory_space=pltpu.HBM),
             ],
             scratch_shapes=[
-                pltpu.VMEM((units, width), bf16),
-                pltpu.VMEM((units, width), bf16),
-                pltpu.VMEM((units, width), bf16),
-                pltpu.VMEM((EXPERTS, 2, SLOT_ROWS, width), bf16),
-                pltpu.SemaphoreType.DMA((3,)),
-                pltpu.SemaphoreType.DMA((EXPERTS,)),
+                pltpu.VMEM((MIX_PARTS, 2 * EXPERTS * SLOT_ROWS // MIX_PARTS, width), bf16),
+                pltpu.SemaphoreType.DMA((MIX_PARTS,)),
             ],
         ),
         out_shape=[
             pltpu.HBM((ROWS, width), f32),
             pltpu.HBM((REQS, width), f32),
-            pltpu.HBM((EXPERTS, 2, SLOT_ROWS, width), bf16),
+            pltpu.HBM((2 * EXPERTS * SLOT_ROWS, width), bf16),
         ],
         compiler_params=pltpu.CompilerParams(vmem_limit_bytes=18 << 20),
         name="mix",
-    )(block, ctx, stream, *in_hbm(prefix_got, got), w_out, gain, routes_t, *in_hbm(*own))
+    )(block, ctx, stream, *in_hbm(prefix_got, got), w_out, gain, routes_t, *own)
 
 
 FFN_TILE = 256
 
 
 def expert_kernel(
-    x_ref, g0, u0, d0, g1, u1, d1, out_ref, gate_v, up_v, down_v, acc_v, out_v, sems, out_sems
+    x_ref, g0, u0, d0, g1, u1, d1, out_ref, acc_v, out_v, out_sems
 ):
-    sources = ((g0, u0, d0), (g1, u1, d1))
-    places = (gate_v, up_v, down_v)
-    copies = [
-        [
-            pltpu.make_async_copy(sources[part][kind], places[kind].at[part], sems.at[part, kind])
-            for kind in range(3)
-        ]
-        for part in range(2)
-    ]
-    for part in range(2):
-        for kind in range(3):
-            copies[part][kind].start()
+    weights = ((g0, u0, d0), (g1, u1, d1))
     count = x_ref.shape[0]
     within = lane_of((16, count)) % PART_ROWS
     extra = ((within == PART_SLOTS) | (within == PART_SLOTS + 1)).astype(f32).astype(bf16)
@@ -545,11 +539,8 @@
         return slice(tile * FFN_TILE, (tile + 1) * FFN_TILE)
 
     def lift(part, tile):
-        if tile == 0:
-            copies[part][0].wait()
-            copies[part][1].wait()
         x = x_ref[span(tile), :]
-        return dot_nt(x, gate_v[part]), dot_nt(x, up_v[part])
+        return dot_nt(x, weights[part][0][...]), dot_nt(x, weights[part][1][...])
 
     ready = lift(*work[0])
     for index, (part, tile) in enumerate(work):
@@ -557,9 +548,7 @@
         if index + 1 < len(work):
             ready = lift(*work[index + 1])
         hidden = (gelu(gate) * up).astype(bf16)
-        if tile == 0:
-            copies[part][2].wait()
-        down = jnp.dot(hidden, down_v[part], preferred_element_type=f32)
+        down = jnp.dot(hidden, weights[part][2][...], preferred_element_type=f32)
         if part == 0:
             acc_v[span(tile), :] = down
         else:
@@ -582,26 +571,20 @@
 
 def expert(rows, own, other):
     count, width = rows.shape
-    units = own[0].shape[0]
-    hbm = pl.BlockSpec(memory_space=pl.ANY)
     vmem = pl.BlockSpec(memory_space=pltpu.VMEM)
     return pl.pallas_call(
         expert_kernel,
-        in_specs=[vmem] + [hbm] * 6,
+        in_specs=[vmem] * 7,
         out_specs=pl.BlockSpec(memory_space=pltpu.HBM),
         out_shape=pltpu.HBM((count, width), bf16),
         scratch_shapes=[
-            pltpu.VMEM((2, units, width), bf16),
-            pltpu.VMEM((2, units, width), bf16),
-            pltpu.VMEM((2, units, width), bf16),
             pltpu.VMEM((count, width), f32),
             pltpu.VMEM((count, width), bf16),
-            pltpu.SemaphoreType.DMA((2, 3)),
             pltpu.SemaphoreType.DMA((count // FFN_TILE,)),
         ],
         compiler_params=pltpu.CompilerParams(vmem_limit_bytes=26 << 20),
         name="expert",
-    )(rows, *in_hbm(*own, *other))
+    )(rows, *own, *other)
 
 
 def column_of(row):
@@ -618,9 +601,6 @@
     wanted = request_row * (2 * PART_ROWS) + PART_SLOTS
     source = lane_of((REQS, count))
     pick_last = ((source == wanted) | (source == wanted + 1)).astype(f32).astype(bf16)
-    moe_last = jnp.dot(pick_last, got, preferred_element_type=f32)
-    hidden_last = (mixed_last_ref[...] + moe_last).astype(bf16).astype(f32)
-    last_ref[...] = rms_scale(hidden_last, gain_ref[...]).astype(bf16)
     first = column_of(routes_ref[0:1, :].astype(f32)).astype(jnp.int32)
     second = column_of(routes_ref[1:2, :].astype(f32)).astype(jnp.int32)
     lane = lane_of((ROWS, LANES))
@@ -631,16 +611,19 @@
     ).astype(bf16)
     slots = jnp.dot(earlier, named, preferred_element_type=f32)
     column = lane_of((ROWS, count))
-    moe = None
-    for which, chosen in enumerate((first, second)):
+    picks = [pick_last]
+    for chosen in (first, second):
         slot = jnp.sum(jnp.where(chosen == lane, slots, 0.0), axis=1, keepdims=True)
         slot = slot.astype(jnp.int32)
         place = slot + jnp.where(slot >= PART_SLOTS, PART_ROWS - PART_SLOTS, 0)
         target = chosen[:, 0:1] * (2 * SLOT_ROWS) + place
         pick = ((column == target) | (column == target + SLOT_ROWS)).astype(f32).astype(bf16)
-        picked = jnp.dot(pick, got, preferred_element_type=f32)
-        term = column_of(gates_ref[which : which + 1, :])[:, 0:1] * picked
-        moe = term if moe is None else moe + term
+        picks.append(pick)
+    picked = jnp.dot(jnp.concatenate(picks, axis=0), got, preferred_element_type=f32)
+    hidden_last = (mixed_last_ref[...] + picked[:REQS]).astype(bf16).astype(f32)
+    last_ref[...] = rms_scale(hidden_last, gain_ref[...]).astype(bf16)
+    moe = column_of(gates_ref[0:1, :])[:, 0:1] * picked[REQS : REQS + ROWS]
+    moe = moe + column_of(gates_ref[1:2, :])[:, 0:1] * picked[REQS + ROWS :]
     hidden = (mixed_ref[...] + moe).astype(bf16)
     hidden_ref[...] = hidden
     wide = hidden.astype(f32)

time: 170 us -> 168 us (0.988)
  Pallas kernels: 42.7 us -> 38.9 us
    pallas_call x1, Pallas kernels: 6.58 us -> 4.87 us  [mix(): pl.pallas_call(mix_kernel, grid_spec=pltpu.PrefetchScalarGridSpec(num_sca...]
where the time goes in v6:
time: 168 us; the launch traced here: 167 us
  blocking collectives  76.7 us (46%)
  Pallas kernels  38.9 us (23%)
  starting transfers between devices  30.7 us (18%)
  waiting for transfers between devices  15.2 us (9%)
  local copies, waits for them, and re-layouts  2.1 us (1%)
    all_to_all x4, blocking collectives, exchange(): return lax.all_to_all(rows, 'blk', split_axis=0, concat_axis=0, tiled=True)  76.7 us
    all_to_all x2, starting transfers between devices, exchange(): return lax.all_to_all(rows, 'blk', split_axis=0, concat_axis=0, tiled=True)  15.9 us
    ppermute x7, waiting for transfers between devices, shift(): return lax.ppermute(one, 'grp', [(i, (i + by) % size) for i in range(size)])  11.2 us
    pallas_call x1, Pallas kernels, expert(): pl.pallas_call(expert_kernel, in_specs=[vmem] * 7, out_specs=pl.BlockSpec...  11.1 us
    ppermute x7, starting transfers between devices, shift(): return lax.ppermute(one, 'grp', [(i, (i + by) % size) for i in range(size)])  10.4 us
    pallas_call x1, Pallas kernels, suffix_attention(): pl.pallas_call(suffix_kernel, grid_spec=pltpu.PrefetchScalarGridSpec(num_...  8.91 us
    pallas_call x1, Pallas kernels, prefix_attention(): pl.pallas_call(prefix_kernel, grid_spec=pltpu.PrefetchScalarGridSpec(num_...  5.38 us
    pallas_call x1, Pallas kernels, mix(): pl.pallas_call(mix_kernel, grid_spec=pltpu.PrefetchScalarGridSpec(num_sca...  4.87 us
  transfers between devices with their start and end apart: 12, of which 7 were waited for; matrix products, arithmetic and copies ran while one was open for 0% of the time, Pallas kernels for 5%

profile of v6, /device:TPU:1, one launch (start us, length us, event | category | flops | bytes accessed | tf_op | source)
XLA Modules:
  0.0 167.0 jit_solution(9031110222717083512)
XLA Ops:
  0.7 0.8 copy-done.9
  1.5 4.3 %project.1 = (bf16[128,1024]{1,0:T(8,128)(2,1)}, bf16[8,4,176,128]{3,2,1,0:T(8,128)(2,1)}) custom-call(s32[1]{0:T(128)} %bitcast.block_ref, s32[16]{0:T(128)S(1)} %bitcast.59, bf16[128,1024]{1,0:T(8,128)(2,1)} %bitcast.53, f32[1,1024]{1,0:T(1,128)} %bitcast.72, bf16[1024,512]{1,0:T(8,128)(2,1)} %wq_ref.1, bf16[1024,1024]{1,0:T(8,128)(2,1)} %wv_ref.1, ...), custom_call_target="tpu_custom_call" | custom-call | tf_op jit(solution)/shard_map/project/pallas_call | solution.py:131
  5.8 8.6 %all-to-all-start = ((bf16[32,176,128]{2,1,0:T(8,128)(2,1)}), bf16[32,176,128]{2,1,0:T(8,128)(2,1)}, u32[]{:S(2)}, u32[]{:S(2)}) async-start(bf16[32,176,128]{2,1,0:T(8,128)(2,1)} %bitcast.8), calls=%async_computation | async-start | bytes 2883584 | tf_op jit(solution)/shard_map/qkv_exchange/all_to_all | solution.py:663
  14.4 5.7 %collective-permute-start.4 = (bf16[64,1024]{1,0:T(8,128)(2,1)}, bf16[64,1024]{1,0:T(8,128)(2,1)}, u32[]{:S(2)}, u32[]{:S(2)}) collective-permute-start(bf16[64,1024]{1,0:T(8,128)(2,1)} %bitcast.10.refs_0_), channel_id=1, source_target_pairs={{0,224},{32,0},{64,32},{96,64},{128,96},{160,128},{192,160},{224,1... | collective-permute-start | bytes 393224 | tf_op jit(solution)/shard_map/prefix_gather/ppermute | solution.py:670
  20.1 2.9 %collective-permute-done.4.refs_7_ = bf16[64,1024]{1,0:T(8,128)(2,1)} collective-permute-done((bf16[64,1024]{1,0:T(8,128)(2,1)}, bf16[64,1024]{1,0:T(8,128)(2,1)}, u32[]{:S(2)}, u32[]{:S(2)}) %collective-permute-start.4) | collective-permute-done | bytes 131104 | tf_op jit(solution)/shard_map/prefix_gather/ppermute | solution.py:670
  23.0 3.4 %collective-permute-start.6 = (bf16[64,1024]{1,0:T(8,128)(2,1)}, bf16[64,1024]{1,0:T(8,128)(2,1)}, u32[]{:S(2)}, u32[]{:S(2)}) collective-permute-start(bf16[64,1024]{1,0:T(8,128)(2,1)} %collective-permute-done.4.refs_7_), channel_id=1, source_target_pairs={{0,224},{32,0},{64,32},{96,64},{128,96},{160,128},{192,160},{224,1... | collective-permute-start | bytes 393224 | tf_op jit(solution)/shard_map/prefix_gather/ppermute | solution.py:670
  26.4 1.3 collective-permute-done.1.refs_2_
  27.7 1.1 collective-permute-start.3
  28.8 0.2 collective-permute-start.2
  29.7 0.7 collective-permute-done.6.refs_6_
  30.4 4.2 %collective-permute-done.5.refs_5_ = bf16[64,1024]{1,0:T(8,128)(2,1)} collective-permute-done((bf16[64,1024]{1,0:T(8,128)(2,1)}, bf16[64,1024]{1,0:T(8,128)(2,1)}, u32[]{:S(2)}, u32[]{:S(2)}) %collective-permute-start.5) | collective-permute-done | bytes 131104 | tf_op jit(solution)/shard_map/prefix_gather/ppermute | solution.py:670
  34.6 0.5 collective-permute-done.3.refs_4_
  35.1 1.6 collective-permute-done.2.refs_3_
  36.7 2.0 %prefix_pack.1 = bf16[8,4,80,128]{3,2,1,0:T(8,128)(2,1)} custom-call(s32[1]{0:T(128)S(6)} %select_n.12.offset_ref, bf16[32,176,128]{2,1,0:T(8,128)(2,1)} %all-to-all-done.got_ref.query_ref.gate_last_ref, bf16[64,1024]{1,0:T(8,128)(2,1)} %bitcast.10.refs_0_, bf16[64,1024]{1,0:T(8,128)(2,1)} %collective-permute-done.refs_1_, ...), custom_call_target="tpu_custom_call" | custom-call | tf_op jit(solution)/shard_map/prefix_pack/pallas_call | solution.py:193
  38.6 4.0 %collective-permute-start.7 = (bf16[704,1024]{1,0:T(8,128)(2,1)S(1)}, bf16[704,1024]{1,0:T(8,128)(2,1)}, u32[]{:S(2)}, u32[]{:S(2)}) collective-permute-start(bf16[704,1024]{1,0:T(8,128)(2,1)S(1)} %bitcast.44), channel_id=1, source_target_pairs={{0,1},{1,0},{2,3},{3,2},{4,5},{5,4},{6,7},{7,6},{8,9},{9,8},{10,11... | collective-permute-start | bytes 4325384 | tf_op jit(solution)/shard_map/weight_swap/ppermute | solution.py:721
  42.6 0.1 collective-permute-start.8
  42.7 0.4 collective-permute-start.9
  43.1 7.2 %all-to-all-start.1 = ((bf16[32,80,128]{2,1,0:T(8,128)(2,1)}), bf16[32,80,128]{2,1,0:T(8,128)(2,1)}, u32[]{:S(2)}, u32[]{:S(2)}) async-start(bf16[32,80,128]{2,1,0:T(8,128)(2,1)} %bitcast.69), calls=%async_computation.1 | async-start | bytes 1310720 | tf_op jit(solution)/shard_map/prefix_exchange/all_to_all | solution.py:663
  50.4 8.9 %suffix_attention.1.part_ref = f32[1024,128]{1,0:T(8,128)} custom-call(s32[1]{0:T(128)S(6)} %select_n.11.quarter_ref, s32[16]{0:T(128)S(1)} %bitcast.60, bf16[32,176,128]{2,1,0:T(8,128)(2,1)} %all-to-all-done.got_ref.query_ref.gate_last_ref, bf16[32,176,128]{2,1,0:T(8,128)(2,1)} %all-to-all-done.got_ref.query_ref.gate_last_ref), custom_call_target="tpu_custom_call" | custom-call | tf_op jit(solution)/shard_map/suffix_attention/pallas_call | solution.py:283
  59.3 4.0 %all-to-all-done.1.keys_ref.tok_last_ref = bf16[32,80,128]{2,1,0:T(8,128)(2,1)} async-done(((bf16[32,80,128]{2,1,0:T(8,128)(2,1)}), bf16[32,80,128]{2,1,0:T(8,128)(2,1)}, u32[]{:S(2)}, u32[]{:S(2)}) %all-to-all-start.1) | async-done | bytes 655392 | tf_op jit(solution)/shard_map/prefix_exchange/all_to_all | solution.py:663
  63.4 5.4 %prefix_attention.1 = bf16[32,32,128]{2,1,0:T(8,128)(2,1)S(1)} custom-call(s32[1]{0:T(128)S(6)} %select_n.11.quarter_ref, s32[16]{0:T(128)S(1)} %bitcast.61, bf16[32,176,128]{2,1,0:T(8,128)(2,1)} %all-to-all-done.got_ref.query_ref.gate_last_ref, bf16[32,80,128]{2,1,0:T(8,128)(2,1)} %all-to-all-done.1.keys_ref.tok_last_ref, f32[1024,128]{1,0:T(8,128)} %suffix_attention.1.part_ref), custom_call_target="tpu_custom_call" | custom-call | tf_op jit(solution)/shard_map/prefix_attention/pallas_call | solution.py:375
  68.7 13.0 %all_to_all.30 = bf16[32,32,128]{2,1,0:T(8,128)(2,1)S(1)} all-to-all(bf16[32,32,128]{2,1,0:T(8,128)(2,1)S(1)} %prefix_attention.1), channel_id=1, replica_groups=mesh['grp'=8,'blk'=32] {'blk'}, dimensions={0} | all-to-all | bytes 524288 | tf_op jit(solution)/shard_map/context_exchange/all_to_all | solution.py:663
  81.7 1.2 copy-done.4
  83.0 4.9 %mix.1 = (f32[128,1024]{1,0:T(8,128)}, f32[16,1024]{1,0:T(8,128)}, bf16[768,1024]{1,0:T(8,128)(2,1)}) custom-call(s32[1]{0:T(128)} %bitcast.block_ref, bf16[8,4,32,128]{3,2,1,0:T(8,128)(2,1)S(1)} %bitcast.55, bf16[128,1024]{1,0:T(8,128)(2,1)S(1)} %bitcast.54, bf16[32,80,128]{2,1,0:T(8,128)(2,1)} %all-to-all-done.1.keys_ref.tok_last_ref, ...), custom_call_target="tpu_custom_call" | custom-call | tf_op jit(solution)/shard_map/mix/pallas_call | solution.py:484
  87.8 26.8 %all_to_all.31 = bf16[32,24,1024]{2,1,0:T(8,128)(2,1)S(1)} all-to-all(bf16[32,24,1024]{2,1,0:T(8,128)(2,1)} %bitcast.70), channel_id=1, replica_groups=mesh['grp'=8,'blk'=32] {'blk'}, dimensions={0} | all-to-all | bytes 3145728 | tf_op jit(solution)/shard_map/dispatch_exchange/all_to_all | solution.py:663
  114.6 11.1 %expert.1 = bf16[768,1024]{1,0:T(8,128)(2,1)} custom-call(bf16[768,1024]{1,0:T(8,128)(2,1)S(1)} %bitcast.43, bf16[704,1024]{1,0:T(8,128)(2,1)S(1)} %bitcast.46, bf16[704,1024]{1,0:T(8,128)(2,1)S(1)} %bitcast.49, bf16[704,1024]{1,0:T(8,128)(2,1)S(1)} %bitcast.52, bf16[704,1024]{1,0:T(8,128)(2,1)} %collective-permute-done.7.g1, ...), custom_call_target="tpu_custom_call" | custom-call | tf_op jit(solution)/shard_map/expert/pallas_call | solution.py:575
  125.8 26.6 %all_to_all.32 = bf16[32,24,1024]{2,1,0:T(8,128)(2,1)S(1)} all-to-all(bf16[32,24,1024]{2,1,0:T(8,128)(2,1)} %bitcast.68), channel_id=1, replica_groups=mesh['grp'=8,'blk'=32] {'blk'}, dimensions={0} | all-to-all | bytes 3145728 | tf_op jit(solution)/shard_map/return_exchange/all_to_all | solution.py:663
  152.4 2.3 %combine.1 = (bf16[128,1024]{1,0:T(8,128)(2,1)}, bf16[16,1024]{1,0:T(8,128)(2,1)S(1)}, f32[1,128]{1,0:T(1,128)S(1)}) custom-call(s32[1]{0:T(128)} %bitcast.block_ref, s32[16]{0:T(128)S(1)} %bitcast.62, f32[128,1024]{1,0:T(8,128)S(1)} %copy-done.6, f32[16,1024]{1,0:T(8,128)S(1)} %copy-done.7, bf16[768,1024]{1,0:T(8,128)(2,1)S(1)} %bitcast.42, ...), custom_call_target="tpu_custom_call" | custom-call | tf_op jit(solution)/shard_map/combine/pallas_call | solution.py:648
  154.7 0.8 convolution_reduce_fusion
  155.6 10.4 %all_to_all.33 = f32[32,1,128]{2,1,0:T(1,128)S(1)} all-to-all(f32[32,1,128]{2,1,0:T(1,128)S(1)} %broadcast_in_dim.25), channel_id=1, replica_groups=mesh['grp'=8,'blk'=32] {'blk'}, dimensions={0} | all-to-all | bytes 32768 | tf_op jit(solution)/shard_map/final_exchange/all_to_all | solution.py:663
  165.9 0.6 slice_reduce_fusion
  166.5 0.5 fusion.1
  (36 shorter events, 0.2 us)
Async XLA Ops:
  0.6 154.1 %copy-start = (bf16[1024,1004]{0,1:T(8,128)(2,1)S(1)}, bf16[1024,1004]{0,1:T(8,128)(2,1)}, u32[]{:S(2)}) copy-start(bf16[1024,1004]{0,1:T(8,128)(2,1)} %param.31) | copy-start | bytes 6168580
  0.7 0.8 copy-start.9
  5.8 30.9 %all-to-all-start = ((bf16[32,176,128]{2,1,0:T(8,128)(2,1)}), bf16[32,176,128]{2,1,0:T(8,128)(2,1)}, u32[]{:S(2)}, u32[]{:S(2)}) async-start(bf16[32,176,128]{2,1,0:T(8,128)(2,1)} %bitcast.8), calls=%async_computation | async-start | bytes 2883584 | tf_op jit(solution)/shard_map/qkv_exchange/all_to_all | solution.py:663
  14.4 8.6 %collective-permute-start.4 = (bf16[64,1024]{1,0:T(8,128)(2,1)}, bf16[64,1024]{1,0:T(8,128)(2,1)}, u32[]{:S(2)}, u32[]{:S(2)}) collective-permute-start(bf16[64,1024]{1,0:T(8,128)(2,1)} %bitcast.10.refs_0_), channel_id=1, source_target_pairs={{0,224},{32,0},{64,32},{96,64},{128,96},{160,128},{192,160},{224,1... | collective-permute-start | bytes 393224 | tf_op jit(solution)/shard_map/prefix_gather/ppermute | solution.py:670
  20.1 7.6 %collective-permute-start.1 = (bf16[64,1024]{1,0:T(8,128)(2,1)}, bf16[64,1024]{1,0:T(8,128)(2,1)}, u32[]{:S(2)}, u32[]{:S(2)}) collective-permute-start(bf16[64,1024]{1,0:T(8,128)(2,1)} %bitcast.10.refs_0_), channel_id=1, source_target_pairs={{0,64},{32,96},{64,128},{96,160},{128,192},{160,224},{192,0},{224,... | collective-permute-start | bytes 393224 | tf_op jit(solution)/shard_map/prefix_gather/ppermute | solution.py:670
  20.1 9.6 %collective-permute-start = (bf16[64,1024]{1,0:T(8,128)(2,1)}, bf16[64,1024]{1,0:T(8,128)(2,1)}, u32[]{:S(2)}, u32[]{:S(2)}) collective-permute-start(bf16[64,1024]{1,0:T(8,128)(2,1)} %bitcast.10.refs_0_), channel_id=1, source_target_pairs={{0,32},{32,64},{64,96},{96,128},{128,160},{160,192},{192,224},{224... | collective-permute-start | bytes 393224 | tf_op jit(solution)/shard_map/prefix_gather/ppermute | solution.py:670
  23.0 7.4 %collective-permute-start.6 = (bf16[64,1024]{1,0:T(8,128)(2,1)}, bf16[64,1024]{1,0:T(8,128)(2,1)}, u32[]{:S(2)}, u32[]{:S(2)}) collective-permute-start(bf16[64,1024]{1,0:T(8,128)(2,1)} %collective-permute-done.4.refs_7_), channel_id=1, source_target_pairs={{0,224},{32,0},{64,32},{96,64},{128,96},{160,128},{192,160},{224,1... | collective-permute-start | bytes 393224 | tf_op jit(solution)/shard_map/prefix_gather/ppermute | solution.py:670
  26.4 8.2 %collective-permute-start.5 = (bf16[64,1024]{1,0:T(8,128)(2,1)}, bf16[64,1024]{1,0:T(8,128)(2,1)}, u32[]{:S(2)}, u32[]{:S(2)}) collective-permute-start(bf16[64,1024]{1,0:T(8,128)(2,1)} %collective-permute-done.4.refs_7_), channel_id=1, source_target_pairs={{0,192},{32,224},{64,0},{96,32},{128,64},{160,96},{192,128},{224,1... | collective-permute-start | bytes 393224 | tf_op jit(solution)/shard_map/prefix_gather/ppermute | solution.py:670
  27.7 7.4 %collective-permute-start.3 = (bf16[64,1024]{1,0:T(8,128)(2,1)}, bf16[64,1024]{1,0:T(8,128)(2,1)}, u32[]{:S(2)}, u32[]{:S(2)}) collective-permute-start(bf16[64,1024]{1,0:T(8,128)(2,1)} %collective-permute-done.1.refs_2_), channel_id=1, source_target_pairs={{0,64},{32,96},{64,128},{96,160},{128,192},{160,224},{192,0},{224,... | collective-permute-start | bytes 393224 | tf_op jit(solution)/shard_map/prefix_gather/ppermute | solution.py:670
  28.8 7.8 %collective-permute-start.2 = (bf16[64,1024]{1,0:T(8,128)(2,1)}, bf16[64,1024]{1,0:T(8,128)(2,1)}, u32[]{:S(2)}, u32[]{:S(2)}) collective-permute-start(bf16[64,1024]{1,0:T(8,128)(2,1)} %collective-permute-done.1.refs_2_), channel_id=1, source_target_pairs={{0,32},{32,64},{64,96},{96,128},{128,160},{160,192},{192,224},{224... | collective-permute-start | bytes 393224 | tf_op jit(solution)/shard_map/prefix_gather/ppermute | solution.py:670
  29.7 9.0 %copy-start.1 = (bf16[1,1024,704]{1,2,0:T(8,128)(2,1)S(1)}, bf16[1,1024,704]{1,2,0:T(8,128)(2,1)}, u32[]{:S(2)}) copy-start(bf16[1,1024,704]{1,2,0:T(8,128)(2,1)} %param.27) | copy-start | bytes 4325380
  29.7 20.7 %copy-start.10 = (s32[1,16]{1,0:T(1,128)S(1)}, s32[1,16]{1,0:T(1,128)}, u32[]{:S(2)}) copy-start(s32[1,16]{1,0:T(1,128)} %param.17) | copy-start | bytes 196
  38.6 20.7 %collective-permute-start.7 = (bf16[704,1024]{1,0:T(8,128)(2,1)S(1)}, bf16[704,1024]{1,0:T(8,128)(2,1)}, u32[]{:S(2)}, u32[]{:S(2)}) collective-permute-start(bf16[704,1024]{1,0:T(8,128)(2,1)S(1)} %bitcast.44), channel_id=1, source_target_pairs={{0,1},{1,0},{2,3},{3,2},{4,5},{5,4},{6,7},{7,6},{8,9},{9,8},{10,11... | collective-permute-start | bytes 4325384 | tf_op jit(solution)/shard_map/weight_swap/ppermute | solution.py:721
  42.6 16.7 %collective-permute-start.8 = (bf16[704,1024]{1,0:T(8,128)(2,1)}, bf16[704,1024]{1,0:T(8,128)(2,1)}, u32[]{:S(2)}, u32[]{:S(2)}) collective-permute-start(bf16[704,1024]{1,0:T(8,128)(2,1)} %bitcast.47), channel_id=1, source_target_pairs={{0,1},{1,0},{2,3},{3,2},{4,5},{5,4},{6,7},{7,6},{8,9},{9,8},{10,11... | collective-permute-start | bytes 4325384 | tf_op jit(solution)/shard_map/weight_swap/ppermute | solution.py:721
  42.7 16.6 %collective-permute-start.9 = (bf16[704,1024]{1,0:T(8,128)(2,1)}, bf16[704,1024]{1,0:T(8,128)(2,1)}, u32[]{:S(2)}, u32[]{:S(2)}) collective-permute-start(bf16[704,1024]{1,0:T(8,128)(2,1)} %bitcast.50), channel_id=1, source_target_pairs={{0,1},{1,0},{2,3},{3,2},{4,5},{5,4},{6,7},{7,6},{8,9},{9,8},{10,11... | collective-permute-start | bytes 4325384 | tf_op jit(solution)/shard_map/weight_swap/ppermute | solution.py:721
  43.1 20.2 %all-to-all-start.1 = ((bf16[32,80,128]{2,1,0:T(8,128)(2,1)}), bf16[32,80,128]{2,1,0:T(8,128)(2,1)}, u32[]{:S(2)}, u32[]{:S(2)}) async-start(bf16[32,80,128]{2,1,0:T(8,128)(2,1)} %bitcast.69), calls=%async_computation.1 | async-start | bytes 1310720 | tf_op jit(solution)/shard_map/prefix_exchange/all_to_all | solution.py:663
  59.3 22.4 %copy-start.8 = (s32[1,128,2]{1,2,0:T(2,128)S(1)}, s32[1,128,2]{1,2,0:T(2,128)}, u32[]{:S(2)}) copy-start(s32[1,128,2]{1,2,0:T(2,128)} %param.20) | copy-start | bytes 3076
  59.3 22.4 %copy-start.11 = (f32[1024]{0:T(1024)S(1)}, f32[1024]{0:T(1024)}, u32[]{:S(2)}) copy-start(f32[1024]{0:T(1024)} %param.26) | copy-start | bytes 12292
  63.3 18.4 %copy-start.2 = (bf16[1,1024,704]{1,2,0:T(8,128)(2,1)S(1)}, bf16[1,1024,704]{1,2,0:T(8,128)(2,1)}, u32[]{:S(2)}) copy-start(bf16[1,1024,704]{1,2,0:T(8,128)(2,1)} %param.28) | copy-start | bytes 4325380
  63.4 18.4 %copy-start.3 = (bf16[1,704,1024]{2,1,0:T(8,128)(2,1)S(1)}, bf16[1,704,1024]{2,1,0:T(8,128)(2,1)}, u32[]{:S(2)}) copy-start(bf16[1,704,1024]{2,1,0:T(8,128)(2,1)} %param.29) | copy-start | bytes 4325380
  63.4 18.4 %copy-start.5 = (bf16[1,128,1024]{2,1,0:T(8,128)(2,1)S(1)}, bf16[1,128,1024]{2,1,0:T(8,128)(2,1)}, u32[]{:S(2)}) copy-start(bf16[1,128,1024]{2,1,0:T(8,128)(2,1)} %param.16) | copy-start | bytes 786436
  81.7 1.2 copy-start.4
  125.7 26.6 %copy-start.6 = (f32[128,1024]{1,0:T(8,128)S(1)}, f32[128,1024]{1,0:T(8,128)}, u32[]{:S(2)}) copy-start(f32[128,1024]{1,0:T(8,128)} %get-tuple-element.26.mixed_ref) | copy-start | bytes 1572868
  125.7 26.6 %copy-start.7 = (f32[16,1024]{1,0:T(8,128)S(1)}, f32[16,1024]{1,0:T(8,128)}, u32[]{:S(2)}) copy-start(f32[16,1024]{1,0:T(8,128)} %get-tuple-element.27.mixed_last_ref) | copy-start | bytes 196612
  125.8 26.6 %copy-start.12 = (f32[1024]{0:T(1024)S(1)}, f32[1024]{0:T(1024)}, u32[]{:S(2)}) copy-start(f32[1024]{0:T(1024)} %param.30) | copy-start | bytes 12292
  125.8 26.6 %copy-start.13 = (f32[1,128,2]{1,2,0:T(2,128)S(1)}, f32[1,128,2]{1,2,0:T(2,128)}, u32[]{:S(2)}) copy-start(f32[1,128,2]{1,2,0:T(2,128)} %param.21) | copy-start | bytes 3076

commit v7 on v6

--- a/solution.py
+++ b/solution.py
@@ -154,7 +154,7 @@
         ],
         compiler_params=pltpu.CompilerParams(vmem_limit_bytes=24 << 20),
         name="project",
-    )(block, lengths, *in_hbm(stream, gain, w_query, w_keyval, w_keyval, routes_t, gates_t))
+    )(block, *in_hbm(lengths, stream, gain, w_query, w_keyval, w_keyval, routes_t, gates_t))
 
 
 def prefix_pack_kernel(offset_ref, got_ref, *refs):
@@ -403,8 +403,10 @@
 
 def mix_kernel(
     block_ref, ctx_ref, tok_ref, tok_last_ref, gate_last_ref, wout_ref, gain_ref, routes_ref, g_ref, u_ref, d_ref,
-    mixed_ref, mixed_last_ref, send_ref, send_v, out_sems,
+    mixed_ref, mixed_last_ref, send_ref, wout_v, send_v, wout_sem, out_sems,
 ):
+    lift_copy = pltpu.make_async_copy(wout_ref, wout_v, wout_sem)
+    lift_copy.start()
     tiles = []
     for pair in range(HEADS // 2):
         even = ctx_ref[2 * pair].astype(f32)
@@ -417,7 +419,8 @@
         ends = jnp.where(low, pltpu.roll(even_last, HALF, 1), odd_last)
         tiles.append(jnp.concatenate([both, ends], axis=0).astype(bf16))
     context = jnp.concatenate(tiles, axis=1)
-    lift = jnp.dot(context, wout_ref[...], preferred_element_type=f32)
+    lift_copy.wait()
+    lift = jnp.dot(context, wout_v[...], preferred_element_type=f32)
     mixed = tok_ref[...].astype(f32) + lift[:ROWS]
     mixed_ref[...] = mixed
     routed = rms_scale(mixed, gain_ref[...]).astype(bf16)
@@ -491,7 +494,7 @@
                 whole(stream.shape),
                 pl.BlockSpec((blocks, REQS, LANES), lambda i, b: (0, 4, 0)),
                 pl.BlockSpec((blocks, REQS, LANES), lambda i, b: (0, 10, 0)),
-                whole(w_out.shape),
+                pl.BlockSpec(memory_space=pl.ANY),
                 whole(gain.shape),
                 whole(routes_t.shape),
                 whole((units, width)),
@@ -504,7 +507,9 @@
                 pl.BlockSpec(memory_space=pltpu.HBM),
             ],
             scratch_shapes=[
+                pltpu.VMEM(w_out.shape, bf16),
                 pltpu.VMEM((MIX_PARTS, 2 * EXPERTS * SLOT_ROWS // MIX_PARTS, width), bf16),
+                pltpu.SemaphoreType.DMA(()),
                 pltpu.SemaphoreType.DMA((MIX_PARTS,)),
             ],
         ),
@@ -515,7 +520,7 @@
         ],
         compiler_params=pltpu.CompilerParams(vmem_limit_bytes=18 << 20),
         name="mix",
-    )(block, ctx, stream, *in_hbm(prefix_got, got), w_out, gain, routes_t, *own)
+    )(block, ctx, stream, *in_hbm(prefix_got, got, w_out), gain, routes_t, *own)
 
 
 FFN_TILE = 256
@@ -593,7 +598,7 @@
 
 def combine_kernel(
     block_ref, lengths_ref, mixed_ref, mixed_last_ref, got_ref, routes_ref, gates_ref, gain_ref,
-    hidden_ref, last_ref, norm_ref,
+    unembed_ref, hidden_ref, packet_ref,
 ):
     got = got_ref[...]
     count = got.shape[0]
@@ -621,7 +626,11 @@
         picks.append(pick)
     picked = jnp.dot(jnp.concatenate(picks, axis=0), got, preferred_element_type=f32)
     hidden_last = (mixed_last_ref[...] + picked[:REQS]).astype(bf16).astype(f32)
-    last_ref[...] = rms_scale(hidden_last, gain_ref[...]).astype(bf16)
+    last_rows = rms_scale(hidden_last, gain_ref[...]).astype(bf16)
+    best = jnp.max(dot_nt(last_rows, unembed_ref[...]), axis=1, keepdims=True)
+    request = lax.broadcasted_iota(jnp.int32, (REQS, LANES), 0)
+    best = jnp.where(lane_of((REQS, LANES)) == request + REQS, best, 0.0)
+    best = jnp.sum(best, axis=0, keepdims=True)
     moe = column_of(gates_ref[0:1, :])[:, 0:1] * picked[REQS : REQS + ROWS]
     moe = moe + column_of(gates_ref[1:2, :])[:, 0:1] * picked[REQS + ROWS :]
     hidden = (mixed_ref[...] + moe).astype(bf16)
@@ -638,25 +647,24 @@
         end = end + lengths_ref[r]
         ends = jnp.where(lane_row == r, end, ends)
     member = (position >= starts) & (position < ends)
-    norm_ref[...] = jnp.sum(jnp.where(member, squares, 0.0), axis=0, keepdims=True)
-
-
-def combine(block, lengths, mixed, mixed_last, got, routes, gates, gain):
+    packet_ref[...] = best + jnp.sum(jnp.where(member, squares, 0.0), axis=0, keepdims=True)
+
+
+def combine(block, lengths, mixed, mixed_last, got, routes, gates, gain, unembed):
     width = mixed.shape[1]
     vmem = pl.BlockSpec(memory_space=pltpu.VMEM)
     smem = pl.BlockSpec(memory_space=pltpu.SMEM)
     return pl.pallas_call(
         combine_kernel,
-        in_specs=[smem, smem] + [vmem] * 6,
-        out_specs=[vmem] * 3,
+        in_specs=[smem, smem] + [vmem] * 7,
+        out_specs=[vmem] * 2,
         out_shape=[
             jax.ShapeDtypeStruct((ROWS, width), bf16),
-            jax.ShapeDtypeStruct((REQS, width), bf16),
             jax.ShapeDtypeStruct((1, LANES), f32),
         ],
         compiler_params=pltpu.CompilerParams(vmem_limit_bytes=16 << 20),
         name="combine",
-    )(block, lengths, mixed, mixed_last, got, routes, gates, gain)
+    )(block, lengths, mixed, mixed_last, got, routes, gates, gain, unembed)
 
 
 def exchange(rows):
@@ -734,15 +742,19 @@
     results = expert(rows.reshape(-1, width), own, other)
     with jax.named_scope("return_exchange"):
         returned = exchange(results.reshape(blocks, PART_ROWS, width)).reshape(-1, width)
-    hidden, last_rows, norm_terms = combine(
-        block, lengths[0], mixed, mixed_last, returned, routes_t, gates_t, final_gain.reshape(1, -1)
-    )
-    logits = jnp.dot(last_rows, unembed, preferred_element_type=f32)
-    best = jnp.max(logits, axis=1)
+    hidden, packet = combine(
+        block,
+        lengths[0],
+        mixed,
+        mixed_last,
+        returned,
+        routes_t,
+        gates_t,
+        final_gain.reshape(1, -1),
+        unembed.T,
+    )
     with jax.named_scope("final_exchange"):
-        final = jnp.concatenate([norm_terms[:, :REQS], best[None, :]], axis=1)
-        final = jnp.pad(final, ((0, 0), (0, LANES - 2 * REQS)))
-        final = exchange(jnp.broadcast_to(final[None], (blocks, 1, LANES)))[:, 0, :]
+        final = exchange(jnp.broadcast_to(packet[None], (blocks, 1, LANES)))[:, 0, :]
     norm_sums = jnp.sum(final[:, :REQS], axis=0)
     greatest = jnp.max(final[:, REQS : 2 * REQS], axis=0)
     request_norm = jnp.sqrt(norm_sums / (lengths[0].astype(f32) * width))

time: 168 us -> 166 us (0.988)
  local copies, waits for them, and re-layouts: 2.1 us -> 0.09 us
    unnamed x28 -> x34, local copies, waits for them, and re-layouts: 2.08 us -> 0.08 us
where the time goes in v7:
time: 166 us; the launch traced here: 165 us
  blocking collectives  76.7 us (46%)
  Pallas kernels  40 us (24%)
  starting transfers between devices  31.2 us (19%)
  waiting for transfers between devices  14.7 us (9%)
    all_to_all x4, blocking collectives, exchange(): return lax.all_to_all(rows, 'blk', split_axis=0, concat_axis=0, tiled=True)  76.7 us
    all_to_all x2, starting transfers between devices, exchange(): return lax.all_to_all(rows, 'blk', split_axis=0, concat_axis=0, tiled=True)  16 us
    pallas_call x1, Pallas kernels, expert(): pl.pallas_call(expert_kernel, in_specs=[vmem] * 7, out_specs=pl.BlockSpec...  11 us
    ppermute x7, waiting for transfers between devices, shift(): return lax.ppermute(one, 'grp', [(i, (i + by) % size) for i in range(size)])  10.6 us
    ppermute x7, starting transfers between devices, shift(): return lax.ppermute(one, 'grp', [(i, (i + by) % size) for i in range(size)])  10.4 us
    pallas_call x1, Pallas kernels, suffix_attention(): pl.pallas_call(suffix_kernel, grid_spec=pltpu.PrefetchScalarGridSpec(num_...  8.89 us
    pallas_call x1, Pallas kernels, mix(): pl.pallas_call(mix_kernel, grid_spec=pltpu.PrefetchScalarGridSpec(num_sca...  6.09 us
    pallas_call x1, Pallas kernels, prefix_attention(): pl.pallas_call(prefix_kernel, grid_spec=pltpu.PrefetchScalarGridSpec(num_...  5.13 us
  transfers between devices with their start and end apart: 12, of which 7 were waited for; matrix products, arithmetic and copies ran while one was open for 0% of the time, Pallas kernels for 5%

profile of v7, /device:TPU:1, one launch (start us, length us, event | category | flops | bytes accessed | tf_op | source)
XLA Modules:
  0.0 165.3 jit_solution(1890559415788849348)
XLA Ops:
  0.6 4.4 %project.1 = (bf16[128,1024]{1,0:T(8,128)(2,1)}, bf16[8,4,176,128]{3,2,1,0:T(8,128)(2,1)}) custom-call(s32[1]{0:T(128)} %bitcast.block_ref, s32[16]{0:T(128)} %bitcast.56, bf16[128,1024]{1,0:T(8,128)(2,1)} %bitcast.50, f32[1,1024]{1,0:T(1,128)} %bitcast.73, bf16[1024,512]{1,0:T(8,128)(2,1)} %wq_ref.1, bf16[1024,1024]{1,0:T(8,128)(2,1)} %wv_ref.1, ...), custom_call_target="tpu_custom_call" | custom-call | tf_op jit(solution)/shard_map/project/pallas_call | solution.py:131
  5.1 8.8 %all-to-all-start = ((bf16[32,176,128]{2,1,0:T(8,128)(2,1)}), bf16[32,176,128]{2,1,0:T(8,128)(2,1)}, u32[]{:S(2)}, u32[]{:S(2)}) async-start(bf16[32,176,128]{2,1,0:T(8,128)(2,1)} %bitcast.8), calls=%async_computation | async-start | bytes 2883584 | tf_op jit(solution)/shard_map/qkv_exchange/all_to_all | solution.py:671
  13.9 5.7 %collective-permute-start.4 = (bf16[64,1024]{1,0:T(8,128)(2,1)S(1)}, bf16[64,1024]{1,0:T(8,128)(2,1)S(1)}, u32[]{:S(2)}, u32[]{:S(2)}) collective-permute-start(bf16[64,1024]{1,0:T(8,128)(2,1)S(1)} %bitcast.70), channel_id=1, source_target_pairs={{0,224},{32,0},{64,32},{96,64},{128,96},{160,128},{192,160},{224,1... | collective-permute-start | bytes 393224 | tf_op jit(solution)/shard_map/prefix_gather/ppermute | solution.py:678
  19.5 2.6 %collective-permute-done.4.refs_7_ = bf16[64,1024]{1,0:T(8,128)(2,1)S(1)} collective-permute-done((bf16[64,1024]{1,0:T(8,128)(2,1)S(1)}, bf16[64,1024]{1,0:T(8,128)(2,1)S(1)}, u32[]{:S(2)}, u32[]{:S(2)}) %collective-permute-start.4) | collective-permute-done | bytes 131104 | tf_op jit(solution)/shard_map/prefix_gather/ppermute | solution.py:678
  22.1 3.5 %collective-permute-start.6 = (bf16[64,1024]{1,0:T(8,128)(2,1)S(1)}, bf16[64,1024]{1,0:T(8,128)(2,1)S(1)}, u32[]{:S(2)}, u32[]{:S(2)}) collective-permute-start(bf16[64,1024]{1,0:T(8,128)(2,1)S(1)} %collective-permute-done.4.refs_7_), channel_id=1, source_target_pairs={{0,224},{32,0},{64,32},{96,64},{128,96},{160,128},{192,160},{224,1... | collective-permute-start | bytes 393224 | tf_op jit(solution)/shard_map/prefix_gather/ppermute | solution.py:678
  25.6 1.3 collective-permute-done.1.refs_2_
  26.9 1.1 collective-permute-start.3
  28.1 0.1 collective-permute-start.2
  28.8 0.0 copy-start.1
  28.8 0.0 copy-start.8
  28.9 0.8 collective-permute-done.6.refs_6_
  29.7 4.0 %collective-permute-done.5.refs_5_ = bf16[64,1024]{1,0:T(8,128)(2,1)} collective-permute-done((bf16[64,1024]{1,0:T(8,128)(2,1)S(1)}, bf16[64,1024]{1,0:T(8,128)(2,1)}, u32[]{:S(2)}, u32[]{:S(2)}) %collective-permute-start.5) | collective-permute-done | bytes 131104 | tf_op jit(solution)/shard_map/prefix_gather/ppermute | solution.py:678
  33.7 0.7 collective-permute-done.3.refs_4_
  34.4 1.3 collective-permute-done.2.refs_3_
  35.7 1.9 %prefix_pack.1 = bf16[8,4,80,128]{3,2,1,0:T(8,128)(2,1)} custom-call(s32[1]{0:T(128)S(6)} %select_n.12.offset_ref, bf16[32,176,128]{2,1,0:T(8,128)(2,1)} %all-to-all-done.got_ref.query_ref.gate_last_ref, bf16[64,1024]{1,0:T(8,128)(2,1)} %bitcast.69, bf16[64,1024]{1,0:T(8,128)(2,1)} %copy-done.15, bf16[64,1024]{1,0:T(8,128)(2,1)} %copy-done.14, ...), custom_call_target="tpu_custom_call" | custom-call | tf_op jit(solution)/shard_map/prefix_pack/pallas_call | solution.py:193
  37.6 4.2 %collective-permute-start.7 = (bf16[704,1024]{1,0:T(8,128)(2,1)S(1)}, bf16[704,1024]{1,0:T(8,128)(2,1)}, u32[]{:S(2)}, u32[]{:S(2)}) collective-permute-start(bf16[704,1024]{1,0:T(8,128)(2,1)S(1)} %bitcast.40), channel_id=1, source_target_pairs={{0,1},{1,0},{2,3},{3,2},{4,5},{5,4},{6,7},{7,6},{8,9},{9,8},{10,11... | collective-permute-start | bytes 4325384 | tf_op jit(solution)/shard_map/weight_swap/ppermute | solution.py:729
  41.9 0.1 collective-permute-start.8
  42.0 0.4 collective-permute-start.9
  42.4 7.2 %all-to-all-start.1 = ((bf16[32,80,128]{2,1,0:T(8,128)(2,1)}), bf16[32,80,128]{2,1,0:T(8,128)(2,1)}, u32[]{:S(2)}, u32[]{:S(2)}) async-start(bf16[32,80,128]{2,1,0:T(8,128)(2,1)} %bitcast.66), calls=%async_computation.1 | async-start | bytes 1310720 | tf_op jit(solution)/shard_map/prefix_exchange/all_to_all | solution.py:671
  49.6 8.9 %suffix_attention.1.part_ref = f32[1024,128]{1,0:T(8,128)} custom-call(s32[1]{0:T(128)S(6)} %select_n.11.quarter_ref, s32[16]{0:T(128)S(1)} %bitcast.57, bf16[32,176,128]{2,1,0:T(8,128)(2,1)} %all-to-all-done.got_ref.query_ref.gate_last_ref, bf16[32,176,128]{2,1,0:T(8,128)(2,1)} %all-to-all-done.got_ref.query_ref.gate_last_ref), custom_call_target="tpu_custom_call" | custom-call | tf_op jit(solution)/shard_map/suffix_attention/pallas_call | solution.py:283
  58.6 4.0 %all-to-all-done.1.keys_ref.tok_last_ref = bf16[32,80,128]{2,1,0:T(8,128)(2,1)} async-done(((bf16[32,80,128]{2,1,0:T(8,128)(2,1)}), bf16[32,80,128]{2,1,0:T(8,128)(2,1)}, u32[]{:S(2)}, u32[]{:S(2)}) %all-to-all-start.1) | async-done | bytes 655392 | tf_op jit(solution)/shard_map/prefix_exchange/all_to_all | solution.py:671
  62.6 5.1 %prefix_attention.1 = bf16[32,32,128]{2,1,0:T(8,128)(2,1)S(1)} custom-call(s32[1]{0:T(128)S(6)} %select_n.11.quarter_ref, s32[16]{0:T(128)S(1)} %bitcast.58, bf16[32,176,128]{2,1,0:T(8,128)(2,1)} %all-to-all-done.got_ref.query_ref.gate_last_ref, bf16[32,80,128]{2,1,0:T(8,128)(2,1)} %all-to-all-done.1.keys_ref.tok_last_ref, f32[1024,128]{1,0:T(8,128)} %suffix_attention.1.part_ref), custom_call_target="tpu_custom_call" | custom-call | tf_op jit(solution)/shard_map/prefix_attention/pallas_call | solution.py:375
  67.7 12.9 %all_to_all.30 = bf16[32,32,128]{2,1,0:T(8,128)(2,1)S(1)} all-to-all(bf16[32,32,128]{2,1,0:T(8,128)(2,1)S(1)} %prefix_attention.1), channel_id=1, replica_groups=mesh['grp'=8,'blk'=32] {'blk'}, dimensions={0} | all-to-all | bytes 524288 | tf_op jit(solution)/shard_map/context_exchange/all_to_all | solution.py:671
  80.7 6.1 %mix.1 = (f32[128,1024]{1,0:T(8,128)}, f32[16,1024]{1,0:T(8,128)}, bf16[768,1024]{1,0:T(8,128)(2,1)}) custom-call(s32[1]{0:T(128)} %bitcast.block_ref, bf16[8,4,32,128]{3,2,1,0:T(8,128)(2,1)S(1)} %bitcast.52, bf16[128,1024]{1,0:T(8,128)(2,1)S(1)} %bitcast.51, bf16[32,80,128]{2,1,0:T(8,128)(2,1)} %all-to-all-done.1.keys_ref.tok_last_ref, ...), custom_call_target="tpu_custom_call" | custom-call | tf_op jit(solution)/shard_map/mix/pallas_call | solution.py:487
  86.8 26.8 %all_to_all.31 = bf16[32,24,1024]{2,1,0:T(8,128)(2,1)S(1)} all-to-all(bf16[32,24,1024]{2,1,0:T(8,128)(2,1)} %bitcast.67), channel_id=1, replica_groups=mesh['grp'=8,'blk'=32] {'blk'}, dimensions={0} | all-to-all | bytes 3145728 | tf_op jit(solution)/shard_map/dispatch_exchange/all_to_all | solution.py:671
  113.6 11.0 %expert.1 = bf16[768,1024]{1,0:T(8,128)(2,1)} custom-call(bf16[768,1024]{1,0:T(8,128)(2,1)S(1)} %bitcast.39, bf16[704,1024]{1,0:T(8,128)(2,1)S(1)} %bitcast.42, bf16[704,1024]{1,0:T(8,128)(2,1)S(1)} %bitcast.45, bf16[704,1024]{1,0:T(8,128)(2,1)S(1)} %bitcast.48, bf16[704,1024]{1,0:T(8,128)(2,1)} %collective-permute-done.7.g1, ...), custom_call_target="tpu_custom_call" | custom-call | tf_op jit(solution)/shard_map/expert/pallas_call | solution.py:580
  124.6 0.0 copy-start.3
  124.6 26.6 %all_to_all.32 = bf16[32,24,1024]{2,1,0:T(8,128)(2,1)S(1)} all-to-all(bf16[32,24,1024]{2,1,0:T(8,128)(2,1)} %bitcast.65), channel_id=1, replica_groups=mesh['grp'=8,'blk'=32] {'blk'}, dimensions={0} | all-to-all | bytes 3145728 | tf_op jit(solution)/shard_map/return_exchange/all_to_all | solution.py:671
  151.3 2.5 %combine.1 = (bf16[128,1024]{1,0:T(8,128)(2,1)}, f32[1,128]{1,0:T(1,128)S(1)}) custom-call(s32[1]{0:T(128)} %bitcast.block_ref, s32[16]{0:T(128)S(1)} %bitcast.59, f32[128,1024]{1,0:T(8,128)S(1)} %copy-done.5, f32[16,1024]{1,0:T(8,128)S(1)} %copy-done.6, bf16[768,1024]{1,0:T(8,128)(2,1)S(1)} %bitcast.38, s32[2,128]{1,0:T(2,128)S(1)} %bitcast.55, ...), custom_call_target="tpu_custom_call" | custom-call | tf_op jit(solution)/shard_map/combine/pallas_call | solution.py:657
  153.8 10.4 %all_to_all.33 = f32[32,1,128]{2,1,0:T(1,128)S(1)} all-to-all(f32[32,1,128]{2,1,0:T(1,128)S(1)} %broadcast_in_dim.21), channel_id=1, replica_groups=mesh['grp'=8,'blk'=32] {'blk'}, dimensions={0} | all-to-all | bytes 32768 | tf_op jit(solution)/shard_map/final_exchange/all_to_all | solution.py:671
  164.1 0.6 slice_reduce_fusion
  164.7 0.5 fusion
  (40 shorter events, 0.1 us)
Async XLA Ops:
  5.1 8.8 %copy-start.12 = (bf16[1,64,1024]{2,1,0:T(8,128)(2,1)S(1)}, bf16[1,64,1024]{2,1,0:T(8,128)(2,1)}, u32[]{:S(2)}) copy-start(bf16[1,64,1024]{2,1,0:T(8,128)(2,1)} %param.19) | copy-start | bytes 393220
  5.1 30.6 %all-to-all-start = ((bf16[32,176,128]{2,1,0:T(8,128)(2,1)}), bf16[32,176,128]{2,1,0:T(8,128)(2,1)}, u32[]{:S(2)}, u32[]{:S(2)}) async-start(bf16[32,176,128]{2,1,0:T(8,128)(2,1)} %bitcast.8), calls=%async_computation | async-start | bytes 2883584 | tf_op jit(solution)/shard_map/qkv_exchange/all_to_all | solution.py:671
  13.9 8.2 %collective-permute-start.4 = (bf16[64,1024]{1,0:T(8,128)(2,1)S(1)}, bf16[64,1024]{1,0:T(8,128)(2,1)S(1)}, u32[]{:S(2)}, u32[]{:S(2)}) collective-permute-start(bf16[64,1024]{1,0:T(8,128)(2,1)S(1)} %bitcast.70), channel_id=1, source_target_pairs={{0,224},{32,0},{64,32},{96,64},{128,96},{160,128},{192,160},{224,1... | collective-permute-start | bytes 393224 | tf_op jit(solution)/shard_map/prefix_gather/ppermute | solution.py:678
  19.5 7.4 %collective-permute-start.1 = (bf16[64,1024]{1,0:T(8,128)(2,1)S(1)}, bf16[64,1024]{1,0:T(8,128)(2,1)S(1)}, u32[]{:S(2)}, u32[]{:S(2)}) collective-permute-start(bf16[64,1024]{1,0:T(8,128)(2,1)S(1)} %bitcast.71), channel_id=1, source_target_pairs={{0,64},{32,96},{64,128},{96,160},{128,192},{160,224},{192,0},{224,... | collective-permute-start | bytes 393224 | tf_op jit(solution)/shard_map/prefix_gather/ppermute | solution.py:678
  19.5 9.3 %collective-permute-start = (bf16[64,1024]{1,0:T(8,128)(2,1)S(1)}, bf16[64,1024]{1,0:T(8,128)(2,1)S(1)}, u32[]{:S(2)}, u32[]{:S(2)}) collective-permute-start(bf16[64,1024]{1,0:T(8,128)(2,1)S(1)} %bitcast.72), channel_id=1, source_target_pairs={{0,32},{32,64},{64,96},{96,128},{128,160},{160,192},{192,224},{224... | collective-permute-start | bytes 393224 | tf_op jit(solution)/shard_map/prefix_gather/ppermute | solution.py:678
  22.1 13.5 %copy-start.13 = (bf16[64,1024]{1,0:T(8,128)(2,1)}, bf16[64,1024]{1,0:T(8,128)(2,1)S(1)}, u32[]{:S(2)}) copy-start(bf16[64,1024]{1,0:T(8,128)(2,1)S(1)} %collective-permute-done.4.refs_7_) | copy-start | bytes 393220
  22.1 7.6 %collective-permute-start.6 = (bf16[64,1024]{1,0:T(8,128)(2,1)S(1)}, bf16[64,1024]{1,0:T(8,128)(2,1)S(1)}, u32[]{:S(2)}, u32[]{:S(2)}) collective-permute-start(bf16[64,1024]{1,0:T(8,128)(2,1)S(1)} %collective-permute-done.4.refs_7_), channel_id=1, source_target_pairs={{0,224},{32,0},{64,32},{96,64},{128,96},{160,128},{192,160},{224,1... | collective-permute-start | bytes 393224 | tf_op jit(solution)/shard_map/prefix_gather/ppermute | solution.py:678
  25.6 8.1 %collective-permute-start.5 = (bf16[64,1024]{1,0:T(8,128)(2,1)S(1)}, bf16[64,1024]{1,0:T(8,128)(2,1)}, u32[]{:S(2)}, u32[]{:S(2)}) collective-permute-start(bf16[64,1024]{1,0:T(8,128)(2,1)S(1)} %collective-permute-done.4.refs_7_), channel_id=1, source_target_pairs={{0,192},{32,224},{64,0},{96,32},{128,64},{160,96},{192,128},{224,1... | collective-permute-start | bytes 393224 | tf_op jit(solution)/shard_map/prefix_gather/ppermute | solution.py:678
  26.9 8.7 %copy-start.14 = (bf16[64,1024]{1,0:T(8,128)(2,1)}, bf16[64,1024]{1,0:T(8,128)(2,1)S(1)}, u32[]{:S(2)}) copy-start(bf16[64,1024]{1,0:T(8,128)(2,1)S(1)} %collective-permute-done.1.refs_2_) | copy-start | bytes 393220
  26.9 7.5 %collective-permute-start.3 = (bf16[64,1024]{1,0:T(8,128)(2,1)S(1)}, bf16[64,1024]{1,0:T(8,128)(2,1)}, u32[]{:S(2)}, u32[]{:S(2)}) collective-permute-start(bf16[64,1024]{1,0:T(8,128)(2,1)S(1)} %collective-permute-done.1.refs_2_), channel_id=1, source_target_pairs={{0,64},{32,96},{64,128},{96,160},{128,192},{160,224},{192,0},{224,... | collective-permute-start | bytes 393224 | tf_op jit(solution)/shard_map/prefix_gather/ppermute | solution.py:678
  28.1 7.6 %collective-permute-start.2 = (bf16[64,1024]{1,0:T(8,128)(2,1)S(1)}, bf16[64,1024]{1,0:T(8,128)(2,1)}, u32[]{:S(2)}, u32[]{:S(2)}) collective-permute-start(bf16[64,1024]{1,0:T(8,128)(2,1)S(1)} %collective-permute-done.1.refs_2_), channel_id=1, source_target_pairs={{0,32},{32,64},{64,96},{96,128},{128,160},{160,192},{192,224},{224... | collective-permute-start | bytes 393224 | tf_op jit(solution)/shard_map/prefix_gather/ppermute | solution.py:678
  28.8 8.8 %copy-start = (bf16[1,1024,704]{1,2,0:T(8,128)(2,1)S(1)}, bf16[1,1024,704]{1,2,0:T(8,128)(2,1)}, u32[]{:S(2)}) copy-start(bf16[1,1024,704]{1,2,0:T(8,128)(2,1)} %param.27) | copy-start | bytes 4325380
  28.8 13.0 %copy-start.1 = (bf16[1,1024,704]{1,2,0:T(8,128)(2,1)S(1)}, bf16[1,1024,704]{1,2,0:T(8,128)(2,1)}, u32[]{:S(2)}) copy-start(bf16[1,1024,704]{1,2,0:T(8,128)(2,1)} %param.28) | copy-start | bytes 4325380
  28.8 20.8 %copy-start.8 = (s32[1,16]{1,0:T(1,128)S(1)}, s32[1,16]{1,0:T(1,128)}, u32[]{:S(2)}) copy-start(s32[1,16]{1,0:T(1,128)} %param.17) | copy-start | bytes 196
  28.9 6.8 %copy-start.15 = (bf16[64,1024]{1,0:T(8,128)(2,1)}, bf16[64,1024]{1,0:T(8,128)(2,1)S(1)}, u32[]{:S(2)}) copy-start(bf16[64,1024]{1,0:T(8,128)(2,1)S(1)} %collective-permute-done.refs_1_) | copy-start | bytes 393220
  29.7 5.9 %copy-start.16 = (bf16[64,1024]{1,0:T(8,128)(2,1)}, bf16[64,1024]{1,0:T(8,128)(2,1)S(1)}, u32[]{:S(2)}) copy-start(bf16[64,1024]{1,0:T(8,128)(2,1)S(1)} %collective-permute-done.6.refs_6_) | copy-start | bytes 393220
  37.6 20.9 %collective-permute-start.7 = (bf16[704,1024]{1,0:T(8,128)(2,1)S(1)}, bf16[704,1024]{1,0:T(8,128)(2,1)}, u32[]{:S(2)}, u32[]{:S(2)}) collective-permute-start(bf16[704,1024]{1,0:T(8,128)(2,1)S(1)} %bitcast.40), channel_id=1, source_target_pairs={{0,1},{1,0},{2,3},{3,2},{4,5},{5,4},{6,7},{7,6},{8,9},{9,8},{10,11... | collective-permute-start | bytes 4325384 | tf_op jit(solution)/shard_map/weight_swap/ppermute | solution.py:729
  41.9 16.7 %collective-permute-start.8 = (bf16[704,1024]{1,0:T(8,128)(2,1)S(1)}, bf16[704,1024]{1,0:T(8,128)(2,1)}, u32[]{:S(2)}, u32[]{:S(2)}) collective-permute-start(bf16[704,1024]{1,0:T(8,128)(2,1)S(1)} %bitcast.43), channel_id=1, source_target_pairs={{0,1},{1,0},{2,3},{3,2},{4,5},{5,4},{6,7},{7,6},{8,9},{9,8},{10,11... | collective-permute-start | bytes 4325384 | tf_op jit(solution)/shard_map/weight_swap/ppermute | solution.py:729
  42.0 16.6 %collective-permute-start.9 = (bf16[704,1024]{1,0:T(8,128)(2,1)}, bf16[704,1024]{1,0:T(8,128)(2,1)}, u32[]{:S(2)}, u32[]{:S(2)}) collective-permute-start(bf16[704,1024]{1,0:T(8,128)(2,1)} %bitcast.46), channel_id=1, source_target_pairs={{0,1},{1,0},{2,3},{3,2},{4,5},{5,4},{6,7},{7,6},{8,9},{9,8},{10,11... | collective-permute-start | bytes 4325384 | tf_op jit(solution)/shard_map/weight_swap/ppermute | solution.py:729
  42.4 20.2 %all-to-all-start.1 = ((bf16[32,80,128]{2,1,0:T(8,128)(2,1)}), bf16[32,80,128]{2,1,0:T(8,128)(2,1)}, u32[]{:S(2)}, u32[]{:S(2)}) async-start(bf16[32,80,128]{2,1,0:T(8,128)(2,1)} %bitcast.66), calls=%async_computation.1 | async-start | bytes 1310720 | tf_op jit(solution)/shard_map/prefix_exchange/all_to_all | solution.py:671
  58.5 22.1 %copy-start.4 = (bf16[1,128,1024]{2,1,0:T(8,128)(2,1)S(1)}, bf16[1,128,1024]{2,1,0:T(8,128)(2,1)}, u32[]{:S(2)}) copy-start(bf16[1,128,1024]{2,1,0:T(8,128)(2,1)} %param.16) | copy-start | bytes 786436
  58.5 22.1 %copy-start.7 = (s32[1,128,2]{1,2,0:T(2,128)S(1)}, s32[1,128,2]{1,2,0:T(2,128)}, u32[]{:S(2)}) copy-start(s32[1,128,2]{1,2,0:T(2,128)} %param.20) | copy-start | bytes 3076
  58.5 22.1 %copy-start.9 = (f32[1024]{0:T(1024)S(1)}, f32[1024]{0:T(1024)}, u32[]{:S(2)}) copy-start(f32[1024]{0:T(1024)} %param.26) | copy-start | bytes 12292
  62.6 18.1 %copy-start.2 = (bf16[1,704,1024]{2,1,0:T(8,128)(2,1)S(1)}, bf16[1,704,1024]{2,1,0:T(8,128)(2,1)}, u32[]{:S(2)}) copy-start(bf16[1,704,1024]{2,1,0:T(8,128)(2,1)} %param.29) | copy-start | bytes 4325380
  124.6 26.7 %copy-start.3 = (bf16[1024,1004]{0,1:T(8,128)(2,1)S(1)}, bf16[1024,1004]{0,1:T(8,128)(2,1)}, u32[]{:S(2)}) copy-start(bf16[1024,1004]{0,1:T(8,128)(2,1)} %param.31) | copy-start | bytes 6168580
  124.6 26.6 %copy-start.5 = (f32[128,1024]{1,0:T(8,128)S(1)}, f32[128,1024]{1,0:T(8,128)}, u32[]{:S(2)}) copy-start(f32[128,1024]{1,0:T(8,128)} %get-tuple-element.25.mixed_ref) | copy-start | bytes 1572868
  124.6 26.6 %copy-start.6 = (f32[16,1024]{1,0:T(8,128)S(1)}, f32[16,1024]{1,0:T(8,128)}, u32[]{:S(2)}) copy-start(f32[16,1024]{1,0:T(8,128)} %get-tuple-element.26.mixed_last_ref) | copy-start | bytes 196612
  124.6 26.6 %copy-start.10 = (f32[1024]{0:T(1024)S(1)}, f32[1024]{0:T(1024)}, u32[]{:S(2)}) copy-start(f32[1024]{0:T(1024)} %param.30) | copy-start | bytes 12292
  124.6 26.6 %copy-start.11 = (f32[1,128,2]{1,2,0:T(2,128)S(1)}, f32[1,128,2]{1,2,0:T(2,128)}, u32[]{:S(2)}) copy-start(f32[1,128,2]{1,2,0:T(2,128)} %param.21) | copy-start | bytes 3076
